TPU v7x, 1024 devices: a whole 4x8x16 slice. The times are simulated.
1024 devices in a mesh: dp: 32 (over z, core), expert: 32 (over y, x).
Axes of the slice: x: 4, y: 8, z: 16, core: 2. Of those that a mesh axis runs over, the one named last changes fastest.
Arguments:
- tokens: bfloat16 [65536, 1024], P(('dp', 'expert')), may hold values from -6 to 6
- expert_ids: int32 [65536, 8], P(('dp', 'expert')), may hold values from 0 to 63, all different within a row; in each aligned block of 64 rows (0 to 63, 64 to 127, ...) at most 12 rows name the same one
- gates: float32 [65536, 8], P(('dp', 'expert')), may hold values from 0.1 to 0.4
- w_in: bfloat16 [64, 1024, 768], P('expert', 'dp'), may hold values from -0.1875 to 0.1875
- w_out: bfloat16 [64, 384, 1024], P('expert', None, 'dp'), may hold values from -0.3125 to 0.3125
Outputs:
- mixed: bfloat16 [65536, 1024], P(('dp', 'expert'))
Inputs may be any that keep to these rules, and one draw needn't show every extreme that they name: `expert_ids`: each row names 8 different experts. Among the 64 rows of one device (aligned blocks), no expert is named by more than 12 rows, a bound that some block reaches.
All inputs are finite; a program needn't handle non-finite values.
Results may differ from a plain program's by a relative error of at most 0.0058.
Values may be sent and summed in bfloat16 or wider, within the bound.
No kernel may reach another device: no remote copies, remote signals or barrier semaphores. Data moves between devices by JAX's collectives and lax.ppermute only.
A program may use at most 32 MiB of HBM per device.

v0:
```python
import jax
import jax.numpy as jnp
from jax import lax
from jax.sharding import Mesh
from jax.sharding import PartitionSpec as P

DP = ("dp_0", "dp_1")
DP_EXPERT = ("dp_0", "dp_1", "expert")


def split_up(x, dim, size):
    before, after = (x.shape[:dim], x.shape[dim + 1 :])
    return jnp.moveaxis(x.reshape(*before, size, -1, *after), dim, 0)


def cut_rows(length, count):
    step = length // count
    if step >= 8:
        step -= step % 8
    return [step * k for k in range(1, count)]


def joined_along(tiles, dim):
    dims = list(tiles.shape[1:])
    dims[dim] *= tiles.shape[0]
    return jnp.moveaxis(tiles, 0, dim).reshape(dims)


def exchange_in_pieces(x, axis, pieces, split_dim, concat_dim):
    tiles = split_up(x, split_dim, lax.axis_size(axis))
    split_at = max(range(1, max(2, tiles.ndim - 1)), key=lambda d: tiles.shape[d])
    gathered = []
    for slab in jnp.split(tiles, cut_rows(tiles.shape[split_at], pieces), axis=split_at):
        if slab.size:
            gathered.append(lax.all_to_all(slab, axis, split_axis=0, concat_axis=0, tiled=True))
    return joined_along(jnp.concatenate(gathered, axis=split_at), concat_dim)


def gather_in_order(x, axes, turns):
    tiles = x[None]
    for k in turns:
        tiles = lax.all_gather(tiles, axes[k], axis=0, tiled=True)
    held = [lax.axis_size(axes[k]) for k in reversed(turns)]
    tiles = tiles.reshape(*held, *x.shape)
    turned = sorted(range(len(turns)), key=lambda place: turns[len(turns) - 1 - place])
    return tiles.transpose(*turned, *range(len(turns), tiles.ndim)).reshape(-1, *x.shape)


def whole_of(x, axes, turns, dim):
    return joined_along(gather_in_order(x, axes, turns), dim)


def slot_index(expert_ids, experts, capacity):
    flat_ids = expert_ids.reshape(-1)
    onehot = (flat_ids[:, None] == jnp.arange(experts, dtype=jnp.int32)[None, :]).astype(jnp.int32)
    before = jnp.cumsum(onehot, axis=0) - onehot
    position = jnp.sum(before * onehot, axis=1)
    return flat_ids * capacity + position


def activate(joint_rows, hidden):
    return (jax.nn.silu(joint_rows[..., :hidden]) * joint_rows[..., hidden:]).astype(jnp.bfloat16)


def shards(tokens, expert_ids, gates, w_in, w_out):
    tok_rows, model_width = tokens.shape
    top_count = expert_ids.shape[1]
    per_device = w_in.shape[0]
    hidden = w_out.shape[1]
    owners = lax.axis_size("expert")
    experts = per_device * owners
    capacity = max(2, min(tok_rows, tok_rows * top_count * 3 // (2 * experts)))
    slot_rows = slot_index(expert_ids, experts, capacity)
    copies = jnp.repeat(tokens, top_count, axis=0)
    outgoing = jnp.zeros((experts * capacity, model_width), jnp.bfloat16).at[slot_rows].set(copies)
    arrived = exchange_in_pieces(
        outgoing.reshape(owners, per_device, capacity, model_width), "expert", 2, 0, 0
    )
    joint_rows = jnp.einsum(
        "necd,edf->necf", arrived, whole_of(w_in, DP, (0, 1), 1), preferred_element_type=jnp.float32
    )
    activated = activate(joint_rows, hidden)
    produced = jnp.einsum(
        "necf,efd->necd",
        activated,
        whole_of(w_out, DP, (0, 1), 2),
        preferred_element_type=jnp.float32,
    ).astype(jnp.bfloat16)
    came_back = lax.all_to_all(produced, "expert", split_axis=0, concat_axis=0, tiled=True)
    picked = came_back.reshape(experts * capacity, model_width)[slot_rows].reshape(
        tok_rows, top_count, model_width
    )
    mixed = jnp.sum(gates[:, :, None] * picked.astype(jnp.float32), axis=1)
    return mixed.astype(jnp.bfloat16)


def solution(mesh):
    finer = Mesh(mesh.devices.reshape(16, 2, mesh.shape["expert"]), ("dp_0", "dp_1", "expert"))
    in_specs = (
        P(DP_EXPERT, None),
        P(DP_EXPERT, None),
        P(DP_EXPERT, None),
        P("expert", DP, None),
        P("expert", None, DP),
    )
    out_specs = P(DP_EXPERT, None)
    return jax.shard_map(
        shards, mesh=finer, in_specs=in_specs, out_specs=out_specs, check_vma=False
    )
```

profile of v0, /device:TPU:4, one launch (start us, length us, event | category | flops | bytes accessed | tf_op | source)
XLA Modules:
  0.0 217.1 jit_solution(1065098035280536627)
XLA Ops:
  6.5 0.0 copy-start
  6.5 0.0 copy-start.1
  6.5 0.0 all-gather.10.cloned.1.call-start
  6.5 0.7 all-gather.10.cloned.1.call-update
  7.3 0.0 all-gather.8.cloned.1.call-start
  7.3 49.6 %all-gather.1 = bf16[32,384,32]{1,2,0:T(8,128)(2,1)} all-gather(bf16[2,384,32]{1,2,0:T(8,128)(2,1)} %param.9), channel_id=3, replica_groups=mesh['dp_0'=16,'dp_1'=2,'expert'=32] {'dp_0'}, dimensions={0}, use_global_device_ids=true | all-gather | bytes 835584 | tf_op jit(solution)/shard_map/all_gather | solution.py:42
  56.9 0.0 all-gather.8.cloned.1.call-update
  56.9 0.0 all-gather.6.cloned.1.call-start
  57.0 0.0 copy-done.1
  57.0 0.1 copy.57
  57.1 0.1 eq.29
  57.2 0.1 eq.25
  57.3 1.2 reduce-window.6
  58.5 0.2 slice_reduce_fusion
  58.8 0.1 copy.56
  58.9 0.1 mul.37
  59.0 0.1 fusion.13
  59.1 0.0 copy-done
  59.1 3.9 %scatter_custom_fusion = bf16[768,1024]{1,0:T(8,128)(2,1)} fusion(s32[512]{0:T(512)S(1)} %bitcast.69, bf16[]{:T(256)} %constant.6.clone.1, bf16[64,1024]{1,0:T(8,128)(2,1)S(1)} %copy-done), kind=kCustom, calls=%fused_computation.12 | custom fusion | bytes 1703938 | tf_op jit(solution)/shard_map/scatter | solution.py:75
  63.0 2.4 %reshape_reshape.3 = bf16[32,1,2,12,1024]{4,3,2,0,1:T(8,128)(2,1)S(1)} reshape(bf16[768,1024]{1,0:T(8,128)(2,1)} %scatter_custom_fusion) | data formatting | bytes 3145728 | tf_op jit(solution)/shard_map/reshape;reshape | solution.py:13
  65.3 28.0 %all-gather.10.cloned.1.call-done = bf16[32,32,768]{2,1,0:T(8,128)(2,1)} async-done(((bf16[2,32,768]{2,1,0:T(8,128)(2,1)}), bf16[32,32,768]{2,1,0:T(8,128)(2,1)}) %all-gather.10.cloned.1.call-update) | async-done | bytes 1572880 | tf_op jit(solution)/shard_map/all_gather | solution.py:42
  93.4 0.0 all-gather.6.cloned.1.call-update
  93.4 0.5 fusion.17
  93.9 1.8 copy.60
  95.6 9.9 %all-to-all-start = ((bf16[32,1,2,6,1024]{4,2,3,1,0:T(2,128)(2,1)}), bf16[32,1,2,6,1024]{4,2,3,1,0:T(2,128)(2,1)S(1)}, u32[]{:S(2)}, u32[]{:S(2)}) async-start(bf16[32,1,2,6,1024]{4,2,3,1,0:T(2,128)(2,1)} %copy.60), calls=%async_computation | async-start | bytes 1572864 | tf_op jit(solution)/shard_map/all_to_all | solution.py:35
  105.5 1.7 copy.61
  107.2 13.8 %all-to-all-done = bf16[32,1,2,6,1024]{4,2,3,1,0:T(2,128)(2,1)S(1)} async-done(((bf16[32,1,2,6,1024]{4,2,3,1,0:T(2,128)(2,1)}), bf16[32,1,2,6,1024]{4,2,3,1,0:T(2,128)(2,1)S(1)}, u32[]{:S(2)}, u32[]{:S(2)}) %all-to-all-start) | async-done | bytes 786464 | tf_op jit(solution)/shard_map/all_to_all | solution.py:35
  121.0 5.5 %all-to-all-start.1 = ((bf16[32,1,2,6,1024]{4,2,3,1,0:T(2,128)(2,1)}), bf16[32,1,2,6,1024]{4,2,3,1,0:T(2,128)(2,1)S(1)}, u32[]{:S(2)}, u32[]{:S(2)}) async-start(bf16[32,1,2,6,1024]{4,2,3,1,0:T(2,128)(2,1)} %copy.61), calls=%async_computation.1 | async-start | bytes 1572864 | tf_op jit(solution)/shard_map/all_to_all | solution.py:35
  126.5 0.2 copy.62
  126.8 15.2 %all-to-all-done.1 = bf16[32,1,2,6,1024]{4,2,3,1,0:T(2,128)(2,1)S(1)} async-done(((bf16[32,1,2,6,1024]{4,2,3,1,0:T(2,128)(2,1)}), bf16[32,1,2,6,1024]{4,2,3,1,0:T(2,128)(2,1)S(1)}, u32[]{:S(2)}, u32[]{:S(2)}) %all-to-all-start.1) | async-done | bytes 786464 | tf_op jit(solution)/shard_map/all_to_all | solution.py:35
  142.0 0.2 copy.63
  142.2 0.0 all-gather.8.cloned.1.call-done
  142.2 1.7 copy.65
  144.0 0.2 copy.66
  144.1 1.4 all-gather.6.cloned.1.call-done
  145.5 2.2 copy.64
  147.7 1.4 convolution_bitcast_fusion
  149.1 1.0 fusion.3
  150.1 2.8 %copy.68 = bf16[32,2,12,1024]{3,1,2,0:T(2,128)(2,1)} copy(bf16[32,2,12,1024]{3,0,2,1:T(8,128)(2,1)S(1)} %fusion.3) | data formatting | bytes 3145728 | tf_op jit(solution)/shard_map/convert_element_type | solution.py:88
  152.9 0.0 copy-start.2
  152.9 10.0 %all-to-all-start.2 = ((bf16[32,2,12,1024]{3,1,2,0:T(2,128)(2,1)}), bf16[32,2,12,1024]{3,1,2,0:T(2,128)(2,1)S(1)}, u32[]{:S(2)}, u32[]{:S(2)}) async-start(bf16[32,2,12,1024]{3,1,2,0:T(2,128)(2,1)} %copy.68), calls=%async_computation.2 | async-start | bytes 3145728 | tf_op jit(solution)/shard_map/all_to_all | solution.py:89
  162.9 0.0 copy-done.2
  163.0 0.1 copy.55
  163.0 39.7 %all-to-all-done.2 = bf16[32,2,12,1024]{3,1,2,0:T(2,128)(2,1)S(1)} async-done(((bf16[32,2,12,1024]{3,1,2,0:T(2,128)(2,1)}), bf16[32,2,12,1024]{3,1,2,0:T(2,128)(2,1)S(1)}, u32[]{:S(2)}, u32[]{:S(2)}) %all-to-all-start.2) | async-done | bytes 1572896 | tf_op jit(solution)/shard_map/all_to_all | solution.py:89
  202.7 1.9 copy.69
  204.6 2.5 %reshape.86 = bf16[768,1024]{1,0:T(8,128)(2,1)S(1)} reshape(bf16[32,2,12,1024]{3,2,1,0:T(8,128)(2,1)} %copy.69) | data formatting | bytes 3145728 | tf_op jit(solution)/shard_map/reshape | solution.py:90
  207.1 2.1 gather_fusion
  209.2 1.3 fusion
  (6 shorter events, 0.1 us)
Async XLA Ops:
  6.5 52.6 %copy-start = (bf16[64,1024]{1,0:T(8,128)(2,1)S(1)}, bf16[64,1024]{1,0:T(8,128)(2,1)}, u32[]{:S(2)}) copy-start(bf16[64,1024]{1,0:T(8,128)(2,1)} %param.5) | copy-start | bytes 393220
  6.5 50.5 %copy-start.1 = (s32[64,8]{0,1:T(8,128)S(1)}, s32[64,8]{0,1:T(8,128)}, u32[]{:S(2)}) copy-start(s32[64,8]{0,1:T(8,128)} %param.6) | copy-start | bytes 6148
  6.5 86.8 %all-gather.10.cloned.1.call-start = ((), (), s32[]{:S(2)}) async-start(), calls=%async_computation.5 | async-start | bytes 1671168 | tf_op jit(solution)/shard_map/all_gather | solution.py:42
  7.3 135.0 %all-gather.8.cloned.1.call-start = ((), (), s32[]{:S(2)}) async-start(), calls=%async_computation.4 | async-start | bytes 2359296 | tf_op jit(solution)/shard_map/all_gather | solution.py:42
  56.9 88.6 %all-gather.6.cloned.1.call-start = ((), (), s32[]{:S(2)}) async-start(), calls=%async_computation.3 | async-start | bytes 4718592 | tf_op jit(solution)/shard_map/all_gather | solution.py:42
  95.6 25.4 %all-to-all-start = ((bf16[32,1,2,6,1024]{4,2,3,1,0:T(2,128)(2,1)}), bf16[32,1,2,6,1024]{4,2,3,1,0:T(2,128)(2,1)S(1)}, u32[]{:S(2)}, u32[]{:S(2)}) async-start(bf16[32,1,2,6,1024]{4,2,3,1,0:T(2,128)(2,1)} %copy.60), calls=%async_computation | async-start | bytes 1572864 | tf_op jit(solution)/shard_map/all_to_all | solution.py:35
  121.0 20.9 %all-to-all-start.1 = ((bf16[32,1,2,6,1024]{4,2,3,1,0:T(2,128)(2,1)}), bf16[32,1,2,6,1024]{4,2,3,1,0:T(2,128)(2,1)S(1)}, u32[]{:S(2)}, u32[]{:S(2)}) async-start(bf16[32,1,2,6,1024]{4,2,3,1,0:T(2,128)(2,1)} %copy.61), calls=%async_computation.1 | async-start | bytes 1572864 | tf_op jit(solution)/shard_map/all_to_all | solution.py:35
  152.9 10.0 %copy-start.2 = (f32[64,8]{0,1:T(8,128)S(1)}, f32[64,8]{0,1:T(8,128)}, u32[]{:S(2)}) copy-start(f32[64,8]{0,1:T(8,128)} %param.7) | copy-start | bytes 6148
  152.9 49.8 %all-to-all-start.2 = ((bf16[32,2,12,1024]{3,1,2,0:T(2,128)(2,1)}), bf16[32,2,12,1024]{3,1,2,0:T(2,128)(2,1)S(1)}, u32[]{:S(2)}, u32[]{:S(2)}) async-start(bf16[32,2,12,1024]{3,1,2,0:T(2,128)(2,1)} %copy.68), calls=%async_computation.2 | async-start | bytes 3145728 | tf_op jit(solution)/shard_map/all_to_all | solution.py:89
Sparse Core Ops, SparseCore 0:
  10.0 83.3 all-gather.9
  96.0 19.6 all-gather.7
  118.4 27.0 all-gather.5
where the time goes:
time: 218 us; the launch traced here: 217 us
  waiting for transfers between devices  98.8 us (45%)
  blocking collectives  49.6 us (23%)
  starting transfers between devices  25.4 us (12%)
  local copies, waits for them, and re-layouts  24.7 us (11%)
  between operations  13.3 us (6%)
  other arithmetic  2.73 us (1%)
  matrix products  2.42 us (1%)
    all_gather x1, blocking collectives, gather_in_order(): tiles = lax.all_gather(tiles, axes[k], axis=0, tiled=True)  49.6 us
    all_to_all x1, waiting for transfers between devices, shards(): lax.all_to_all(produced, 'expert', split_axis=0, concat_axis=0, tiled=True)  39.7 us
    all_gather x3, waiting for transfers between devices, gather_in_order(): tiles = lax.all_gather(tiles, axes[k], axis=0, tiled=True)  29.4 us
    all_to_all x2, waiting for transfers between devices, exchange_in_pieces(): lax.all_to_all(slab, axis, split_axis=0, concat_axis=0, tiled=True)  29 us
    all_to_all x2, starting transfers between devices, exchange_in_pieces(): lax.all_to_all(slab, axis, split_axis=0, concat_axis=0, tiled=True)  15.4 us
    all_to_all x1, starting transfers between devices, shards(): lax.all_to_all(produced, 'expert', split_axis=0, concat_axis=0, tiled=True)  9.99 us
  transfers between devices with their start and end apart: 6, of which 5 were waited for; matrix products, arithmetic and copies ran while one was open for 7% of the time, Pallas kernels for 0%

commit v1 on v0

v1 whole, which is shorter than its diff:
```python
import functools

import jax
import jax.numpy as jnp
from jax import lax
from jax.experimental import pallas as pl
from jax.experimental.pallas import tpu as pltpu
from jax.sharding import Mesh
from jax.sharding import PartitionSpec as P

BF16 = jnp.bfloat16
F32 = jnp.float32
DP = ("z", "c")
ALL = ("z", "c", "expert")
ROWS = 24
BLOCK = 32


def iota(shape, dim):
    return lax.broadcasted_iota(jnp.int32, shape, dim)


def which_expert(q):
    return jnp.where((q >= 20) | ((q >= 8) & (q < 16)), 1, 0)


def which_slot(q):
    return jnp.where(q < 8, q, jnp.where(q < 20, q - 8, q - 12))


def dot(a, b):
    return jnp.dot(a, b, preferred_element_type=F32)


def dot_t(a, b):
    return lax.dot_general(a, b, (((1,), (1,)), ((), ())), preferred_element_type=F32)


def half_order(transposed):
    shape = (256, 256)
    j, k = iota(shape, 1 if transposed else 0), iota(shape, 0 if transposed else 1)
    goes_to = ((j // BLOCK) % 2) * 128 + (j // (2 * BLOCK)) * BLOCK + j % BLOCK
    return (goes_to == k).astype(F32).astype(BF16)


def places(ids, experts):
    rows, top = ids.shape
    lane = iota((rows, experts), 1)
    routed = jnp.zeros((rows, experts), F32)
    for k in range(top):
        routed = routed + (ids[:, k : k + 1] == lane).astype(F32)
    earlier = (iota((rows, rows), 1) < iota((rows, rows), 0)).astype(F32).astype(BF16)
    before = dot(earlier, routed.astype(BF16))
    return jnp.where(routed > 0, before + 1.0, 0.0)


def pack_kernel(ids_ref, tok_ref, out_ref):
    owners, per, width = out_ref.shape
    rows, experts = ids_ref.shape[0], 2 * owners
    place = places(ids_ref[...], experts)
    shape = (owners, per, experts)
    dst, q, lane = iota(shape, 0), iota(shape, 1), iota(shape, 2)
    named = (2 * dst + which_expert(q) == lane).astype(F32).astype(BF16)
    found = dot_t(named.reshape(owners * per, experts), place.astype(BF16))
    shape = (owners, per, rows)
    slot = (which_slot(iota(shape, 1)) + 1).astype(F32).reshape(owners * per, rows)
    pick = (found == slot).astype(F32).astype(BF16)
    order = half_order(False)
    for g in range(width // 256):
        cols = dot(tok_ref[:, g * 256 : (g + 1) * 256], order).astype(BF16)
        for h in range(2):
            placed = dot(pick, cols[:, h * 128 : (h + 1) * 128]).astype(BF16)
            at = h * (width // 2) + g * 128
            out_ref[:, :, at : at + 128] = placed.reshape(owners, per, 128)


def gate_kernel(owners, per, ids_ref, gates_ref, high_ref, low_ref):
    rows, top = ids_ref.shape
    experts = 2 * owners
    ids, gates = ids_ref[...], gates_ref[...]
    place = places(ids, experts)
    lane = iota((rows, experts), 1)
    spread = jnp.zeros((rows, experts), F32)
    for k in range(top):
        spread = spread + jnp.where(ids[:, k : k + 1] == lane, gates[:, k : k + 1], 0.0)
    shape = (owners, per, experts)
    dst, q, lane = iota(shape, 0), iota(shape, 1), iota(shape, 2)
    named = (2 * dst + which_expert(q) == lane).astype(F32).astype(BF16)
    named = named.reshape(owners * per, experts)
    found = dot_t(place.astype(BF16), named)
    q = iota((rows, owners * per), 1) % per
    here = found == (which_slot(q) + 1).astype(F32)
    high = spread.astype(BF16)
    low = (spread - high.astype(F32)).astype(BF16)
    high_ref[...] = jnp.where(here, dot_t(high, named), 0.0).astype(BF16)
    low_ref[...] = jnp.where(here, dot_t(low, named), 0.0).astype(BF16)


def expert_kernel(core_ref, x_ref, a_own, a_other, b_own, b_other, o_own, o_other, y_ref):
    owners, per, width = x_ref.shape
    half = width // 2
    hidden = o_own.shape[-1]
    core = core_ref[0]
    own = pl.ds(pl.multiple_of(core * half, half), half)
    other = pl.ds(pl.multiple_of((1 - core) * half, half), half)
    results = []
    for e, (w_own, w_other) in enumerate(((a_own, a_other), (b_own, b_other))):
        parts = []
        for at in (own, other):
            full = x_ref[:, e * 8 : e * 8 + 8, at].reshape(owners * 8, half)
            rest = x_ref[:, 16:24, at].reshape(owners * 8, half)
            parts.append(jnp.concatenate([full, rest], axis=0))
        joint = dot(parts[0], w_own[...].reshape(half, 2 * hidden))
        joint = joint + dot(parts[1], w_other[...].reshape(half, 2 * hidden))
        gate, up = joint[:, :hidden], joint[:, hidden:]
        activated = (gate * jax.nn.sigmoid(gate) * up).astype(BF16)
        made = []
        for w in (o_own, o_other):
            made.append(dot_t(activated, w[:, e].reshape(half, hidden)))
        results.append(made)
    shape = (owners, 8, half)
    first = iota(shape, 1) < 4
    for at, ya, yb in ((own, results[0][0], results[1][0]), (other, results[0][1], results[1][1])):
        n = owners * 8
        y_ref[:, 0:8, at] = ya[:n].reshape(shape).astype(BF16)
        y_ref[:, 8:16, at] = yb[:n].reshape(shape).astype(BF16)
        rest = jnp.where(first, ya[n:].reshape(shape), yb[n:].reshape(shape))
        y_ref[:, 16:24, at] = rest.astype(BF16)


def combine_kernel(high_ref, low_ref, back_ref, out_ref):
    owners, per, width = back_ref.shape
    back = back_ref[...].reshape(owners * per, width)
    mixed = dot(high_ref[...], back) + dot(low_ref[...], back)
    mixed = mixed.astype(BF16)
    order = half_order(True)
    for g in range(width // 256):
        at = g * 128
        halves = [mixed[:, at : at + 128], mixed[:, width // 2 + at : width // 2 + at + 128]]
        cols = dot(jnp.concatenate(halves, axis=1), order)
        out_ref[:, g * 256 : (g + 1) * 256] = cols.astype(BF16)


def call(kernel, outs, args, flops, moved, smem=0):
    vmem = pl.BlockSpec(memory_space=pltpu.VMEM)
    scalar = pl.BlockSpec(memory_space=pltpu.SMEM)
    return pl.pallas_call(
        kernel,
        out_shape=outs,
        in_specs=[scalar] * smem + [vmem] * (len(args) - smem),
        out_specs=jax.tree.map(lambda _: vmem, outs),
        cost_estimate=pl.CostEstimate(flops=flops, bytes_accessed=moved, transcendentals=0),
    )(*args)


def shards(tokens, expert_ids, gates, w_in, w_out):
    rows, width = tokens.shape
    owners = lax.axis_size("expert")
    hidden = w_out.shape[1]
    slots = owners * ROWS
    shape = jax.ShapeDtypeStruct

    w_out_t = jnp.swapaxes(w_out, 1, 2)
    gathered = [lax.all_gather(w, "z", axis=0) for w in (w_in[0], w_in[1], w_out_t)]
    swapped = [lax.ppermute(w, "c", [(0, 1), (1, 0)]) for w in gathered]
    weights = [w for pair in zip(gathered, swapped) for w in pair]

    outgoing = call(
        pack_kernel,
        shape((owners, ROWS, width), BF16),
        (expert_ids, tokens),
        2 * slots * rows * width,
        2 * slots * width,
    )
    arrived = lax.all_to_all(outgoing, "expert", split_axis=0, concat_axis=0, tiled=True)
    high, low = call(
        functools.partial(gate_kernel, owners, ROWS),
        (shape((rows, slots), BF16), shape((rows, slots), BF16)),
        (expert_ids, gates),
        2 * slots * rows * 256,
        4 * slots * rows,
    )
    core = lax.axis_index("c").astype(jnp.int32).reshape(1)
    produced = call(
        expert_kernel,
        shape((owners, ROWS, width), BF16),
        (core, arrived, *weights),
        2 * 1024 * 3 * hidden * width,
        4 * slots * width + 12 * hidden * width,
        smem=1,
    )
    came_back = lax.all_to_all(produced, "expert", split_axis=0, concat_axis=0, tiled=True)
    return call(
        combine_kernel,
        shape((rows, width), BF16),
        (high, low, came_back),
        4 * slots * rows * width,
        2 * slots * width,
    )


def solution(mesh):
    dp = mesh.shape["dp"]
    finer = Mesh(mesh.devices.reshape(dp // 2, 2, mesh.shape["expert"]), ALL)
    in_specs = (P(ALL, None), P(ALL, None), P(ALL, None), P("expert", DP, None), P("expert", None, DP))
    return jax.shard_map(
        shards, mesh=finer, in_specs=in_specs, out_specs=P(ALL, None), check_vma=False
    )
```

time: 218 us -> 199 us (0.913)
  waiting for transfers between devices: 98.8 us -> 39.5 us
  blocking collectives: 49.6 us -> 106 us
  local copies, waits for them, and re-layouts: 24.7 us -> 4.38 us
  Pallas kernels: 0 us -> 16 us
  between operations: 13.3 us -> 0.12 us
  starting transfers between devices: 25.4 us -> 32.5 us
  other arithmetic: 2.73 us -> 0 us
  matrix products: 2.42 us -> 0 us
    all_gather x1 -> x3, blocking collectives: 49.6 us -> 106 us  [shards(): lax.all_gather(w, 'z', axis=0)]
    all_gather x3 -> x0, waiting for transfers between devices: 29.4 us -> none  [gather_in_order(): tiles = lax.all_gather(tiles, axes[k], axis=0, tiled=True)]
    all_to_all x2 -> x1, waiting for transfers between devices: 29 us -> 0.01 us  [shards(): lax.all_to_all(outgoing, 'expert', split_axis=0, concat_axis=0, tiled=True)]
    pallas_call x0 -> x4, Pallas kernels: none -> 16 us  [call(): pl.pallas_call(kernel, out_shape=outs, in_specs=[scalar] * smem + [vmem]...]
    ppermute x0 -> x3, starting transfers between devices: none -> 5.73 us  [shards(): swapped = [lax.ppermute(w, 'c', [(0, 1), (1, 0)]) for w in gathered]]
    unnamed x8 -> x16, local copies, waits for them, and re-layouts: 0.18 us -> 4.37 us
    transpose x3 -> x0, local copies, waits for them, and re-layouts: 4.06 us -> none  [the longest x2 3.9 us: gather_in_order(): tiles.transpose(*turned, *range(len(turns), tiles.ndim))]
    split x3 -> x0, local copies, waits for them, and re-layouts: 3.94 us -> none  [exchange_in_pieces(): jnp.split(tiles, cut_rows(tiles.shape[split_at], pieces), axis=split_at)]
  transfers between devices with their start and end apart: 6 -> 5, of which waited for: 5 -> 2; matrix products, arithmetic and copies ran while one was open for 7% -> 0% of each run, Pallas kernels for 0% -> 1%
where the time goes in v1:
time: 199 us; the launch traced here: 198 us
  blocking collectives  106 us (53%)
  waiting for transfers between devices  39.5 us (20%)
  starting transfers between devices  32.5 us (16%)
  Pallas kernels  16 us (8%)
  local copies, waits for them, and re-layouts  4.38 us (2%)
    all_gather x3, blocking collectives, shards(): lax.all_gather(w, 'z', axis=0)  106 us
    all_to_all x1, waiting for transfers between devices, shards(): lax.all_to_all(produced, 'expert', split_axis=0, concat_axis=0, tiled=True)  36.9 us
    all_to_all x1, starting transfers between devices, shards(): lax.all_to_all(outgoing, 'expert', split_axis=0, concat_axis=0, tiled=True)  16.9 us
    pallas_call x4, Pallas kernels, call(): pl.pallas_call(kernel, out_shape=outs, in_specs=[scalar] * smem + [vmem]...  16 us
    all_to_all x1, starting transfers between devices, shards(): lax.all_to_all(produced, 'expert', split_axis=0, concat_axis=0, tiled=True)  9.9 us
    ppermute x3, starting transfers between devices, shards(): swapped = [lax.ppermute(w, 'c', [(0, 1), (1, 0)]) for w in gathered]  5.73 us
    unnamed x16, local copies, waits for them, and re-layouts  4.37 us
  transfers between devices with their start and end apart: 5, of which 2 were waited for; matrix products, arithmetic and copies ran while one was open for 0% of the time, Pallas kernels for 1%

profile of v1, /device:TPU:4, one launch (start us, length us, event | category | flops | bytes accessed | tf_op | source)
XLA Modules:
  0.0 198.4 jit_solution(312506401754381612)
XLA Ops:
  0.0 1.4 copy.9.ids_ref
  1.4 3.5 %shard_map.56 = bf16[32,24,1024]{2,1,0:T(8,128)(2,1)} custom-call(s32[64,8]{1,0:T(8,128)} %copy.9.ids_ref, bf16[64,1024]{1,0:T(8,128)(2,1)} %tok_ref.1), custom_call_target="tpu_custom_call" | custom-call | flops 100663296 | bytes 1572864 | tf_op jit(solution)/shard_map/pallas_call | solution.py:147
  4.9 0.0 copy-start.4
  4.9 16.9 %all-to-all-start = ((bf16[32,24,1024]{2,1,0:T(8,128)(2,1)}), bf16[32,24,1024]{2,1,0:T(8,128)(2,1)S(1)}, u32[]{:S(2)}, u32[]{:S(2)}) async-start(bf16[32,24,1024]{2,1,0:T(8,128)(2,1)} %shard_map.56), calls=%async_computation | async-start | bytes 3145728 | tf_op jit(solution)/shard_map/all_to_all | solution.py:175
  21.8 0.0 copy-done.4
  21.8 0.0 copy-start.5
  21.8 40.4 %all_gather.12.a_own = bf16[16,32,768]{2,1,0:T(8,128)(2,1)S(1)} all-gather(bf16[1,32,768]{2,1,0:T(8,128)(2,1)S(1)} %get-tuple-element.10), channel_id=1, replica_groups=mesh['z'=16,'c'=2,'expert'=32] {'z'}, dimensions={0}, use_global_device_ids=true | all-gather | bytes 835584 | tf_op jit(solution)/shard_map/all_gather | solution.py:164
  62.2 0.0 copy-start.2
  62.2 1.9 collective-permute-start
  64.1 30.6 %all_gather.13.b_own = bf16[16,32,768]{2,1,0:T(8,128)(2,1)S(1)} all-gather(bf16[1,32,768]{2,1,0:T(8,128)(2,1)S(1)} %get-tuple-element.9), channel_id=1, replica_groups=mesh['z'=16,'c'=2,'expert'=32] {'z'}, dimensions={0}, use_global_device_ids=true | all-gather | bytes 835584 | tf_op jit(solution)/shard_map/all_gather | solution.py:164
  94.8 0.0 copy-start.3
  94.8 1.9 collective-permute-start.1
  96.7 0.0 copy-done.5
  96.7 34.9 %all-gather = bf16[32,32,384]{2,1,0:T(8,128)(2,1)} all-gather(bf16[2,32,384]{2,1,0:T(8,128)(2,1)S(1)} %bitcast.3), channel_id=2, replica_groups=mesh['z'=16,'c'=2,'expert'=32] {'z'}, dimensions={0}, use_global_device_ids=true | all-gather | bytes 835584 | tf_op jit(solution)/shard_map/all_gather | solution.py:164
  131.6 1.9 collective-permute-start.2
  133.5 0.0 collective-permute-done.a_other
  133.5 0.0 collective-permute-done.1.b_other
  133.5 2.6 %collective-permute-done.2.o_other = bf16[16,2,32,384]{3,2,1,0:T(8,128)(2,1)} collective-permute-done((bf16[16,2,32,384]{3,2,1,0:T(8,128)(2,1)}, bf16[16,2,32,384]{3,2,1,0:T(8,128)(2,1)}, u32[]{:S(2)}, u32[]{:S(2)}) %collective-permute-start.2) | collective-permute-done | bytes 786464 | tf_op jit(solution)/shard_map/ppermute | solution.py:165
  136.1 0.0 all-to-all-done.x_ref
  136.1 0.0 copy-start.1
  136.1 0.0 copy-done.2
  136.1 0.0 copy-done.3
  136.1 1.1 copy-done.1
  137.2 7.4 %shard_map.57 = bf16[32,24,1024]{2,1,0:T(8,128)(2,1)} custom-call(s32[1]{0:T(128)} %bitcast.core_ref, bf16[32,24,1024]{2,1,0:T(8,128)(2,1)} %copy-done.1, bf16[16,32,768]{2,1,0:T(8,128)(2,1)} %copy-done.2, bf16[16,32,768]{2,1,0:T(8,128)(2,1)} %collective-permute-done.a_other, bf16[16,32,768]{2,1,0:T(8,128)(2,1)} %copy-done.3, ...), custom_call_target="tpu_custom_call" | custom-call | flops 2415919104 | bytes 7864320 | tf_op jit(solution)/shard_map/pallas_call | solution.py:147
  144.7 0.0 copy-start.6
  144.7 9.9 %all-to-all-start.1 = ((bf16[32,24,1024]{2,1,0:T(8,128)(2,1)}), bf16[32,24,1024]{2,1,0:T(8,128)(2,1)S(1)}, u32[]{:S(2)}, u32[]{:S(2)}) async-start(bf16[32,24,1024]{2,1,0:T(8,128)(2,1)} %shard_map.57), calls=%async_computation.1 | async-start | bytes 3145728 | tf_op jit(solution)/shard_map/all_to_all | solution.py:192
  154.6 0.0 copy-done.6
  154.6 0.7 copy.10.gates_ref
  155.3 2.0 %shard_map.55 = (bf16[64,768]{1,0:T(8,128)(2,1)}, bf16[64,768]{1,0:T(8,128)(2,1)}) custom-call(s32[64,8]{1,0:T(8,128)} %copy.9.ids_ref, f32[64,8]{1,0:T(8,128)} %copy.10.gates_ref), custom_call_target="tpu_custom_call" | custom-call | flops 25165824 | bytes 196608 | tf_op jit(solution)/shard_map/pallas_call | solution.py:147
  157.3 36.9 %all-to-all-done.1.back_ref = bf16[32,24,1024]{2,1,0:T(8,128)(2,1)S(1)} async-done(((bf16[32,24,1024]{2,1,0:T(8,128)(2,1)}), bf16[32,24,1024]{2,1,0:T(8,128)(2,1)S(1)}, u32[]{:S(2)}, u32[]{:S(2)}) %all-to-all-start.1) | async-done | bytes 1572896 | tf_op jit(solution)/shard_map/all_to_all | solution.py:192
  194.2 0.0 copy-start
  194.2 1.2 copy-done
  195.3 3.0 %shard_map.58 = bf16[64,1024]{1,0:T(8,128)(2,1)} custom-call(bf16[64,768]{1,0:T(8,128)(2,1)} %get-tuple-element.7.high_ref, bf16[64,768]{1,0:T(8,128)(2,1)} %get-tuple-element.8.low_ref, bf16[32,24,1024]{2,1,0:T(8,128)(2,1)} %copy-done), custom_call_target="tpu_custom_call" | custom-call | flops 201326592 | bytes 1572864 | tf_op jit(solution)/shard_map/pallas_call | solution.py:147
  (1 shorter events, 0.0 us)
Async XLA Ops:
  4.9 16.9 %copy-start.4 = (bf16[2,32,768]{2,1,0:T(8,128)(2,1)S(1)}, bf16[2,32,768]{2,1,0:T(8,128)(2,1)}, u32[]{:S(2)}) copy-start(bf16[2,32,768]{2,1,0:T(8,128)(2,1)} %param.8) | copy-start | bytes 294916
  4.9 131.2 %all-to-all-start = ((bf16[32,24,1024]{2,1,0:T(8,128)(2,1)}), bf16[32,24,1024]{2,1,0:T(8,128)(2,1)S(1)}, u32[]{:S(2)}, u32[]{:S(2)}) async-start(bf16[32,24,1024]{2,1,0:T(8,128)(2,1)} %shard_map.56), calls=%async_computation | async-start | bytes 3145728 | tf_op jit(solution)/shard_map/all_to_all | solution.py:175
  21.8 74.9 %copy-start.5 = (bf16[2,384,32]{1,2,0:T(8,128)(2,1)S(1)}, bf16[2,384,32]{1,2,0:T(8,128)(2,1)}, u32[]{:S(2)}) copy-start(bf16[2,384,32]{1,2,0:T(8,128)(2,1)} %param.9) | copy-start | bytes 147460
  62.2 73.9 %copy-start.2 = (bf16[16,32,768]{2,1,0:T(8,128)(2,1)}, bf16[16,32,768]{2,1,0:T(8,128)(2,1)S(1)}, u32[]{:S(2)}) copy-start(bf16[16,32,768]{2,1,0:T(8,128)(2,1)S(1)} %all_gather.12.a_own) | copy-start | bytes 2359300
  62.2 71.3 %collective-permute-start = (bf16[16,32,768]{2,1,0:T(8,128)(2,1)S(1)}, bf16[16,32,768]{2,1,0:T(8,128)(2,1)}, u32[]{:S(2)}, u32[]{:S(2)}) collective-permute-start(bf16[16,32,768]{2,1,0:T(8,128)(2,1)S(1)} %all_gather.12.a_own), channel_id=1, source_target_pairs={{0,32},{32,0},{1,33},{33,1},{2,34},{34,2},{3,35},{35,3},{4,36},{36... | collective-permute-start | bytes 2359304 | tf_op jit(solution)/shard_map/ppermute | solution.py:165
  94.8 41.3 %copy-start.3 = (bf16[16,32,768]{2,1,0:T(8,128)(2,1)}, bf16[16,32,768]{2,1,0:T(8,128)(2,1)S(1)}, u32[]{:S(2)}) copy-start(bf16[16,32,768]{2,1,0:T(8,128)(2,1)S(1)} %all_gather.13.b_own) | copy-start | bytes 2359300
  94.8 38.8 %collective-permute-start.1 = (bf16[16,32,768]{2,1,0:T(8,128)(2,1)S(1)}, bf16[16,32,768]{2,1,0:T(8,128)(2,1)}, u32[]{:S(2)}, u32[]{:S(2)}) collective-permute-start(bf16[16,32,768]{2,1,0:T(8,128)(2,1)S(1)} %all_gather.13.b_own), channel_id=1, source_target_pairs={{0,32},{32,0},{1,33},{33,1},{2,34},{34,2},{3,35},{35,3},{4,36},{36... | collective-permute-start | bytes 2359304 | tf_op jit(solution)/shard_map/ppermute | solution.py:165
  131.6 4.5 %collective-permute-start.2 = (bf16[16,2,32,384]{3,2,1,0:T(8,128)(2,1)}, bf16[16,2,32,384]{3,2,1,0:T(8,128)(2,1)}, u32[]{:S(2)}, u32[]{:S(2)}) collective-permute-start(bf16[16,2,32,384]{3,2,1,0:T(8,128)(2,1)} %bitcast.2.o_own), channel_id=1, source_target_pairs={{0,32},{32,0},{1,33},{33,1},{2,34},{34,2},{3,35},{35,3},{4,36},{36... | collective-permute-start | bytes 2359304 | tf_op jit(solution)/shard_map/ppermute | solution.py:165
  136.1 1.1 copy-start.1
  144.7 9.9 %copy-start.6 = (f32[64,8]{0,1:T(8,128)S(1)}, f32[64,8]{0,1:T(8,128)}, u32[]{:S(2)}) copy-start(f32[64,8]{0,1:T(8,128)} %param.7) | copy-start | bytes 6148
  144.7 49.5 %all-to-all-start.1 = ((bf16[32,24,1024]{2,1,0:T(8,128)(2,1)}), bf16[32,24,1024]{2,1,0:T(8,128)(2,1)S(1)}, u32[]{:S(2)}, u32[]{:S(2)}) async-start(bf16[32,24,1024]{2,1,0:T(8,128)(2,1)} %shard_map.57), calls=%async_computation.1 | async-start | bytes 3145728 | tf_op jit(solution)/shard_map/all_to_all | solution.py:192
  194.2 1.2 copy-start

commit v2 on v1

--- a/solution.py
+++ b/solution.py
@@ -8,6 +8,7 @@
 from jax.sharding import Mesh
 from jax.sharding import PartitionSpec as P
 
+
 BF16 = jnp.bfloat16
 F32 = jnp.float32
 DP = ("z", "c")
@@ -44,24 +45,27 @@
 
 
 def places(ids, experts):
-    rows, top = ids.shape
-    lane = iota((rows, experts), 1)
-    routed = jnp.zeros((rows, experts), F32)
+    top, rows = ids.shape
+    line = iota((experts, rows), 0)
+    routed = jnp.zeros((experts, rows), F32)
     for k in range(top):
-        routed = routed + (ids[:, k : k + 1] == lane).astype(F32)
-    earlier = (iota((rows, rows), 1) < iota((rows, rows), 0)).astype(F32).astype(BF16)
-    before = dot(earlier, routed.astype(BF16))
+        routed = routed + (ids[k : k + 1, :] == line).astype(F32)
+    earlier = (iota((rows, rows), 0) < iota((rows, rows), 1)).astype(F32).astype(BF16)
+    before = dot(routed.astype(BF16), earlier)
     return jnp.where(routed > 0, before + 1.0, 0.0)
+
+
+def row_owners(owners, per):
+    shape = (owners, per, 2 * owners)
+    named = 2 * iota(shape, 0) + which_expert(iota(shape, 1)) == iota(shape, 2)
+    return named.astype(F32).astype(BF16).reshape(owners * per, 2 * owners)
 
 
 def pack_kernel(ids_ref, tok_ref, out_ref):
     owners, per, width = out_ref.shape
-    rows, experts = ids_ref.shape[0], 2 * owners
-    place = places(ids_ref[...], experts)
-    shape = (owners, per, experts)
-    dst, q, lane = iota(shape, 0), iota(shape, 1), iota(shape, 2)
-    named = (2 * dst + which_expert(q) == lane).astype(F32).astype(BF16)
-    found = dot_t(named.reshape(owners * per, experts), place.astype(BF16))
+    rows = ids_ref.shape[1]
+    place = places(ids_ref[...], 2 * owners)
+    found = dot(row_owners(owners, per), place.astype(BF16))
     shape = (owners, per, rows)
     slot = (which_slot(iota(shape, 1)) + 1).astype(F32).reshape(owners * per, rows)
     pick = (found == slot).astype(F32).astype(BF16)
@@ -75,53 +79,60 @@
 
 
 def gate_kernel(owners, per, ids_ref, gates_ref, high_ref, low_ref):
-    rows, top = ids_ref.shape
+    top, rows = ids_ref.shape
     experts = 2 * owners
     ids, gates = ids_ref[...], gates_ref[...]
-    place = places(ids, experts)
-    lane = iota((rows, experts), 1)
-    spread = jnp.zeros((rows, experts), F32)
+    line = iota((experts, rows), 0)
+    spread = jnp.zeros((experts, rows), F32)
     for k in range(top):
-        spread = spread + jnp.where(ids[:, k : k + 1] == lane, gates[:, k : k + 1], 0.0)
-    shape = (owners, per, experts)
-    dst, q, lane = iota(shape, 0), iota(shape, 1), iota(shape, 2)
-    named = (2 * dst + which_expert(q) == lane).astype(F32).astype(BF16)
-    named = named.reshape(owners * per, experts)
-    found = dot_t(place.astype(BF16), named)
-    q = iota((rows, owners * per), 1) % per
-    here = found == (which_slot(q) + 1).astype(F32)
+        spread = spread + jnp.where(ids[k : k + 1, :] == line, gates[k : k + 1, :], 0.0)
+    named = row_owners(owners, per)
+    found = dot(named, places(ids, experts).astype(BF16))
+    shape = (owners, per, rows)
+    slot = (which_slot(iota(shape, 1)) + 1).astype(F32).reshape(owners * per, rows)
+    here = found == slot
     high = spread.astype(BF16)
     low = (spread - high.astype(F32)).astype(BF16)
-    high_ref[...] = jnp.where(here, dot_t(high, named), 0.0).astype(BF16)
-    low_ref[...] = jnp.where(here, dot_t(low, named), 0.0).astype(BF16)
-
-
-def expert_kernel(core_ref, x_ref, a_own, a_other, b_own, b_other, o_own, o_other, y_ref):
-    owners, per, width = x_ref.shape
+    high_ref[...] = jnp.where(here, dot(named, high), 0.0).astype(BF16).T
+    low_ref[...] = jnp.where(here, dot(named, low), 0.0).astype(BF16).T
+
+
+def assemble_kernel(table_ref, *refs):
+    *blocks, out_ref, sems = refs
+    copies = []
+    for k, block in enumerate(blocks):
+        copies.append(pltpu.make_async_copy(block, out_ref.at[table_ref[k]], sems.at[k]))
+    for copy in copies:
+        copy.start()
+    for copy in copies:
+        copy.wait()
+
+
+def expert_kernel(core_ref, x_ref, own_ref, other_ref, y_ref):
+    owners, _, width = x_ref.shape
     half = width // 2
-    hidden = o_own.shape[-1]
+    hidden = own_ref.shape[-1] // 3
     core = core_ref[0]
     own = pl.ds(pl.multiple_of(core * half, half), half)
     other = pl.ds(pl.multiple_of((1 - core) * half, half), half)
+    sides = ((own, own_ref), (other, other_ref))
     results = []
-    for e, (w_own, w_other) in enumerate(((a_own, a_other), (b_own, b_other))):
-        parts = []
-        for at in (own, other):
+    for e in range(2):
+        joint = 0.0
+        for at, w_ref in sides:
             full = x_ref[:, e * 8 : e * 8 + 8, at].reshape(owners * 8, half)
             rest = x_ref[:, 16:24, at].reshape(owners * 8, half)
-            parts.append(jnp.concatenate([full, rest], axis=0))
-        joint = dot(parts[0], w_own[...].reshape(half, 2 * hidden))
-        joint = joint + dot(parts[1], w_other[...].reshape(half, 2 * hidden))
+            part = jnp.concatenate([full, rest], axis=0)
+            joint = joint + dot(part, w_ref[:, e, :, : 2 * hidden].reshape(half, 2 * hidden))
         gate, up = joint[:, :hidden], joint[:, hidden:]
         activated = (gate * jax.nn.sigmoid(gate) * up).astype(BF16)
-        made = []
-        for w in (o_own, o_other):
-            made.append(dot_t(activated, w[:, e].reshape(half, hidden)))
-        results.append(made)
+        results.append(
+            [dot_t(activated, w_ref[:, e, :, 2 * hidden :].reshape(half, hidden)) for _, w_ref in sides]
+        )
     shape = (owners, 8, half)
     first = iota(shape, 1) < 4
-    for at, ya, yb in ((own, results[0][0], results[1][0]), (other, results[0][1], results[1][1])):
-        n = owners * 8
+    n = owners * 8
+    for (at, _), ya, yb in zip(sides, results[0], results[1]):
         y_ref[:, 0:8, at] = ya[:n].reshape(shape).astype(BF16)
         y_ref[:, 8:16, at] = yb[:n].reshape(shape).astype(BF16)
         rest = jnp.where(first, ya[n:].reshape(shape), yb[n:].reshape(shape))
@@ -153,22 +164,45 @@
     )(*args)
 
 
+def all_blocks(block):
+    count = lax.axis_size("z")
+
+    def moved(x, by):
+        return lax.ppermute(x, "z", [(i, (i + by) % count) for i in range(count)])
+
+    held = {0: block}
+    far = {1: block, -1: block}
+    for step in range(1, count // 4 + 1):
+        last = 2 * step == count // 2
+        coming = {}
+        for way in (1, -1):
+            x = far[way][max(0, -way)] if last else far[way]
+            coming[way] = moved(x, 2 * way)
+        for way in (1, -1):
+            held[way * (2 * step - 1)] = moved(far[way], way)
+        if last:
+            held[2 * step] = jnp.stack([coming[1], coming[-1]])
+        else:
+            held[2 * step], held[-2 * step] = coming[1], coming[-1]
+        far = coming
+    return held
+
+
 def shards(tokens, expert_ids, gates, w_in, w_out):
     rows, width = tokens.shape
     owners = lax.axis_size("expert")
+    chips = lax.axis_size("z")
     hidden = w_out.shape[1]
     slots = owners * ROWS
     shape = jax.ShapeDtypeStruct
-
-    w_out_t = jnp.swapaxes(w_out, 1, 2)
-    gathered = [lax.all_gather(w, "z", axis=0) for w in (w_in[0], w_in[1], w_out_t)]
-    swapped = [lax.ppermute(w, "c", [(0, 1), (1, 0)]) for w in gathered]
-    weights = [w for pair in zip(gathered, swapped) for w in pair]
-
+    ids = expert_ids.T
+
+    block = jnp.concatenate([w_in, jnp.swapaxes(w_out, 1, 2)], axis=2)
+    held = all_blocks(block)
     outgoing = call(
         pack_kernel,
         shape((owners, ROWS, width), BF16),
-        (expert_ids, tokens),
+        (ids, tokens),
         2 * slots * rows * width,
         2 * slots * width,
     )
@@ -176,15 +210,27 @@
     high, low = call(
         functools.partial(gate_kernel, owners, ROWS),
         (shape((rows, slots), BF16), shape((rows, slots), BF16)),
-        (expert_ids, gates),
+        (ids, gates.T),
         2 * slots * rows * 256,
         4 * slots * rows,
     )
+    distances = sorted(held)
+    table = (lax.axis_index("z").astype(jnp.int32) - jnp.array(distances, jnp.int32)) % chips
+    anywhere = pl.BlockSpec(memory_space=pl.ANY)
+    own = pl.pallas_call(
+        assemble_kernel,
+        out_shape=shape((chips, *block.shape), BF16),
+        in_specs=[pl.BlockSpec(memory_space=pltpu.SMEM)] + [anywhere] * chips,
+        out_specs=anywhere,
+        scratch_shapes=[pltpu.SemaphoreType.DMA((chips,))],
+        cost_estimate=pl.CostEstimate(flops=0, bytes_accessed=4 * chips * block.size, transcendentals=0),
+    )(table, *[held[d] for d in distances])
+    other = lax.ppermute(own, "c", [(0, 1), (1, 0)])
     core = lax.axis_index("c").astype(jnp.int32).reshape(1)
     produced = call(
         expert_kernel,
         shape((owners, ROWS, width), BF16),
-        (core, arrived, *weights),
+        (core, arrived, own, other),
         2 * 1024 * 3 * hidden * width,
         4 * slots * width + 12 * hidden * width,
         smem=1,

time: 199 us -> 243 us (1.22)
  blocking collectives: 106 us -> 0 us
  Pallas kernels: 16 us -> 89.2 us
  starting transfers between devices: 32.5 us -> 96.7 us
  waiting for transfers between devices: 39.5 us -> 50.4 us
    all_gather x3 -> x0, blocking collectives: 106 us -> none  [shards(): lax.all_gather(w, 'z', axis=0)]
    pallas_call x0 -> x1, Pallas kernels: none -> 73.4 us  [shards(): pl.pallas_call(assemble_kernel, out_shape=shape((chips, *block.shape), BF...]
    ppermute x3 -> x17, starting transfers between devices: 5.73 us -> 76.6 us  [the longest x16 74.7 us: moved(): return lax.ppermute(x, 'z', [(i, (i + by) % count) for i in range(count)])]
    ppermute x3 -> x17, waiting for transfers between devices: 2.57 us -> 12.7 us  [the longest x16 7.87 us: moved(): return lax.ppermute(x, 'z', [(i, (i + by) % count) for i in range(count)])]
    all_to_all x1, starting transfers between devices: 16.9 us -> 10.4 us  [shards(): lax.all_to_all(outgoing, 'expert', split_axis=0, concat_axis=0, tiled=True)]
  transfers between devices with their start and end apart: 5 -> 19, of which waited for: 2 -> 7; matrix products, arithmetic and copies ran while one was open for 0% -> 1% of each run, Pallas kernels for 1% -> 33%
where the time goes in v2:
time: 243 us; the launch traced here: 242 us
  starting transfers between devices  96.7 us (40%)
  Pallas kernels  89.2 us (37%)
  waiting for transfers between devices  50.4 us (21%)
  local copies, waits for them, and re-layouts  3.08 us (1%)
    ppermute x16, starting transfers between devices, moved(): return lax.ppermute(x, 'z', [(i, (i + by) % count) for i in range(count)])  74.7 us
    pallas_call x1, Pallas kernels, shards(): pl.pallas_call(assemble_kernel, out_shape=shape((chips, *block.shape), BF...  73.4 us
    all_to_all x1, waiting for transfers between devices, shards(): lax.all_to_all(produced, 'expert', split_axis=0, concat_axis=0, tiled=True)  37.7 us
    pallas_call x4, Pallas kernels, call(): pl.pallas_call(kernel, out_shape=outs, in_specs=[scalar] * smem + [vmem]...  15.8 us
    all_to_all x1, starting transfers between devices, shards(): lax.all_to_all(outgoing, 'expert', split_axis=0, concat_axis=0, tiled=True)  10.4 us
    all_to_all x1, starting transfers between devices, shards(): lax.all_to_all(produced, 'expert', split_axis=0, concat_axis=0, tiled=True)  9.77 us
    ppermute x16, waiting for transfers between devices, moved(): return lax.ppermute(x, 'z', [(i, (i + by) % count) for i in range(count)])  7.87 us
  transfers between devices with their start and end apart: 19, of which 7 were waited for; matrix products, arithmetic and copies ran while one was open for 1% of the time, Pallas kernels for 33%

profile of v2, /device:TPU:4, one launch (start us, length us, event | category | flops | bytes accessed | tf_op | source)
XLA Modules:
  0.0 242.0 jit_solution(9242050768291440488)
XLA Ops:
  0.0 0.9 pad_maximum_fusion.refs_7_
  0.9 6.1 %collective-permute-start.8 = (bf16[2,32,1152]{2,1,0:T(8,128)(2,1)S(1)}, bf16[2,32,1152]{2,1,0:T(8,128)(2,1)S(1)}, u32[]{:S(2)}, u32[]{:S(2)}) collective-permute-start(bf16[2,32,1152]{2,1,0:T(8,128)(2,1)S(1)} %pad_maximum_fusion.refs_7_), channel_id=1, source_target_pairs={{0,128},{64,192},{128,256},{192,320},{256,384},{320,448},{384,512}... | collective-permute-start | bytes 442376 | tf_op jit(solution)/shard_map/ppermute | solution.py:171
  7.0 14.0 %collective-permute-start = (bf16[2,32,1152]{2,1,0:T(8,128)(2,1)S(1)}, bf16[2,32,1152]{2,1,0:T(8,128)(2,1)S(1)}, u32[]{:S(2)}, u32[]{:S(2)}) collective-permute-start(bf16[2,32,1152]{2,1,0:T(8,128)(2,1)S(1)} %pad_maximum_fusion.refs_7_), channel_id=1, source_target_pairs={{0,896},{64,960},{128,0},{192,64},{256,128},{320,192},{384,256},{4... | collective-permute-start | bytes 442376 | tf_op jit(solution)/shard_map/ppermute | solution.py:171
  21.1 2.0 collective-permute-done.8.refs_9_
  23.1 1.9 collective-permute-start.10
  25.1 2.3 collective-permute-done.refs_5_
  27.3 6.5 %collective-permute-start.1 = (bf16[2,32,1152]{2,1,0:T(8,128)(2,1)S(1)}, bf16[2,32,1152]{2,1,0:T(8,128)(2,1)S(1)}, u32[]{:S(2)}, u32[]{:S(2)}) collective-permute-start(bf16[2,32,1152]{2,1,0:T(8,128)(2,1)S(1)} %collective-permute-done.refs_5_), channel_id=1, source_target_pairs={{0,896},{64,960},{128,0},{192,64},{256,128},{320,192},{384,256},{4... | collective-permute-start | bytes 442376 | tf_op jit(solution)/shard_map/ppermute | solution.py:171
  33.9 0.0 collective-permute-done.10.refs_11_
  33.9 1.9 collective-permute-start.12
  35.8 8.1 %collective-permute-start.6 = (bf16[2,32,1152]{2,1,0:T(8,128)(2,1)S(1)}, bf16[2,32,1152]{2,1,0:T(8,128)(2,1)S(1)}, u32[]{:S(2)}, u32[]{:S(2)}) collective-permute-start(bf16[2,32,1152]{2,1,0:T(8,128)(2,1)S(1)} %pad_maximum_fusion.refs_7_), channel_id=1, source_target_pairs={{0,960},{64,0},{128,64},{192,128},{256,192},{320,256},{384,320},{4... | collective-permute-start | bytes 442376 | tf_op jit(solution)/shard_map/ppermute | solution.py:171
  43.9 1.9 collective-permute-start.7
  45.8 3.4 %shard_map.65 = bf16[32,24,1024]{2,1,0:T(8,128)(2,1)} custom-call(s32[8,64]{1,0:T(8,128)} %bitcast.13, bf16[64,1024]{1,0:T(8,128)(2,1)} %tok_ref.1), custom_call_target="tpu_custom_call" | custom-call | flops 100663296 | bytes 1572864 | tf_op jit(solution)/shard_map/pallas_call | solution.py:158
  49.2 10.4 %all-to-all-start = ((bf16[32,24,1024]{2,1,0:T(8,128)(2,1)}), bf16[32,24,1024]{2,1,0:T(8,128)(2,1)S(1)}, u32[]{:S(2)}, u32[]{:S(2)}) async-start(bf16[32,24,1024]{2,1,0:T(8,128)(2,1)} %shard_map.65), calls=%async_computation | async-start | bytes 3145728 | tf_op jit(solution)/shard_map/all_to_all | solution.py:209
  59.6 5.1 %collective-permute-start.5 = (bf16[2,32,1152]{2,1,0:T(8,128)(2,1)S(1)}, bf16[2,32,1152]{2,1,0:T(8,128)(2,1)S(1)}, u32[]{:S(2)}, u32[]{:S(2)}) collective-permute-start(bf16[2,32,1152]{2,1,0:T(8,128)(2,1)S(1)} %collective-permute-done.refs_5_), channel_id=1, source_target_pairs={{0,960},{64,0},{128,64},{192,128},{256,192},{320,256},{384,320},{4... | collective-permute-start | bytes 442376 | tf_op jit(solution)/shard_map/ppermute | solution.py:171
  64.8 0.0 collective-permute-done.1.refs_3_
  64.8 1.9 collective-permute-start.2
  66.7 0.0 collective-permute-done.12.refs_13_
  66.7 4.8 %collective-permute-start.14 = (bf16[32,1152]{1,0:T(8,128)(2,1)S(1)}, bf16[32,1152]{1,0:T(8,128)(2,1)S(1)}, u32[]{:S(2)}, u32[]{:S(2)}) collective-permute-start(bf16[32,1152]{1,0:T(8,128)(2,1)S(1)} %slice_bitcast_fusion.1), channel_id=1, source_target_pairs={{0,128},{64,192},{128,256},{192,320},{256,384},{320,448},{384,512}... | collective-permute-start | bytes 221192 | tf_op jit(solution)/shard_map/ppermute | solution.py:171
  71.6 1.6 collective-permute-done.2.refs_1_
  73.2 5.6 %collective-permute-start.15 = (bf16[32,1152]{1,0:T(8,128)(2,1)S(1)}, bf16[32,1152]{1,0:T(8,128)(2,1)S(1)}, u32[]{:S(2)}, u32[]{:S(2)}) collective-permute-start(bf16[32,1152]{1,0:T(8,128)(2,1)S(1)} %slice_bitcast_fusion), channel_id=1, source_target_pairs={{0,896},{64,960},{128,0},{192,64},{256,128},{320,192},{384,256},{4... | collective-permute-start | bytes 221192 | tf_op jit(solution)/shard_map/ppermute | solution.py:171
  78.8 0.5 and_select_fusion.table_ref
  79.3 0.0 collective-permute-done.6.refs_6_
  79.3 2.6 %collective-permute-start.9 = (bf16[2,32,1152]{2,1,0:T(8,128)(2,1)S(1)}, bf16[2,32,1152]{2,1,0:T(8,128)(2,1)S(1)}, u32[]{:S(2)}, u32[]{:S(2)}) collective-permute-start(bf16[2,32,1152]{2,1,0:T(8,128)(2,1)S(1)} %collective-permute-done.8.refs_9_), channel_id=1, source_target_pairs={{0,64},{64,128},{128,192},{192,256},{256,320},{320,384},{384,448},... | collective-permute-start | bytes 442376 | tf_op jit(solution)/shard_map/ppermute | solution.py:171
  81.9 0.0 collective-permute-done.7.refs_8_
  82.0 1.9 collective-permute-start.11
  83.9 0.0 collective-permute-done.5.refs_4_
  83.9 5.1 %collective-permute-start.4 = (bf16[2,32,1152]{2,1,0:T(8,128)(2,1)S(1)}, bf16[2,32,1152]{2,1,0:T(8,128)(2,1)S(1)}, u32[]{:S(2)}, u32[]{:S(2)}) collective-permute-start(bf16[2,32,1152]{2,1,0:T(8,128)(2,1)S(1)} %collective-permute-done.1.refs_3_), channel_id=1, source_target_pairs={{0,960},{64,0},{128,64},{192,128},{256,192},{320,256},{384,320},{4... | collective-permute-start | bytes 442376 | tf_op jit(solution)/shard_map/ppermute | solution.py:171
  89.1 0.0 collective-permute-done.14
  89.1 1.9 collective-permute-start.13
  91.0 0.0 collective-permute-done.15
  91.0 5.1 %collective-permute-start.3 = (bf16[2,32,1152]{2,1,0:T(8,128)(2,1)S(1)}, bf16[2,32,1152]{2,1,0:T(8,128)(2,1)S(1)}, u32[]{:S(2)}, u32[]{:S(2)}) collective-permute-start(bf16[2,32,1152]{2,1,0:T(8,128)(2,1)S(1)} %collective-permute-done.2.refs_1_), channel_id=1, source_target_pairs={{0,960},{64,0},{128,64},{192,128},{256,192},{320,256},{384,320},{4... | collective-permute-start | bytes 442376 | tf_op jit(solution)/shard_map/ppermute | solution.py:171
  96.2 0.7 pad_maximum_fusion.1.refs_15_
  96.8 0.0 collective-permute-done.9.refs_10_
  96.8 0.0 collective-permute-done.11.refs_12_
  96.9 0.0 collective-permute-done.4.refs_2_
  96.9 0.4 collective-permute-done.13.refs_14_
  97.3 1.5 collective-permute-done.3.refs_0_
  98.9 0.6 copy-done.16
  99.5 73.4 %shard_map.66.own_ref = bf16[16,2,32,1152]{3,2,1,0:T(8,128)(2,1)} custom-call(s32[16]{0:T(128)} %and_select_fusion.table_ref, bf16[2,32,1152]{2,1,0:T(8,128)(2,1)} %copy-done.16, bf16[2,32,1152]{2,1,0:T(8,128)(2,1)} %copy-done.4, bf16[2,32,1152]{2,1,0:T(8,128)(2,1)} %copy-done.14, bf16[2,32,1152]{2,1,0:T(8,128)(2,1)} %copy-done.8, ...), custom_call_target="tpu_custom_call" | custom-call | bytes 4718592 | tf_op jit(solution)/shard_map/pallas_call | solution.py:220
  172.9 1.9 collective-permute-start.16
  174.9 4.8 %collective-permute-done.16.other_ref = bf16[16,2,32,1152]{3,2,1,0:T(8,128)(2,1)} collective-permute-done((bf16[16,2,32,1152]{3,2,1,0:T(8,128)(2,1)}, bf16[16,2,32,1152]{3,2,1,0:T(8,128)(2,1)}, u32[]{:S(2)}, u32[]{:S(2)}) %collective-permute-start.16) | collective-permute-done | bytes 2359328 | tf_op jit(solution)/shard_map/ppermute | solution.py:228
  179.7 1.2 copy-done.1
  180.9 7.6 %shard_map.67 = bf16[32,24,1024]{2,1,0:T(8,128)(2,1)} custom-call(s32[1]{0:T(128)} %bitcast.2.core_ref, bf16[32,24,1024]{2,1,0:T(8,128)(2,1)} %copy-done.1, bf16[16,2,32,1152]{3,2,1,0:T(8,128)(2,1)} %shard_map.66.own_ref, bf16[16,2,32,1152]{3,2,1,0:T(8,128)(2,1)} %collective-permute-done.16.other_ref), custom_call_target="tpu_custom_call" | custom-call | flops 2415919104 | bytes 7864320 | tf_op jit(solution)/shard_map/pallas_call | solution.py:158
  188.4 9.8 %all-to-all-start.1 = ((bf16[32,24,1024]{2,1,0:T(8,128)(2,1)}), bf16[32,24,1024]{2,1,0:T(8,128)(2,1)S(1)}, u32[]{:S(2)}, u32[]{:S(2)}) async-start(bf16[32,24,1024]{2,1,0:T(8,128)(2,1)} %shard_map.67), calls=%async_computation.1 | async-start | bytes 3145728 | tf_op jit(solution)/shard_map/all_to_all | solution.py:238
  198.2 1.9 shard_map.64
  200.1 37.7 %all-to-all-done.1.back_ref = bf16[32,24,1024]{2,1,0:T(8,128)(2,1)S(1)} async-done(((bf16[32,24,1024]{2,1,0:T(8,128)(2,1)}), bf16[32,24,1024]{2,1,0:T(8,128)(2,1)S(1)}, u32[]{:S(2)}, u32[]{:S(2)}) %all-to-all-start.1) | async-done | bytes 1572896 | tf_op jit(solution)/shard_map/all_to_all | solution.py:238
  237.8 1.2 copy-done
  239.0 3.0 %shard_map.68 = bf16[64,1024]{1,0:T(8,128)(2,1)} custom-call(bf16[64,768]{1,0:T(8,128)(2,1)} %get-tuple-element.7.high_ref, bf16[64,768]{1,0:T(8,128)(2,1)} %get-tuple-element.8.low_ref, bf16[32,24,1024]{2,1,0:T(8,128)(2,1)} %copy-done), custom_call_target="tpu_custom_call" | custom-call | flops 201326592 | bytes 1572864 | tf_op jit(solution)/shard_map/pallas_call | solution.py:158
  (36 shorter events, 0.1 us)
Async XLA Ops:
  0.9 48.3 %copy-start.2 = (bf16[2,32,1152]{2,1,0:T(8,128)(2,1)}, bf16[2,32,1152]{2,1,0:T(8,128)(2,1)S(1)}, u32[]{:S(2)}) copy-start(bf16[2,32,1152]{2,1,0:T(8,128)(2,1)S(1)} %pad_maximum_fusion.refs_7_) | copy-start | bytes 442372
  0.9 22.2 %collective-permute-start.8 = (bf16[2,32,1152]{2,1,0:T(8,128)(2,1)S(1)}, bf16[2,32,1152]{2,1,0:T(8,128)(2,1)S(1)}, u32[]{:S(2)}, u32[]{:S(2)}) collective-permute-start(bf16[2,32,1152]{2,1,0:T(8,128)(2,1)S(1)} %pad_maximum_fusion.refs_7_), channel_id=1, source_target_pairs={{0,128},{64,192},{128,256},{192,320},{256,384},{320,448},{384,512}... | collective-permute-start | bytes 442376 | tf_op jit(solution)/shard_map/ppermute | solution.py:171
  7.0 20.3 %collective-permute-start = (bf16[2,32,1152]{2,1,0:T(8,128)(2,1)S(1)}, bf16[2,32,1152]{2,1,0:T(8,128)(2,1)S(1)}, u32[]{:S(2)}, u32[]{:S(2)}) collective-permute-start(bf16[2,32,1152]{2,1,0:T(8,128)(2,1)S(1)} %pad_maximum_fusion.refs_7_), channel_id=1, source_target_pairs={{0,896},{64,960},{128,0},{192,64},{256,128},{320,192},{384,256},{4... | collective-permute-start | bytes 442376 | tf_op jit(solution)/shard_map/ppermute | solution.py:171
  23.1 56.2 %copy-start.5 = (bf16[2,32,1152]{2,1,0:T(8,128)(2,1)}, bf16[2,32,1152]{2,1,0:T(8,128)(2,1)S(1)}, u32[]{:S(2)}) copy-start(bf16[2,32,1152]{2,1,0:T(8,128)(2,1)S(1)} %collective-permute-done.8.refs_9_) | copy-start | bytes 442372
  23.1 10.7 %collective-permute-start.10 = (bf16[2,32,1152]{2,1,0:T(8,128)(2,1)S(1)}, bf16[2,32,1152]{2,1,0:T(8,128)(2,1)S(1)}, u32[]{:S(2)}, u32[]{:S(2)}) collective-permute-start(bf16[2,32,1152]{2,1,0:T(8,128)(2,1)S(1)} %collective-permute-done.8.refs_9_), channel_id=1, source_target_pairs={{0,128},{64,192},{128,256},{192,320},{256,384},{320,448},{384,512}... | collective-permute-start | bytes 442376 | tf_op jit(solution)/shard_map/ppermute | solution.py:171
  27.3 32.3 %copy-start.6 = (bf16[2,32,1152]{2,1,0:T(8,128)(2,1)}, bf16[2,32,1152]{2,1,0:T(8,128)(2,1)S(1)}, u32[]{:S(2)}) copy-start(bf16[2,32,1152]{2,1,0:T(8,128)(2,1)S(1)} %collective-permute-done.refs_5_) | copy-start | bytes 442372
  27.3 37.4 %collective-permute-start.1 = (bf16[2,32,1152]{2,1,0:T(8,128)(2,1)S(1)}, bf16[2,32,1152]{2,1,0:T(8,128)(2,1)S(1)}, u32[]{:S(2)}, u32[]{:S(2)}) collective-permute-start(bf16[2,32,1152]{2,1,0:T(8,128)(2,1)S(1)} %collective-permute-done.refs_5_), channel_id=1, source_target_pairs={{0,896},{64,960},{128,0},{192,64},{256,128},{320,192},{384,256},{4... | collective-permute-start | bytes 442376 | tf_op jit(solution)/shard_map/ppermute | solution.py:171
  33.9 48.1 %copy-start.7 = (bf16[2,32,1152]{2,1,0:T(8,128)(2,1)}, bf16[2,32,1152]{2,1,0:T(8,128)(2,1)S(1)}, u32[]{:S(2)}) copy-start(bf16[2,32,1152]{2,1,0:T(8,128)(2,1)S(1)} %collective-permute-done.10.refs_11_) | copy-start | bytes 442372
  33.9 32.8 %collective-permute-start.12 = (bf16[2,32,1152]{2,1,0:T(8,128)(2,1)S(1)}, bf16[2,32,1152]{2,1,0:T(8,128)(2,1)S(1)}, u32[]{:S(2)}, u32[]{:S(2)}) collective-permute-start(bf16[2,32,1152]{2,1,0:T(8,128)(2,1)S(1)} %collective-permute-done.10.refs_11_), channel_id=1, source_target_pairs={{0,128},{64,192},{128,256},{192,320},{256,384},{320,448},{384,512}... | collective-permute-start | bytes 442376 | tf_op jit(solution)/shard_map/ppermute | solution.py:171
  35.8 43.5 %collective-permute-start.6 = (bf16[2,32,1152]{2,1,0:T(8,128)(2,1)S(1)}, bf16[2,32,1152]{2,1,0:T(8,128)(2,1)S(1)}, u32[]{:S(2)}, u32[]{:S(2)}) collective-permute-start(bf16[2,32,1152]{2,1,0:T(8,128)(2,1)S(1)} %pad_maximum_fusion.refs_7_), channel_id=1, source_target_pairs={{0,960},{64,0},{128,64},{192,128},{256,192},{320,256},{384,320},{4... | collective-permute-start | bytes 442376 | tf_op jit(solution)/shard_map/ppermute | solution.py:171
  43.9 38.0 %collective-permute-start.7 = (bf16[2,32,1152]{2,1,0:T(8,128)(2,1)S(1)}, bf16[2,32,1152]{2,1,0:T(8,128)(2,1)S(1)}, u32[]{:S(2)}, u32[]{:S(2)}) collective-permute-start(bf16[2,32,1152]{2,1,0:T(8,128)(2,1)S(1)} %pad_maximum_fusion.refs_7_), channel_id=1, source_target_pairs={{0,64},{64,128},{128,192},{192,256},{256,320},{320,384},{384,448},... | collective-permute-start | bytes 442376 | tf_op jit(solution)/shard_map/ppermute | solution.py:171
  49.2 29.5 %copy-start.17 = (s32[16]{0:T(128)S(1)}, s32[16]{0:T(128)}, u32[]{:S(2)}) copy-start(s32[16]{0:T(128)} %constant.35) | copy-start | bytes 196
  49.2 130.5 %all-to-all-start = ((bf16[32,24,1024]{2,1,0:T(8,128)(2,1)}), bf16[32,24,1024]{2,1,0:T(8,128)(2,1)S(1)}, u32[]{:S(2)}, u32[]{:S(2)}) async-start(bf16[32,24,1024]{2,1,0:T(8,128)(2,1)} %shard_map.65), calls=%async_computation | async-start | bytes 3145728 | tf_op jit(solution)/shard_map/all_to_all | solution.py:209
  59.6 24.3 %collective-permute-start.5 = (bf16[2,32,1152]{2,1,0:T(8,128)(2,1)S(1)}, bf16[2,32,1152]{2,1,0:T(8,128)(2,1)S(1)}, u32[]{:S(2)}, u32[]{:S(2)}) collective-permute-start(bf16[2,32,1152]{2,1,0:T(8,128)(2,1)S(1)} %collective-permute-done.refs_5_), channel_id=1, source_target_pairs={{0,960},{64,0},{128,64},{192,128},{256,192},{320,256},{384,320},{4... | collective-permute-start | bytes 442376 | tf_op jit(solution)/shard_map/ppermute | solution.py:171
  64.8 34.0 %copy-start.8 = (bf16[2,32,1152]{2,1,0:T(8,128)(2,1)}, bf16[2,32,1152]{2,1,0:T(8,128)(2,1)S(1)}, u32[]{:S(2)}) copy-start(bf16[2,32,1152]{2,1,0:T(8,128)(2,1)S(1)} %collective-permute-done.1.refs_3_) | copy-start | bytes 442372
  64.8 8.4 %collective-permute-start.2 = (bf16[2,32,1152]{2,1,0:T(8,128)(2,1)S(1)}, bf16[2,32,1152]{2,1,0:T(8,128)(2,1)S(1)}, u32[]{:S(2)}, u32[]{:S(2)}) collective-permute-start(bf16[2,32,1152]{2,1,0:T(8,128)(2,1)S(1)} %collective-permute-done.1.refs_3_), channel_id=1, source_target_pairs={{0,896},{64,960},{128,0},{192,64},{256,128},{320,192},{384,256},{4... | collective-permute-start | bytes 442376 | tf_op jit(solution)/shard_map/ppermute | solution.py:171
  66.7 32.1 %copy-start.3 = (bf16[2,32,1152]{2,1,0:T(8,128)(2,1)}, bf16[2,32,1152]{2,1,0:T(8,128)(2,1)S(1)}, u32[]{:S(2)}) copy-start(bf16[2,32,1152]{2,1,0:T(8,128)(2,1)S(1)} %collective-permute-done.12.refs_13_) | copy-start | bytes 442372
  66.7 22.3 %collective-permute-start.14 = (bf16[32,1152]{1,0:T(8,128)(2,1)S(1)}, bf16[32,1152]{1,0:T(8,128)(2,1)S(1)}, u32[]{:S(2)}, u32[]{:S(2)}) collective-permute-start(bf16[32,1152]{1,0:T(8,128)(2,1)S(1)} %slice_bitcast_fusion.1), channel_id=1, source_target_pairs={{0,128},{64,192},{128,256},{192,320},{256,384},{320,448},{384,512}... | collective-permute-start | bytes 221192 | tf_op jit(solution)/shard_map/ppermute | solution.py:171
  73.2 25.7 %copy-start.4 = (bf16[2,32,1152]{2,1,0:T(8,128)(2,1)}, bf16[2,32,1152]{2,1,0:T(8,128)(2,1)S(1)}, u32[]{:S(2)}) copy-start(bf16[2,32,1152]{2,1,0:T(8,128)(2,1)S(1)} %collective-permute-done.2.refs_1_) | copy-start | bytes 442372
  73.2 17.8 %collective-permute-start.15 = (bf16[32,1152]{1,0:T(8,128)(2,1)S(1)}, bf16[32,1152]{1,0:T(8,128)(2,1)S(1)}, u32[]{:S(2)}, u32[]{:S(2)}) collective-permute-start(bf16[32,1152]{1,0:T(8,128)(2,1)S(1)} %slice_bitcast_fusion), channel_id=1, source_target_pairs={{0,896},{64,960},{128,0},{192,64},{256,128},{320,192},{384,256},{4... | collective-permute-start | bytes 221192 | tf_op jit(solution)/shard_map/ppermute | solution.py:171
  79.3 19.5 %copy-start.9 = (bf16[2,32,1152]{2,1,0:T(8,128)(2,1)}, bf16[2,32,1152]{2,1,0:T(8,128)(2,1)S(1)}, u32[]{:S(2)}) copy-start(bf16[2,32,1152]{2,1,0:T(8,128)(2,1)S(1)} %collective-permute-done.6.refs_6_) | copy-start | bytes 442372
  79.3 17.5 %collective-permute-start.9 = (bf16[2,32,1152]{2,1,0:T(8,128)(2,1)S(1)}, bf16[2,32,1152]{2,1,0:T(8,128)(2,1)S(1)}, u32[]{:S(2)}, u32[]{:S(2)}) collective-permute-start(bf16[2,32,1152]{2,1,0:T(8,128)(2,1)S(1)} %collective-permute-done.8.refs_9_), channel_id=1, source_target_pairs={{0,64},{64,128},{128,192},{192,256},{256,320},{320,384},{384,448},... | collective-permute-start | bytes 442376 | tf_op jit(solution)/shard_map/ppermute | solution.py:171
  82.0 16.9 %copy-start.10 = (bf16[2,32,1152]{2,1,0:T(8,128)(2,1)}, bf16[2,32,1152]{2,1,0:T(8,128)(2,1)S(1)}, u32[]{:S(2)}) copy-start(bf16[2,32,1152]{2,1,0:T(8,128)(2,1)S(1)} %collective-permute-done.7.refs_8_) | copy-start | bytes 442372
  82.0 14.9 %collective-permute-start.11 = (bf16[2,32,1152]{2,1,0:T(8,128)(2,1)S(1)}, bf16[2,32,1152]{2,1,0:T(8,128)(2,1)S(1)}, u32[]{:S(2)}, u32[]{:S(2)}) collective-permute-start(bf16[2,32,1152]{2,1,0:T(8,128)(2,1)S(1)} %collective-permute-done.10.refs_11_), channel_id=1, source_target_pairs={{0,64},{64,128},{128,192},{192,256},{256,320},{320,384},{384,448},... | collective-permute-start | bytes 442376 | tf_op jit(solution)/shard_map/ppermute | solution.py:171
  83.9 14.9 %copy-start.11 = (bf16[2,32,1152]{2,1,0:T(8,128)(2,1)}, bf16[2,32,1152]{2,1,0:T(8,128)(2,1)S(1)}, u32[]{:S(2)}) copy-start(bf16[2,32,1152]{2,1,0:T(8,128)(2,1)S(1)} %collective-permute-done.5.refs_4_) | copy-start | bytes 442372
  83.9 12.9 %collective-permute-start.4 = (bf16[2,32,1152]{2,1,0:T(8,128)(2,1)S(1)}, bf16[2,32,1152]{2,1,0:T(8,128)(2,1)S(1)}, u32[]{:S(2)}, u32[]{:S(2)}) collective-permute-start(bf16[2,32,1152]{2,1,0:T(8,128)(2,1)S(1)} %collective-permute-done.1.refs_3_), channel_id=1, source_target_pairs={{0,960},{64,0},{128,64},{192,128},{256,192},{320,256},{384,320},{4... | collective-permute-start | bytes 442376 | tf_op jit(solution)/shard_map/ppermute | solution.py:171
  89.1 8.2 %collective-permute-start.13 = (bf16[2,32,1152]{2,1,0:T(8,128)(2,1)S(1)}, bf16[2,32,1152]{2,1,0:T(8,128)(2,1)S(1)}, u32[]{:S(2)}, u32[]{:S(2)}) collective-permute-start(bf16[2,32,1152]{2,1,0:T(8,128)(2,1)S(1)} %collective-permute-done.12.refs_13_), channel_id=1, source_target_pairs={{0,64},{64,128},{128,192},{192,256},{256,320},{320,384},{384,448},... | collective-permute-start | bytes 442376 | tf_op jit(solution)/shard_map/ppermute | solution.py:171
  91.0 7.8 %collective-permute-start.3 = (bf16[2,32,1152]{2,1,0:T(8,128)(2,1)S(1)}, bf16[2,32,1152]{2,1,0:T(8,128)(2,1)S(1)}, u32[]{:S(2)}, u32[]{:S(2)}) collective-permute-start(bf16[2,32,1152]{2,1,0:T(8,128)(2,1)S(1)} %collective-permute-done.2.refs_1_), channel_id=1, source_target_pairs={{0,960},{64,0},{128,64},{192,128},{256,192},{320,256},{384,320},{4... | collective-permute-start | bytes 442376 | tf_op jit(solution)/shard_map/ppermute | solution.py:171
  96.8 2.0 copy-start.12
  96.8 2.0 copy-start.13
  96.9 2.0 copy-start.14
  97.3 1.6 copy-start.15
  98.9 0.7 copy-start.16
  172.9 6.8 %collective-permute-start.16 = (bf16[16,2,32,1152]{3,2,1,0:T(8,128)(2,1)}, bf16[16,2,32,1152]{3,2,1,0:T(8,128)(2,1)}, u32[]{:S(2)}, u32[]{:S(2)}) collective-permute-start(bf16[16,2,32,1152]{3,2,1,0:T(8,128)(2,1)} %shard_map.66.own_ref), channel_id=1, source_target_pairs={{0,32},{32,0},{1,33},{33,1},{2,34},{34,2},{3,35},{35,3},{4,36},{36... | collective-permute-start | bytes 7077896 | tf_op jit(solution)/shard_map/ppermute | solution.py:228
  179.7 1.2 copy-start.1
  188.4 49.4 %all-to-all-start.1 = ((bf16[32,24,1024]{2,1,0:T(8,128)(2,1)}), bf16[32,24,1024]{2,1,0:T(8,128)(2,1)S(1)}, u32[]{:S(2)}, u32[]{:S(2)}) async-start(bf16[32,24,1024]{2,1,0:T(8,128)(2,1)} %shard_map.67), calls=%async_computation.1 | async-start | bytes 3145728 | tf_op jit(solution)/shard_map/all_to_all | solution.py:238
  237.8 1.2 copy-start

commit v3 on v2

--- a/solution.py
+++ b/solution.py
@@ -7,7 +7,6 @@
 from jax.experimental.pallas import tpu as pltpu
 from jax.sharding import Mesh
 from jax.sharding import PartitionSpec as P
-
 
 BF16 = jnp.bfloat16
 F32 = jnp.float32
@@ -37,10 +36,9 @@
     return lax.dot_general(a, b, (((1,), (1,)), ((), ())), preferred_element_type=F32)
 
 
-def half_order(transposed):
-    shape = (256, 256)
-    j, k = iota(shape, 1 if transposed else 0), iota(shape, 0 if transposed else 1)
-    goes_to = ((j // BLOCK) % 2) * 128 + (j // (2 * BLOCK)) * BLOCK + j % BLOCK
+def chip_order():
+    j, k = iota((256, 256), 0), iota((256, 256), 1)
+    goes_to = ((j // BLOCK) % 4) * (2 * BLOCK) + (j // 128) * BLOCK + j % BLOCK
     return (goes_to == k).astype(F32).astype(BF16)
 
 
@@ -69,13 +67,8 @@
     shape = (owners, per, rows)
     slot = (which_slot(iota(shape, 1)) + 1).astype(F32).reshape(owners * per, rows)
     pick = (found == slot).astype(F32).astype(BF16)
-    order = half_order(False)
-    for g in range(width // 256):
-        cols = dot(tok_ref[:, g * 256 : (g + 1) * 256], order).astype(BF16)
-        for h in range(2):
-            placed = dot(pick, cols[:, h * 128 : (h + 1) * 128]).astype(BF16)
-            at = h * (width // 2) + g * 128
-            out_ref[:, :, at : at + 128] = placed.reshape(owners, per, 128)
+    placed = dot(pick, tok_ref[...]).astype(BF16)
+    out_ref[...] = placed.reshape(owners, per, width)
 
 
 def gate_kernel(owners, per, ids_ref, gates_ref, high_ref, low_ref):
@@ -97,38 +90,23 @@
     low_ref[...] = jnp.where(here, dot(named, low), 0.0).astype(BF16).T
 
 
-def assemble_kernel(table_ref, *refs):
-    *blocks, out_ref, sems = refs
-    copies = []
-    for k, block in enumerate(blocks):
-        copies.append(pltpu.make_async_copy(block, out_ref.at[table_ref[k]], sems.at[k]))
-    for copy in copies:
-        copy.start()
-    for copy in copies:
-        copy.wait()
-
-
-def expert_kernel(core_ref, x_ref, own_ref, other_ref, y_ref):
-    owners, _, width = x_ref.shape
+def expert_kernel(core_ref, x_ref, in_ref, own_ref, other_ref, y_ref):
+    owners, per, width = x_ref.shape
     half = width // 2
-    hidden = own_ref.shape[-1] // 3
+    hidden = own_ref.shape[-1]
     core = core_ref[0]
     own = pl.ds(pl.multiple_of(core * half, half), half)
     other = pl.ds(pl.multiple_of((1 - core) * half, half), half)
     sides = ((own, own_ref), (other, other_ref))
     results = []
     for e in range(2):
-        joint = 0.0
-        for at, w_ref in sides:
-            full = x_ref[:, e * 8 : e * 8 + 8, at].reshape(owners * 8, half)
-            rest = x_ref[:, 16:24, at].reshape(owners * 8, half)
-            part = jnp.concatenate([full, rest], axis=0)
-            joint = joint + dot(part, w_ref[:, e, :, : 2 * hidden].reshape(half, 2 * hidden))
+        full = x_ref[:, e * 8 : e * 8 + 8, :].reshape(owners * 8, width)
+        rest = x_ref[:, 16:24, :].reshape(owners * 8, width)
+        rows = jnp.concatenate([full, rest], axis=0)
+        joint = dot(rows, in_ref[:, e].reshape(width, 2 * hidden))
         gate, up = joint[:, :hidden], joint[:, hidden:]
         activated = (gate * jax.nn.sigmoid(gate) * up).astype(BF16)
-        results.append(
-            [dot_t(activated, w_ref[:, e, :, 2 * hidden :].reshape(half, hidden)) for _, w_ref in sides]
-        )
+        results.append([dot_t(activated, w_ref[:, e].reshape(half, hidden)) for _, w_ref in sides])
     shape = (owners, 8, half)
     first = iota(shape, 1) < 4
     n = owners * 8
@@ -144,7 +122,7 @@
     back = back_ref[...].reshape(owners * per, width)
     mixed = dot(high_ref[...], back) + dot(low_ref[...], back)
     mixed = mixed.astype(BF16)
-    order = half_order(True)
+    order = chip_order()
     for g in range(width // 256):
         at = g * 128
         halves = [mixed[:, at : at + 128], mixed[:, width // 2 + at : width // 2 + at + 128]]
@@ -164,41 +142,15 @@
     )(*args)
 
 
-def all_blocks(block):
-    count = lax.axis_size("z")
-
-    def moved(x, by):
-        return lax.ppermute(x, "z", [(i, (i + by) % count) for i in range(count)])
-
-    held = {0: block}
-    far = {1: block, -1: block}
-    for step in range(1, count // 4 + 1):
-        last = 2 * step == count // 2
-        coming = {}
-        for way in (1, -1):
-            x = far[way][max(0, -way)] if last else far[way]
-            coming[way] = moved(x, 2 * way)
-        for way in (1, -1):
-            held[way * (2 * step - 1)] = moved(far[way], way)
-        if last:
-            held[2 * step] = jnp.stack([coming[1], coming[-1]])
-        else:
-            held[2 * step], held[-2 * step] = coming[1], coming[-1]
-        far = coming
-    return held
-
-
 def shards(tokens, expert_ids, gates, w_in, w_out):
     rows, width = tokens.shape
     owners = lax.axis_size("expert")
-    chips = lax.axis_size("z")
     hidden = w_out.shape[1]
     slots = owners * ROWS
     shape = jax.ShapeDtypeStruct
     ids = expert_ids.T
 
-    block = jnp.concatenate([w_in, jnp.swapaxes(w_out, 1, 2)], axis=2)
-    held = all_blocks(block)
+    whole_in = lax.all_gather(w_in, DP, axis=0)
     outgoing = call(
         pack_kernel,
         shape((owners, ROWS, width), BF16),
@@ -207,6 +159,8 @@
         2 * slots * width,
     )
     arrived = lax.all_to_all(outgoing, "expert", split_axis=0, concat_axis=0, tiled=True)
+    own_out = lax.all_gather(jnp.swapaxes(w_out, 1, 2), "z", axis=0)
+    other_out = lax.ppermute(own_out, "c", [(0, 1), (1, 0)])
     high, low = call(
         functools.partial(gate_kernel, owners, ROWS),
         (shape((rows, slots), BF16), shape((rows, slots), BF16)),
@@ -214,27 +168,16 @@
         2 * slots * rows * 256,
         4 * slots * rows,
     )
-    distances = sorted(held)
-    table = (lax.axis_index("z").astype(jnp.int32) - jnp.array(distances, jnp.int32)) % chips
-    anywhere = pl.BlockSpec(memory_space=pl.ANY)
-    own = pl.pallas_call(
-        assemble_kernel,
-        out_shape=shape((chips, *block.shape), BF16),
-        in_specs=[pl.BlockSpec(memory_space=pltpu.SMEM)] + [anywhere] * chips,
-        out_specs=anywhere,
-        scratch_shapes=[pltpu.SemaphoreType.DMA((chips,))],
-        cost_estimate=pl.CostEstimate(flops=0, bytes_accessed=4 * chips * block.size, transcendentals=0),
-    )(table, *[held[d] for d in distances])
-    other = lax.ppermute(own, "c", [(0, 1), (1, 0)])
     core = lax.axis_index("c").astype(jnp.int32).reshape(1)
     produced = call(
         expert_kernel,
         shape((owners, ROWS, width), BF16),
-        (core, arrived, own, other),
+        (core, arrived, whole_in, own_out, other_out),
         2 * 1024 * 3 * hidden * width,
         4 * slots * width + 12 * hidden * width,
         smem=1,
     )
+    produced, high, low = lax.optimization_barrier((produced, high, low))
     came_back = lax.all_to_all(produced, "expert", split_axis=0, concat_axis=0, tiled=True)
     return call(
         combine_kernel,

time: 243 us -> 162 us (0.67)
  the two profiles are of different devices: /device:TPU:4 before, /device:TPU:8 now
where the time goes in v3:
time: 162 us
  blocking collectives  91.3 us (56%)
  waiting for transfers between devices  22.9 us (14%)
  starting transfers between devices  18.8 us (12%)
  Pallas kernels  15.2 us (9%)
  between operations  13.4 us (8%)
    all_to_all x1, blocking collectives, shards(): lax.all_to_all(produced, 'expert', split_axis=0, concat_axis=0, tiled=True)  49.4 us
    all_gather x1, blocking collectives, shards(): own_out = lax.all_gather(jnp.swapaxes(w_out, 1, 2), 'z', axis=0)  41.9 us
    all_gather x1, waiting for transfers between devices, shards(): whole_in = lax.all_gather(w_in, DP, axis=0)  21.8 us
    all_to_all x1, starting transfers between devices, shards(): lax.all_to_all(outgoing, 'expert', split_axis=0, concat_axis=0, tiled=True)  16.8 us
    pallas_call x4, Pallas kernels, call(): pl.pallas_call(kernel, out_shape=outs, in_specs=[scalar] * smem + [vmem]...  15.2 us
  transfers between devices with their start and end apart: 3, of which 2 were waited for; matrix products, arithmetic and copies ran while one was open for 0% of the time, Pallas kernels for 3%

profile of v3, /device:TPU:8, one launch (start us, length us, event | category | flops | bytes accessed | tf_op | source)
XLA Modules:
  0.0 161.6 jit_solution(17356041302258704783)
XLA Ops:
  6.5 0.0 all-gather.4.cloned.1.call-start
  6.5 0.7 all-gather.4.cloned.1.call-update
  7.3 2.9 %shard_map.55 = bf16[32,24,1024]{2,1,0:T(8,128)(2,1)} custom-call(s32[8,64]{1,0:T(8,128)} %bitcast.9, bf16[64,1024]{1,0:T(8,128)(2,1)} %tok_ref.1), custom_call_target="tpu_custom_call" | custom-call | flops 100663296 | bytes 1572864 | tf_op jit(solution)/shard_map/pallas_call | solution.py:136
  10.2 0.0 copy-start.2
  10.2 16.8 %all-to-all-start = ((bf16[32,24,1024]{2,1,0:T(8,128)(2,1)}), bf16[32,24,1024]{2,1,0:T(8,128)(2,1)S(1)}, u32[]{:S(2)}, u32[]{:S(2)}) async-start(bf16[32,24,1024]{2,1,0:T(8,128)(2,1)} %shard_map.55), calls=%async_computation | async-start | bytes 3145728 | tf_op jit(solution)/shard_map/all_to_all | solution.py:161
  27.0 0.0 copy-done.2
  27.0 41.9 %all-gather.1 = bf16[32,32,384]{2,1,0:T(8,128)(2,1)S(1)} all-gather(bf16[2,32,384]{2,1,0:T(8,128)(2,1)S(1)} %bitcast.8), channel_id=3, replica_groups=mesh['z'=16,'c'=2,'expert'=32] {'z'}, dimensions={0}, use_global_device_ids=true | all-gather | bytes 835584 | tf_op jit(solution)/shard_map/all_gather | solution.py:162
  68.9 0.0 copy-start.1
  68.9 1.9 %collective-permute-start = (bf16[16,2,32,384]{3,2,1,0:T(8,128)(2,1)S(1)}, bf16[16,2,32,384]{3,2,1,0:T(8,128)(2,1)S(1)}, u32[]{:S(2)}, u32[]{:S(2)}) collective-permute-start(bf16[16,2,32,384]{3,2,1,0:T(8,128)(2,1)S(1)} %bitcast.6), channel_id=1, source_target_pairs={{0,32},{32,0},{1,33},{33,1},{2,34},{34,2},{3,35},{35,3},{4,36},{36... | collective-permute-start | bytes 2359304 | tf_op jit(solution)/shard_map/ppermute | solution.py:163
  70.8 1.9 %shard_map.57 = (bf16[64,768]{1,0:T(8,128)(2,1)}, bf16[64,768]{1,0:T(8,128)(2,1)}) custom-call(s32[8,64]{1,0:T(8,128)} %bitcast.10, f32[8,64]{1,0:T(8,128)} %bitcast.12), custom_call_target="tpu_custom_call" | custom-call | flops 25165824 | bytes 196608 | tf_op jit(solution)/shard_map/pallas_call | solution.py:136
  72.7 0.4 collective-permute-done.other_ref
  73.1 0.0 copy-start.3
  73.1 0.0 all-to-all-done.x_ref
  73.1 0.0 copy-start
  73.1 21.8 %all-gather.4.cloned.1.call-done = bf16[64,32,768]{2,1,0:T(8,128)(2,1)} async-done(((bf16[2,32,768]{2,1,0:T(8,128)(2,1)}), bf16[64,32,768]{2,1,0:T(8,128)(2,1)}) %all-gather.4.cloned.1.call-update) | async-done | bytes 3145744 | tf_op jit(solution)/shard_map/all_gather | solution.py:153
  94.9 0.0 copy-done.1
  94.9 0.0 copy-done.3
  94.9 0.0 copy-done
  94.9 7.4 %shard_map.56 = bf16[32,24,1024]{2,1,0:T(8,128)(2,1)} custom-call(s32[1]{0:T(128)} %bitcast.core_ref, bf16[32,24,1024]{2,1,0:T(8,128)(2,1)} %copy-done, bf16[32,2,32,768]{3,2,1,0:T(8,128)(2,1)} %bitcast.11, bf16[16,2,32,384]{3,2,1,0:T(8,128)(2,1)} %bitcast.7, bf16[16,2,32,384]{3,2,1,0:T(8,128)(2,1)} %copy-done.3), custom_call_target="tpu_custom_call" | custom-call | flops 2415919104 | bytes 7864320 | tf_op jit(solution)/shard_map/pallas_call | solution.py:136
  102.4 49.4 %all_to_all.10.back_ref = bf16[32,24,1024]{2,1,0:T(8,128)(2,1)} all-to-all(bf16[32,24,1024]{2,1,0:T(8,128)(2,1)} %shard_map.56), channel_id=1, replica_groups=mesh['z'=16,'c'=2,'expert'=32] {'expert'}, dimensions={0} | all-to-all | bytes 3145728 | tf_op jit(solution)/shard_map/all_to_all | solution.py:181
  151.7 3.0 %shard_map.58 = bf16[64,1024]{1,0:T(8,128)(2,1)} custom-call(bf16[64,768]{1,0:T(8,128)(2,1)} %get-tuple-element.12.high_ref, bf16[64,768]{1,0:T(8,128)(2,1)} %get-tuple-element.13.low_ref, bf16[32,24,1024]{2,1,0:T(8,128)(2,1)} %all_to_all.10.back_ref), custom_call_target="tpu_custom_call" | custom-call | flops 201326592 | bytes 1572864 | tf_op jit(solution)/shard_map/pallas_call | solution.py:136
Async XLA Ops:
  6.5 88.4 %all-gather.4.cloned.1.call-start = ((), (), s32[]{:S(2)}) async-start(), calls=%async_computation.2 | async-start | bytes 3244032 | tf_op jit(solution)/shard_map/all_gather | solution.py:153
  10.2 16.9 %copy-start.2 = (bf16[2,384,32]{1,2,0:T(8,128)(2,1)S(1)}, bf16[2,384,32]{1,2,0:T(8,128)(2,1)}, u32[]{:S(2)}) copy-start(bf16[2,384,32]{1,2,0:T(8,128)(2,1)} %param.9) | copy-start | bytes 147460
  10.2 62.9 %all-to-all-start = ((bf16[32,24,1024]{2,1,0:T(8,128)(2,1)}), bf16[32,24,1024]{2,1,0:T(8,128)(2,1)S(1)}, u32[]{:S(2)}, u32[]{:S(2)}) async-start(bf16[32,24,1024]{2,1,0:T(8,128)(2,1)} %shard_map.55), calls=%async_computation | async-start | bytes 3145728 | tf_op jit(solution)/shard_map/all_to_all | solution.py:161
  68.9 26.0 %copy-start.1 = (bf16[32,32,384]{2,1,0:T(8,128)(2,1)}, bf16[32,32,384]{2,1,0:T(8,128)(2,1)S(1)}, u32[]{:S(2)}) copy-start(bf16[32,32,384]{2,1,0:T(8,128)(2,1)S(1)} %all-gather.1) | copy-start | bytes 2359300
  68.9 4.2 %collective-permute-start = (bf16[16,2,32,384]{3,2,1,0:T(8,128)(2,1)S(1)}, bf16[16,2,32,384]{3,2,1,0:T(8,128)(2,1)S(1)}, u32[]{:S(2)}, u32[]{:S(2)}) collective-permute-start(bf16[16,2,32,384]{3,2,1,0:T(8,128)(2,1)S(1)} %bitcast.6), channel_id=1, source_target_pairs={{0,32},{32,0},{1,33},{33,1},{2,34},{34,2},{3,35},{35,3},{4,36},{36... | collective-permute-start | bytes 2359304 | tf_op jit(solution)/shard_map/ppermute | solution.py:163
  73.1 21.8 %copy-start.3 = (bf16[16,2,32,384]{3,2,1,0:T(8,128)(2,1)}, bf16[16,2,32,384]{3,2,1,0:T(8,128)(2,1)S(1)}, u32[]{:S(2)}) copy-start(bf16[16,2,32,384]{3,2,1,0:T(8,128)(2,1)S(1)} %collective-permute-done.other_ref) | copy-start | bytes 2359300
  73.1 21.8 %copy-start = (bf16[32,24,1024]{2,1,0:T(8,128)(2,1)}, bf16[32,24,1024]{2,1,0:T(8,128)(2,1)S(1)}, u32[]{:S(2)}) copy-start(bf16[32,24,1024]{2,1,0:T(8,128)(2,1)S(1)} %all-to-all-done.x_ref) | copy-start | bytes 4718596
Sparse Core Ops, SparseCore 0:
  10.0 84.8 all-gather.3

commit v4 on v3

v4 whole, which is shorter than its diff:
```python
import functools

import jax
import jax.numpy as jnp
from jax import lax
from jax.experimental import pallas as pl
from jax.experimental.pallas import tpu as pltpu
from jax.sharding import Mesh
from jax.sharding import PartitionSpec as P

BF16 = jnp.bfloat16
F32 = jnp.float32
DP = ("z", "c")
ALL = ("z", "c", "expert")
ROWS = 24
BLOCK = 32


def iota(shape, dim):
    return lax.broadcasted_iota(jnp.int32, shape, dim)


def which_expert(q):
    return jnp.where((q >= 20) | ((q >= 8) & (q < 16)), 1, 0)


def which_slot(q):
    return jnp.where(q < 8, q, jnp.where(q < 20, q - 8, q - 12))


def dot(a, b):
    return jnp.dot(a, b, preferred_element_type=F32)


def dot_t(a, b):
    return lax.dot_general(a, b, (((1,), (1,)), ((), ())), preferred_element_type=F32)


def places(ids, experts):
    top, rows = ids.shape
    line = iota((experts, rows), 0)
    routed = jnp.zeros((experts, rows), F32)
    for k in range(top):
        routed = routed + (ids[k : k + 1, :] == line).astype(F32)
    earlier = (iota((rows, rows), 0) < iota((rows, rows), 1)).astype(F32).astype(BF16)
    before = dot(routed.astype(BF16), earlier)
    return jnp.where(routed > 0, before + 1.0, 0.0)


def row_owners(owners, per):
    shape = (owners, per, 2 * owners)
    named = 2 * iota(shape, 0) + which_expert(iota(shape, 1)) == iota(shape, 2)
    return named.astype(F32).astype(BF16).reshape(owners * per, 2 * owners)


def pack_kernel(ids_ref, tok_ref, out_ref):
    owners, per, width = out_ref.shape
    rows = ids_ref.shape[1]
    place = places(ids_ref[...], 2 * owners)
    found = dot(row_owners(owners, per), place.astype(BF16))
    shape = (owners, per, rows)
    slot = (which_slot(iota(shape, 1)) + 1).astype(F32).reshape(owners * per, rows)
    pick = (found == slot).astype(F32).astype(BF16)
    placed = dot(pick, tok_ref[...]).astype(BF16)
    out_ref[...] = placed.reshape(owners, per, width)


def gate_kernel(owners, per, ids_ref, gates_ref, *weight_refs):
    top, rows = ids_ref.shape
    experts = 2 * owners
    ids, gates = ids_ref[...], gates_ref[...]
    line = iota((experts, rows), 0)
    spread = jnp.zeros((experts, rows), F32)
    for k in range(top):
        spread = spread + jnp.where(ids[k : k + 1, :] == line, gates[k : k + 1, :], 0.0)
    named = row_owners(owners, per)
    found = dot(named, places(ids, experts).astype(BF16))
    shape = (owners, per, rows)
    slot = (which_slot(iota(shape, 1)) + 1).astype(F32).reshape(owners * per, rows)
    here = found == slot
    high = spread.astype(BF16)
    low = (spread - high.astype(F32)).astype(BF16)
    for at, part in enumerate((high, low)):
        full = jnp.where(here, dot(named, part), 0.0).reshape(shape)
        for ref, piece in zip(weight_refs, (full[:, :8], full[:, 8:])):
            n = piece.shape[0] * piece.shape[1]
            ref[at * rows : (at + 1) * rows, :] = piece.reshape(n, rows).astype(BF16).T


def expert_rows(x_ref, start, w_in, w_out):
    owners, per, width = x_ref.shape
    hidden = w_out.shape[1]
    full = x_ref[:, start : start + 8, :].reshape(owners * 8, width)
    rest = x_ref[:, 16:24, :].reshape(owners * 8, width)
    joint = dot(jnp.concatenate([full, rest], axis=0), w_in)
    gate, up = joint[:, :hidden], joint[:, hidden:]
    activated = (gate * jax.nn.sigmoid(gate) * up).astype(BF16)
    made = dot_t(activated, w_out)
    shape = (owners, 8, width)
    return made[: owners * 8].reshape(shape), made[owners * 8 :].reshape(shape)


def first_kernel(x_ref, w_ref, full_ref, rest_ref):
    width, both = x_ref.shape[2], w_ref.shape[2]
    wide = 2 * both // 3
    w_in = w_ref[:, :, :wide].reshape(width, wide)
    w_out = w_ref[:, :, wide:].reshape(width, both - wide)
    full, rest = expert_rows(x_ref, 0, w_in, w_out)
    full_ref[...] = full.astype(BF16)
    rest_ref[...] = rest.astype(BF16)


def second_kernel(core_ref, x_ref, in_own, in_other, out_own, out_other, rest_ref, y_ref, w_in, w_out):
    width = x_ref.shape[2]
    core = core_ref[0]
    for whole, own, other in ((w_in, in_own, in_other), (w_out, out_own, out_other)):
        whole[:, pl.ds(core, 1)] = own[...][:, None]
        whole[:, pl.ds(1 - core, 1)] = other[...][:, None]
    full, rest = expert_rows(
        x_ref, 8, w_in[...].reshape(width, w_in.shape[3]), w_out[...].reshape(width, w_out.shape[3])
    )
    y_ref[:, :8] = full.astype(BF16)
    first = iota(rest.shape, 1) < 4
    y_ref[:, 8:] = jnp.where(first, rest_ref[...].astype(F32), rest).astype(BF16)


def combine_kernel(first_weight, second_weight, first_ref, second_ref, out_ref):
    width = out_ref.shape[1]
    mixed = 0.0
    for weight, back in ((first_weight, first_ref), (second_weight, second_ref)):
        mixed = mixed + dot(weight[...], back[...].reshape(-1, width))
    rows = out_ref.shape[0]
    out_ref[...] = (mixed[:rows] + mixed[rows:]).astype(BF16)


def call(kernel, outs, args, flops, moved, smem=0, scratch=()):
    vmem = pl.BlockSpec(memory_space=pltpu.VMEM)
    scalar = pl.BlockSpec(memory_space=pltpu.SMEM)
    return pl.pallas_call(
        kernel,
        out_shape=outs,
        in_specs=[scalar] * smem + [vmem] * (len(args) - smem),
        out_specs=jax.tree.map(lambda _: vmem, outs),
        scratch_shapes=list(scratch),
        cost_estimate=pl.CostEstimate(flops=flops, bytes_accessed=moved, transcendentals=0),
    )(*args)


def swapped(x):
    return lax.ppermute(x, "c", [(0, 1), (1, 0)])


def exchanged(x):
    return lax.all_to_all(x, "expert", split_axis=0, concat_axis=0, tiled=True)


def shards(tokens, expert_ids, gates, w_in, w_out):
    rows, width = tokens.shape
    owners = lax.axis_size("expert")
    chips = lax.axis_size("z")
    hidden = w_out.shape[1]
    slots = owners * ROWS
    ids = expert_ids.T
    w_out = jnp.swapaxes(w_out, 1, 2)

    def bf16(*shape):
        return jax.ShapeDtypeStruct(shape, BF16)

    first_own = jnp.concatenate([w_in[0], w_out[0]], axis=1)
    first_whole = lax.all_gather(first_own, DP, axis=0)
    outgoing = call(
        pack_kernel,
        bf16(owners, ROWS, width),
        (ids, tokens),
        2 * slots * rows * width,
        2 * slots * width,
    )
    arrived = exchanged(outgoing)
    in_own = lax.all_gather(w_in[1], "z", axis=0)
    in_other = swapped(in_own)
    out_own = lax.all_gather(w_out[1], "z", axis=0)
    out_other = swapped(out_own)
    weights = call(
        functools.partial(gate_kernel, owners, ROWS),
        (bf16(2 * rows, owners * 8), bf16(2 * rows, owners * 16)),
        (ids, gates.T),
        2 * slots * rows * 256,
        4 * slots * rows,
    )
    arrived, in_own, out_own, weights = lax.optimization_barrier(
        (arrived, in_own, out_own, tuple(weights))
    )
    work = 2 * 512 * 3 * hidden * width
    first, rest = call(
        first_kernel,
        (bf16(owners, 8, width), bf16(owners, 8, width)),
        (arrived, first_whole),
        work,
        4 * slots * width + 6 * hidden * width,
    )
    first_back = exchanged(first)
    core = lax.axis_index("c").astype(jnp.int32).reshape(1)
    second = call(
        second_kernel,
        bf16(owners, 16, width),
        (core, arrived, in_own, in_other, out_own, out_other, rest),
        work,
        4 * slots * width + 6 * hidden * width,
        smem=1,
        scratch=[
            pltpu.VMEM((chips, 2, BLOCK, 2 * hidden), BF16),
            pltpu.VMEM((chips, 2, BLOCK, hidden), BF16),
        ],
    )
    second_back = exchanged(second)
    return call(
        combine_kernel,
        bf16(rows, width),
        (*weights, first_back, second_back),
        4 * slots * rows * width,
        2 * slots * width,
    )


def solution(mesh):
    dp = mesh.shape["dp"]
    finer = Mesh(mesh.devices.reshape(dp // 2, 2, mesh.shape["expert"]), ALL)
    in_specs = (P(ALL, None), P(ALL, None), P(ALL, None), P("expert", DP, None), P("expert", None, DP))
    return jax.shard_map(
        shards, mesh=finer, in_specs=in_specs, out_specs=P(ALL, None), check_vma=False
    )
```

time: 162 us -> 178 us (1.099)
  the two profiles are of different devices: /device:TPU:8 before, /device:TPU:4 now
where the time goes in v4:
time: 178 us; the launch traced here: 177 us
  blocking collectives  109 us (61%)
  starting transfers between devices  30.8 us (17%)
  Pallas kernels  17.8 us (10%)
  between operations  13.5 us (8%)
  local copies, waits for them, and re-layouts  3.82 us (2%)
  waiting for transfers between devices  1.86 us (1%)
    all_gather x1, blocking collectives, shards(): out_own = lax.all_gather(w_out[1], 'z', axis=0)  38.6 us
    all_to_all x1, blocking collectives, exchanged(): return lax.all_to_all(x, 'expert', split_axis=0, concat_axis=0, tiled=True)  38 us
    all_gather x1, blocking collectives, shards(): in_own = lax.all_gather(w_in[1], 'z', axis=0)  32 us
    all_to_all x2, starting transfers between devices, exchanged(): return lax.all_to_all(x, 'expert', split_axis=0, concat_axis=0, tiled=True)  26.4 us
    pallas_call x5, Pallas kernels, call(): pl.pallas_call(kernel, out_shape=outs, in_specs=[scalar] * smem + [vmem]...  17.8 us
    ppermute x2, starting transfers between devices, swapped(): return lax.ppermute(x, 'c', [(0, 1), (1, 0)])  4.33 us
  transfers between devices with their start and end apart: 5, of which 2 were waited for; matrix products, arithmetic and copies ran while one was open for 0% of the time, Pallas kernels for 6%

profile of v4, /device:TPU:4, one launch (start us, length us, event | category | flops | bytes accessed | tf_op | source)
XLA Modules:
  0.0 177.0 jit_solution(13316522675947924109)
XLA Ops:
  6.5 0.0 all-gather.3.cloned.1.call-start
  6.5 0.8 slice_bitcast_fusion
  7.4 0.8 slice_bitcast_fusion.1
  8.1 0.6 pad_maximum_fusion
  8.8 0.0 all-gather.3.cloned.1.call-update
  8.8 2.9 %shard_map.55 = bf16[32,24,1024]{2,1,0:T(8,128)(2,1)} custom-call(s32[8,64]{1,0:T(8,128)} %bitcast.10, bf16[64,1024]{1,0:T(8,128)(2,1)} %tok_ref.1), custom_call_target="tpu_custom_call" | custom-call | flops 100663296 | bytes 1572864 | tf_op jit(solution)/shard_map/pallas_call | solution.py:139
  11.7 16.8 %all-to-all-start = ((bf16[32,24,1024]{2,1,0:T(8,128)(2,1)}), bf16[32,24,1024]{2,1,0:T(8,128)(2,1)S(1)}, u32[]{:S(2)}, u32[]{:S(2)}) async-start(bf16[32,24,1024]{2,1,0:T(8,128)(2,1)} %shard_map.55), calls=%async_computation | async-start | bytes 3145728 | tf_op jit(solution)/shard_map/all_to_all | solution.py:154
  28.5 1.9 %shard_map.56 = (bf16[128,256]{1,0:T(8,128)(2,1)}, bf16[128,512]{1,0:T(8,128)(2,1)}) custom-call(s32[8,64]{1,0:T(8,128)} %bitcast.11, f32[8,64]{1,0:T(8,128)} %bitcast.13), custom_call_target="tpu_custom_call" | custom-call | flops 25165824 | bytes 196608 | tf_op jit(solution)/shard_map/pallas_call | solution.py:139
  30.4 38.6 %all_gather.13.out_own = bf16[16,32,384]{2,1,0:T(8,128)(2,1)S(1)} all-gather(bf16[1,32,384]{2,1,0:T(8,128)(2,1)S(1)} %get-tuple-element.26), channel_id=1, replica_groups=mesh['z'=16,'c'=2,'expert'=32] {'z'}, dimensions={0}, use_global_device_ids=true | all-gather | bytes 417792 | tf_op jit(solution)/shard_map/all_gather | solution.py:181
  69.0 0.0 copy-start.3
  69.0 32.0 %all_gather.12.in_own = bf16[16,32,768]{2,1,0:T(8,128)(2,1)S(1)} all-gather(bf16[1,32,768]{2,1,0:T(8,128)(2,1)S(1)} %get-tuple-element.24), channel_id=1, replica_groups=mesh['z'=16,'c'=2,'expert'=32] {'z'}, dimensions={0}, use_global_device_ids=true | all-gather | bytes 835584 | tf_op jit(solution)/shard_map/all_gather | solution.py:179
  101.0 0.0 copy-start.1
  101.0 0.0 all-to-all-done.x_ref
  101.0 0.0 copy-start
  101.0 0.0 all-gather.3.cloned.1.call-done
  101.0 1.2 copy-done
  102.2 5.1 %shard_map.57 = (bf16[32,8,1024]{2,1,0:T(8,128)(2,1)}, bf16[32,8,1024]{2,1,0:T(8,128)(2,1)}) custom-call(bf16[32,24,1024]{2,1,0:T(8,128)(2,1)} %copy-done, bf16[32,32,1152]{2,1,0:T(8,128)(2,1)} %bitcast.12), custom_call_target="tpu_custom_call" | custom-call | flops 1207959552 | bytes 5505024 | tf_op jit(solution)/shard_map/pallas_call | solution.py:139
  107.3 9.7 %all-to-all-start.1 = ((bf16[32,8,1024]{2,1,0:T(8,128)(2,1)}), bf16[32,8,1024]{2,1,0:T(8,128)(2,1)S(1)}, u32[]{:S(2)}, u32[]{:S(2)}) async-start(bf16[32,8,1024]{2,1,0:T(8,128)(2,1)} %get-tuple-element.19), calls=%async_computation.1 | async-start | bytes 1048576 | tf_op jit(solution)/shard_map/all_to_all | solution.py:154
  117.0 1.9 %collective-permute-start = (bf16[16,32,768]{2,1,0:T(8,128)(2,1)S(1)}, bf16[16,32,768]{2,1,0:T(8,128)(2,1)S(1)}, u32[]{:S(2)}, u32[]{:S(2)}) collective-permute-start(bf16[16,32,768]{2,1,0:T(8,128)(2,1)S(1)} %all_gather.12.in_own), channel_id=1, source_target_pairs={{0,32},{32,0},{1,33},{33,1},{2,34},{34,2},{3,35},{35,3},{4,36},{36... | collective-permute-start | bytes 2359304 | tf_op jit(solution)/shard_map/ppermute | solution.py:150
  118.9 0.0 copy-done.3
  118.9 2.4 %collective-permute-start.1 = (bf16[16,32,384]{2,1,0:T(8,128)(2,1)S(1)}, bf16[16,32,384]{2,1,0:T(8,128)(2,1)S(1)}, u32[]{:S(2)}, u32[]{:S(2)}) collective-permute-start(bf16[16,32,384]{2,1,0:T(8,128)(2,1)S(1)} %all_gather.13.out_own), channel_id=1, source_target_pairs={{0,32},{32,0},{1,33},{33,1},{2,34},{34,2},{3,35},{35,3},{4,36},{36... | collective-permute-start | bytes 1179656 | tf_op jit(solution)/shard_map/ppermute | solution.py:150
  121.3 1.3 collective-permute-done.1.out_other
  122.7 0.0 copy-start.5
  122.7 0.0 collective-permute-done.in_other
  122.7 0.0 copy-start.4
  122.7 0.0 copy-done.1
  122.7 0.7 copy-done.5
  123.4 0.3 copy-done.4
  123.7 5.4 %shard_map.58 = bf16[32,16,1024]{2,1,0:T(8,128)(2,1)} custom-call(s32[1]{0:T(128)} %bitcast.6.core_ref, bf16[32,24,1024]{2,1,0:T(8,128)(2,1)} %copy-done, bf16[16,32,768]{2,1,0:T(8,128)(2,1)} %copy-done.1, bf16[16,32,768]{2,1,0:T(8,128)(2,1)} %copy-done.4, bf16[16,32,384]{2,1,0:T(8,128)(2,1)} %copy-done.3, bf16[16,32,384]{2,1,0:T(8,128)(2,1)} %copy-done.5, ...), custom_call_target="tpu_custom_call" | custom-call | flops 1207959552 | bytes 5505024 | tf_op jit(solution)/shard_map/pallas_call | solution.py:139
  129.1 0.5 all-to-all-done.1.first_ref
  129.6 0.0 copy-start.2
  129.6 38.0 %all_to_all.15.second_ref = bf16[32,16,1024]{2,1,0:T(8,128)(2,1)} all-to-all(bf16[32,16,1024]{2,1,0:T(8,128)(2,1)} %shard_map.58), channel_id=1, replica_groups=mesh['z'=16,'c'=2,'expert'=32] {'expert'}, dimensions={0} | all-to-all | bytes 2097152 | tf_op jit(solution)/shard_map/all_to_all | solution.py:154
  167.6 0.0 copy-done.2
  167.6 2.5 %shard_map.59 = bf16[64,1024]{1,0:T(8,128)(2,1)} custom-call(bf16[128,256]{1,0:T(8,128)(2,1)} %get-tuple-element.16.first_weight, bf16[128,512]{1,0:T(8,128)(2,1)} %get-tuple-element.17.second_weight, bf16[32,8,1024]{2,1,0:T(8,128)(2,1)} %copy-done.2, bf16[32,16,1024]{2,1,0:T(8,128)(2,1)} %all_to_all.15.second_ref), custom_call_target="tpu_custom_call" | custom-call | flops 201326592 | bytes 1572864 | tf_op jit(solution)/shard_map/pallas_call | solution.py:139
Async XLA Ops:
  6.5 94.5 %all-gather.3.cloned.1.call-start = ((), (), s32[]{:S(2)}) async-start(), calls=%async_computation.3 | async-start | bytes 2433024 | tf_op jit(solution)/shard_map/all_gather | solution.py:170
  11.7 89.3 %all-to-all-start = ((bf16[32,24,1024]{2,1,0:T(8,128)(2,1)}), bf16[32,24,1024]{2,1,0:T(8,128)(2,1)S(1)}, u32[]{:S(2)}, u32[]{:S(2)}) async-start(bf16[32,24,1024]{2,1,0:T(8,128)(2,1)} %shard_map.55), calls=%async_computation | async-start | bytes 3145728 | tf_op jit(solution)/shard_map/all_to_all | solution.py:154
  69.0 49.9 %copy-start.3 = (bf16[16,32,384]{2,1,0:T(8,128)(2,1)}, bf16[16,32,384]{2,1,0:T(8,128)(2,1)S(1)}, u32[]{:S(2)}) copy-start(bf16[16,32,384]{2,1,0:T(8,128)(2,1)S(1)} %all_gather.13.out_own) | copy-start | bytes 1179652
  101.0 21.7 %copy-start.1 = (bf16[16,32,768]{2,1,0:T(8,128)(2,1)}, bf16[16,32,768]{2,1,0:T(8,128)(2,1)S(1)}, u32[]{:S(2)}) copy-start(bf16[16,32,768]{2,1,0:T(8,128)(2,1)S(1)} %all_gather.12.in_own) | copy-start | bytes 2359300
  101.0 1.2 copy-start
  107.3 22.3 %all-to-all-start.1 = ((bf16[32,8,1024]{2,1,0:T(8,128)(2,1)}), bf16[32,8,1024]{2,1,0:T(8,128)(2,1)S(1)}, u32[]{:S(2)}, u32[]{:S(2)}) async-start(bf16[32,8,1024]{2,1,0:T(8,128)(2,1)} %get-tuple-element.19), calls=%async_computation.1 | async-start | bytes 1048576 | tf_op jit(solution)/shard_map/all_to_all | solution.py:154
  117.0 5.7 %collective-permute-start = (bf16[16,32,768]{2,1,0:T(8,128)(2,1)S(1)}, bf16[16,32,768]{2,1,0:T(8,128)(2,1)S(1)}, u32[]{:S(2)}, u32[]{:S(2)}) collective-permute-start(bf16[16,32,768]{2,1,0:T(8,128)(2,1)S(1)} %all_gather.12.in_own), channel_id=1, source_target_pairs={{0,32},{32,0},{1,33},{33,1},{2,34},{34,2},{3,35},{35,3},{4,36},{36... | collective-permute-start | bytes 2359304 | tf_op jit(solution)/shard_map/ppermute | solution.py:150
  118.9 3.7 %collective-permute-start.1 = (bf16[16,32,384]{2,1,0:T(8,128)(2,1)S(1)}, bf16[16,32,384]{2,1,0:T(8,128)(2,1)S(1)}, u32[]{:S(2)}, u32[]{:S(2)}) collective-permute-start(bf16[16,32,384]{2,1,0:T(8,128)(2,1)S(1)} %all_gather.13.out_own), channel_id=1, source_target_pairs={{0,32},{32,0},{1,33},{33,1},{2,34},{34,2},{3,35},{35,3},{4,36},{36... | collective-permute-start | bytes 1179656 | tf_op jit(solution)/shard_map/ppermute | solution.py:150
  122.7 0.7 copy-start.5
  122.7 1.1 copy-start.4
  129.6 38.0 %copy-start.2 = (bf16[32,8,1024]{2,1,0:T(8,128)(2,1)}, bf16[32,8,1024]{2,1,0:T(8,128)(2,1)S(1)}, u32[]{:S(2)}) copy-start(bf16[32,8,1024]{2,1,0:T(8,128)(2,1)S(1)} %all-to-all-done.1.first_ref) | copy-start | bytes 1572868
Sparse Core Ops, SparseCore 0:
  10.0 83.9 all-gather.2

commit v5 on v4

v5 whole, which is shorter than its diff:
```python
import functools

import jax
import jax.numpy as jnp
from jax import lax
from jax.experimental import pallas as pl
from jax.experimental.pallas import tpu as pltpu
from jax.sharding import Mesh
from jax.sharding import PartitionSpec as P


BF16 = jnp.bfloat16
F32 = jnp.float32
DP = ("z", "c")
ALL = ("z", "c", "expert")
ROWS = 24
BLOCK = 32


def iota(shape, dim):
    return lax.broadcasted_iota(jnp.int32, shape, dim)


def which_expert(q):
    return jnp.where((q >= 20) | ((q >= 8) & (q < 16)), 1, 0)


def which_slot(q):
    return jnp.where(q < 8, q, jnp.where(q < 20, q - 8, q - 12))


def dot(a, b):
    return jnp.dot(a, b, preferred_element_type=F32)


def dot_t(a, b):
    return lax.dot_general(a, b, (((1,), (1,)), ((), ())), preferred_element_type=F32)


def places(ids, experts):
    top, rows = ids.shape
    line = iota((experts, rows), 0)
    routed = jnp.zeros((experts, rows), F32)
    for k in range(top):
        routed = routed + (ids[k : k + 1, :] == line).astype(F32)
    earlier = (iota((rows, rows), 0) < iota((rows, rows), 1)).astype(F32).astype(BF16)
    before = dot(routed.astype(BF16), earlier)
    return jnp.where(routed > 0, before + 1.0, 0.0)


def row_owners(owners, per):
    shape = (owners, per, 2 * owners)
    named = 2 * iota(shape, 0) + which_expert(iota(shape, 1)) == iota(shape, 2)
    return named.astype(F32).astype(BF16).reshape(owners * per, 2 * owners)


def pack_kernel(ids_ref, tok_ref, out_ref):
    owners, per, width = out_ref.shape
    rows = ids_ref.shape[1]
    place = places(ids_ref[...], 2 * owners)
    found = dot(row_owners(owners, per), place.astype(BF16))
    shape = (owners, per, rows)
    slot = (which_slot(iota(shape, 1)) + 1).astype(F32).reshape(owners * per, rows)
    pick = (found == slot).astype(F32).astype(BF16)
    placed = dot(pick, tok_ref[...]).astype(BF16)
    out_ref[...] = placed.reshape(owners, per, width)


def gate_kernel(owners, per, ids_ref, gates_ref, weight_ref):
    top, rows = ids_ref.shape
    experts = 2 * owners
    ids, gates = ids_ref[...], gates_ref[...]
    line = iota((experts, rows), 0)
    spread = jnp.zeros((experts, rows), F32)
    for k in range(top):
        spread = spread + jnp.where(ids[k : k + 1, :] == line, gates[k : k + 1, :], 0.0)
    named = row_owners(owners, per)
    found = dot(named, places(ids, experts).astype(BF16))
    shape = (owners, per, rows)
    slot = (which_slot(iota(shape, 1)) + 1).astype(F32).reshape(owners * per, rows)
    here = found == slot
    high = spread.astype(BF16)
    low = (spread - high.astype(F32)).astype(BF16)
    for at, part in enumerate((high, low)):
        weight = jnp.where(here, dot(named, part), 0.0).astype(BF16)
        weight_ref[at * rows : (at + 1) * rows, :] = weight.T


def expert_rows(x_ref, start, w_in, w_out):
    owners, _, width = x_ref.shape
    hidden = w_out.shape[1]
    full = x_ref[:, start : start + 8, :].reshape(owners * 8, width)
    rest = x_ref[:, 16:24, :].reshape(owners * 8, width)
    joint = dot(jnp.concatenate([full, rest], axis=0), w_in)
    gate, up = joint[:, :hidden], joint[:, hidden:]
    activated = (gate * jax.nn.sigmoid(gate) * up).astype(BF16)
    made = dot_t(activated, w_out)
    shape = (owners, 8, width)
    return made[: owners * 8].reshape(shape), made[owners * 8 :].reshape(shape)


def expert_kernel(place_ref, x_ref, *refs):
    *blocks, y_ref, whole, sems = refs
    chips = whole.shape[0]
    width, both = x_ref.shape[2], whole.shape[4]
    z, core = place_ref[0], place_ref[1]
    copies = []

    def put(block, chip, lane):
        copies.append(pltpu.make_async_copy(block, whole.at[chip, lane], sems.at[len(copies)]))

    count = chips // 2
    for k, block in enumerate(blocks):
        distance = k if k <= count else k - count
        lane = core if k <= count else 1 - core
        chip = lax.rem(z + (2 * lane - 1) * distance + chips, chips)
        if len(block.shape) == 3:
            put(block, chip, lane)
        else:
            put(block.at[0], chip, lane)
            put(block.at[1], chip, 1 - lane)
    for copy in copies:
        copy.start()
    for copy in copies:
        copy.wait()
    wide = 2 * both // 3
    made = []
    for e in range(2):
        w_in = whole[:, :, e, :, :wide].reshape(width, wide)
        w_out = whole[:, :, e, :, wide:].reshape(width, both - wide)
        full, rest = expert_rows(x_ref, 8 * e, w_in, w_out)
        y_ref[:, 8 * e : 8 * e + 8] = full.astype(BF16)
        made.append(rest)
    first = iota(made[0].shape, 1) < 4
    y_ref[:, 16:24] = jnp.where(first, made[0], made[1]).astype(BF16)


def combine_kernel(weight_ref, back_ref, out_ref):
    rows, width = out_ref.shape
    mixed = dot(weight_ref[...], back_ref[...].reshape(-1, width))
    out_ref[...] = (mixed[:rows] + mixed[rows:]).astype(BF16)


VMEM = pl.BlockSpec(memory_space=pltpu.VMEM)


def call(kernel, outs, args, flops, moved, specs=None, scratch=()):
    return pl.pallas_call(
        kernel,
        out_shape=outs,
        in_specs=[VMEM] * len(args) if specs is None else specs,
        out_specs=VMEM,
        scratch_shapes=list(scratch),
        cost_estimate=pl.CostEstimate(flops=flops, bytes_accessed=moved, transcendentals=0),
    )(*args)


def swapped(x):
    return lax.ppermute(x, "c", [(0, 1), (1, 0)])


def exchanged(x):
    return lax.all_to_all(x, "expert", split_axis=0, concat_axis=0, tiled=True)


def along(x, by):
    n = lax.axis_size("z")
    pairs = [(2 * i + c, 2 * ((i + (1 - 2 * c) * by) % n) + c) for i in range(n) for c in range(2)]
    return lax.ppermute(x, ("z", "c"), pairs)


def all_blocks(own):
    count = lax.axis_size("z") // 2
    block = jnp.stack([own, swapped(own)])
    held = [block] + [None] * count
    far = block
    for step in range(1, count // 2 + 1):
        coming = along(far if 2 * step < count else far[0], 2)
        held[2 * step - 1] = along(far, 1)
        held[2 * step] = far = coming
    return held + [swapped(held[d]) for d in range(1, count + 1)]


def shards(tokens, expert_ids, gates, w_in, w_out):
    rows, width = tokens.shape
    owners = lax.axis_size("expert")
    chips = lax.axis_size("z")
    hidden = w_out.shape[1]
    slots = owners * ROWS
    ids = expert_ids.T

    def bf16(*shape):
        return jax.ShapeDtypeStruct(shape, BF16)

    blocks = all_blocks(jnp.concatenate([w_in, jnp.swapaxes(w_out, 1, 2)], axis=2))
    outgoing = call(
        pack_kernel,
        bf16(owners, ROWS, width),
        (ids, tokens),
        2 * slots * rows * width,
        2 * slots * width,
    )
    arrived = exchanged(outgoing)
    weight = call(
        functools.partial(gate_kernel, owners, ROWS),
        bf16(2 * rows, slots),
        (ids, gates.T),
        2 * slots * rows * 256,
        4 * slots * rows,
    )
    place = jnp.stack([lax.axis_index("z"), lax.axis_index("c")]).astype(jnp.int32)
    produced = call(
        expert_kernel,
        bf16(owners, ROWS, width),
        (place, arrived, *blocks),
        2 * 1024 * 3 * hidden * width,
        4 * slots * width + 12 * hidden * width,
        specs=[pl.BlockSpec(memory_space=pltpu.SMEM), VMEM]
        + [pl.BlockSpec(memory_space=pl.ANY)] * len(blocks),
        scratch=[
            pltpu.VMEM((chips, 2, 2, BLOCK, 3 * hidden), BF16),
            pltpu.SemaphoreType.DMA((2 * chips,)),
        ],
    )
    produced, weight = lax.optimization_barrier((produced, weight))
    back = exchanged(produced)
    return call(
        combine_kernel,
        bf16(rows, width),
        (weight, back),
        4 * slots * rows * width,
        2 * slots * width,
    )


def solution(mesh):
    dp = mesh.shape["dp"]
    finer = Mesh(mesh.devices.reshape(dp // 2, 2, mesh.shape["expert"]), ALL)
    in_specs = (P(ALL, None), P(ALL, None), P(ALL, None), P("expert", DP, None), P("expert", None, DP))
    return jax.shard_map(
        shards, mesh=finer, in_specs=in_specs, out_specs=P(ALL, None), check_vma=False
    )
```

time: 178 us -> 154 us (0.87)
  the two profiles are of different devices: /device:TPU:4 before, /device:TPU:1 now
where the time goes in v5:
time: 154 us; the launch traced here: 153 us
  starting transfers between devices  75.4 us (49%)
  blocking collectives  49.4 us (32%)
  Pallas kernels  16.1 us (10%)
  waiting for transfers between devices  9.84 us (6%)
    all_to_all x1, blocking collectives, exchanged(): return lax.all_to_all(x, 'expert', split_axis=0, concat_axis=0, tiled=True)  49.4 us
    ppermute x8, starting transfers between devices, along(): return lax.ppermute(x, ('z', 'c'), pairs)  37.8 us
    ppermute x9, starting transfers between devices, swapped(): return lax.ppermute(x, 'c', [(0, 1), (1, 0)])  27 us
    pallas_call x4, Pallas kernels, call(): pl.pallas_call(kernel, out_shape=outs, in_specs=[VMEM] * len(args) if spe...  16.1 us
    all_to_all x1, starting transfers between devices, exchanged(): return lax.all_to_all(x, 'expert', split_axis=0, concat_axis=0, tiled=True)  10.6 us
    ppermute x8, waiting for transfers between devices, along(): return lax.ppermute(x, ('z', 'c'), pairs)  8.83 us
  transfers between devices with their start and end apart: 18, of which 3 were waited for; matrix products, arithmetic and copies ran while one was open for 0% of the time, Pallas kernels for 1%

profile of v5, /device:TPU:1, one launch (start us, length us, event | category | flops | bytes accessed | tf_op | source)
XLA Modules:
  0.0 153.2 jit_solution(10452840577753249251)
XLA Ops:
  0.0 2.9 %shard_map.55 = bf16[32,24,1024]{2,1,0:T(8,128)(2,1)} custom-call(s32[8,64]{1,0:T(8,128)} %bitcast.12, bf16[64,1024]{1,0:T(8,128)(2,1)} %tok_ref.1), custom_call_target="tpu_custom_call" | custom-call | flops 100663296 | bytes 1572864 | tf_op jit(solution)/shard_map/pallas_call | solution.py:148
  2.9 10.6 %all-to-all-start = ((bf16[32,24,1024]{2,1,0:T(8,128)(2,1)}), bf16[32,24,1024]{2,1,0:T(8,128)(2,1)S(1)}, u32[]{:S(2)}, u32[]{:S(2)}) async-start(bf16[32,24,1024]{2,1,0:T(8,128)(2,1)} %shard_map.55), calls=%async_computation | async-start | bytes 3145728 | tf_op jit(solution)/shard_map/all_to_all | solution.py:163
  13.6 0.0 copy-done.2
  13.6 0.0 copy-done.4
  13.6 9.5 %collective-permute-start = (bf16[2,32,1152]{2,1,0:T(8,128)(2,1)S(1)}, bf16[2,32,1152]{2,1,0:T(8,128)(2,1)S(1)}, u32[]{:S(2)}, u32[]{:S(2)}) collective-permute-start(bf16[2,32,1152]{2,1,0:T(8,128)(2,1)S(1)} %get-tuple-element.10), channel_id=1, source_target_pairs={{0,32},{32,0},{1,33},{33,1},{2,34},{34,2},{3,35},{35,3},{4,36},{36... | collective-permute-start | bytes 442376 | tf_op jit(solution)/shard_map/ppermute | solution.py:159
  23.1 1.0 collective-permute-done
  24.2 0.0 copy-start.1
  24.2 11.3 %collective-permute-start.2 = (bf16[2,2,32,1152]{3,2,1,0:T(8,128)(2,1)S(1)}, bf16[2,2,32,1152]{3,2,1,0:T(8,128)(2,1)S(1)}, u32[]{:S(2)}, u32[]{:S(2)}) collective-permute-start(bf16[2,2,32,1152]{3,2,1,0:T(8,128)(2,1)S(1)} %pad_maximum_fusion.refs_0_), channel_id=1, source_target_pairs={{0,128},{32,928},{64,192},{96,992},{128,256},{160,32},{192,320},{2... | collective-permute-start | bytes 884744 | tf_op jit(solution)/shard_map/ppermute | solution.py:169
  35.5 6.8 %collective-permute-done.2.refs_2_ = bf16[2,2,32,1152]{3,2,1,0:T(8,128)(2,1)S(1)} collective-permute-done((bf16[2,2,32,1152]{3,2,1,0:T(8,128)(2,1)S(1)}, bf16[2,2,32,1152]{3,2,1,0:T(8,128)(2,1)S(1)}, u32[]{:S(2)}, u32[]{:S(2)}) %collective-permute-start.2) | collective-permute-done | bytes 294944 | tf_op jit(solution)/shard_map/ppermute | solution.py:169
  42.3 6.2 %collective-permute-start.4 = (bf16[2,2,32,1152]{3,2,1,0:T(8,128)(2,1)S(1)}, bf16[2,2,32,1152]{3,2,1,0:T(8,128)(2,1)S(1)}, u32[]{:S(2)}, u32[]{:S(2)}) collective-permute-start(bf16[2,2,32,1152]{3,2,1,0:T(8,128)(2,1)S(1)} %collective-permute-done.2.refs_2_), channel_id=1, source_target_pairs={{0,128},{32,928},{64,192},{96,992},{128,256},{160,32},{192,320},{2... | collective-permute-start | bytes 884744 | tf_op jit(solution)/shard_map/ppermute | solution.py:169
  48.5 1.9 %collective-permute-start.1 = (bf16[2,2,32,1152]{3,2,1,0:T(8,128)(2,1)S(1)}, bf16[2,2,32,1152]{3,2,1,0:T(8,128)(2,1)S(1)}, u32[]{:S(2)}, u32[]{:S(2)}) collective-permute-start(bf16[2,2,32,1152]{3,2,1,0:T(8,128)(2,1)S(1)} %pad_maximum_fusion.refs_0_), channel_id=1, source_target_pairs={{0,64},{32,992},{64,128},{96,32},{128,192},{160,96},{192,256},{224... | collective-permute-start | bytes 884744 | tf_op jit(solution)/shard_map/ppermute | solution.py:169
  50.4 2.2 %collective-permute-start.3 = (bf16[2,2,32,1152]{3,2,1,0:T(8,128)(2,1)S(1)}, bf16[2,2,32,1152]{3,2,1,0:T(8,128)(2,1)S(1)}, u32[]{:S(2)}, u32[]{:S(2)}) collective-permute-start(bf16[2,2,32,1152]{3,2,1,0:T(8,128)(2,1)S(1)} %collective-permute-done.2.refs_2_), channel_id=1, source_target_pairs={{0,64},{32,992},{64,128},{96,32},{128,192},{160,96},{192,256},{224... | collective-permute-start | bytes 884744 | tf_op jit(solution)/shard_map/ppermute | solution.py:169
  52.6 2.0 %collective-permute-done.4.refs_4_ = bf16[2,2,32,1152]{3,2,1,0:T(8,128)(2,1)S(1)} collective-permute-done((bf16[2,2,32,1152]{3,2,1,0:T(8,128)(2,1)S(1)}, bf16[2,2,32,1152]{3,2,1,0:T(8,128)(2,1)S(1)}, u32[]{:S(2)}, u32[]{:S(2)}) %collective-permute-start.4) | collective-permute-done | bytes 294944 | tf_op jit(solution)/shard_map/ppermute | solution.py:169
  54.6 6.1 %collective-permute-start.6 = (bf16[2,2,32,1152]{3,2,1,0:T(8,128)(2,1)S(1)}, bf16[2,2,32,1152]{3,2,1,0:T(8,128)(2,1)S(1)}, u32[]{:S(2)}, u32[]{:S(2)}) collective-permute-start(bf16[2,2,32,1152]{3,2,1,0:T(8,128)(2,1)S(1)} %collective-permute-done.4.refs_4_), channel_id=1, source_target_pairs={{0,128},{32,928},{64,192},{96,992},{128,256},{160,32},{192,320},{2... | collective-permute-start | bytes 884744 | tf_op jit(solution)/shard_map/ppermute | solution.py:169
  60.7 1.9 %collective-permute-start.10 = (bf16[2,2,32,1152]{3,2,1,0:T(8,128)(2,1)S(1)}, bf16[2,2,32,1152]{3,2,1,0:T(8,128)(2,1)S(1)}, u32[]{:S(2)}, u32[]{:S(2)}) collective-permute-start(bf16[2,2,32,1152]{3,2,1,0:T(8,128)(2,1)S(1)} %collective-permute-done.2.refs_2_), channel_id=1, source_target_pairs={{0,32},{32,0},{1,33},{33,1},{2,34},{34,2},{3,35},{35,3},{4,36},{36... | collective-permute-start | bytes 884744 | tf_op jit(solution)/shard_map/ppermute | solution.py:159
  62.6 0.0 collective-permute-done.1.refs_1_
  62.6 0.0 copy-start.7
  62.6 2.4 %collective-permute-start.9 = (bf16[2,2,32,1152]{3,2,1,0:T(8,128)(2,1)S(1)}, bf16[2,2,32,1152]{3,2,1,0:T(8,128)(2,1)S(1)}, u32[]{:S(2)}, u32[]{:S(2)}) collective-permute-start(bf16[2,2,32,1152]{3,2,1,0:T(8,128)(2,1)S(1)} %collective-permute-done.1.refs_1_), channel_id=1, source_target_pairs={{0,32},{32,0},{1,33},{33,1},{2,34},{34,2},{3,35},{35,3},{4,36},{36... | collective-permute-start | bytes 884744 | tf_op jit(solution)/shard_map/ppermute | solution.py:159
  65.1 2.5 %collective-permute-start.5 = (bf16[2,2,32,1152]{3,2,1,0:T(8,128)(2,1)S(1)}, bf16[2,2,32,1152]{3,2,1,0:T(8,128)(2,1)}, u32[]{:S(2)}, u32[]{:S(2)}) collective-permute-start(bf16[2,2,32,1152]{3,2,1,0:T(8,128)(2,1)S(1)} %collective-permute-done.4.refs_4_), channel_id=1, source_target_pairs={{0,64},{32,992},{64,128},{96,32},{128,192},{160,96},{192,256},{224... | collective-permute-start | bytes 884744 | tf_op jit(solution)/shard_map/ppermute | solution.py:169
  67.6 0.0 collective-permute-done.3.refs_3_
  67.6 0.0 copy-start.8
  67.6 1.9 %collective-permute-start.11 = (bf16[2,2,32,1152]{3,2,1,0:T(8,128)(2,1)S(1)}, bf16[2,2,32,1152]{3,2,1,0:T(8,128)(2,1)S(1)}, u32[]{:S(2)}, u32[]{:S(2)}) collective-permute-start(bf16[2,2,32,1152]{3,2,1,0:T(8,128)(2,1)S(1)} %collective-permute-done.3.refs_3_), channel_id=1, source_target_pairs={{0,32},{32,0},{1,33},{33,1},{2,34},{34,2},{3,35},{35,3},{4,36},{36... | collective-permute-start | bytes 884744 | tf_op jit(solution)/shard_map/ppermute | solution.py:159
  69.5 0.0 collective-permute-done.6.refs_6_
  69.6 4.2 %collective-permute-start.7 = (bf16[2,2,32,1152]{3,2,1,0:T(8,128)(2,1)S(1)}, bf16[2,2,32,1152]{3,2,1,0:T(8,128)(2,1)}, u32[]{:S(2)}, u32[]{:S(2)}) collective-permute-start(bf16[2,2,32,1152]{3,2,1,0:T(8,128)(2,1)S(1)} %collective-permute-done.6.refs_6_), channel_id=1, source_target_pairs={{0,64},{32,992},{64,128},{96,32},{128,192},{160,96},{192,256},{224... | collective-permute-start | bytes 884744 | tf_op jit(solution)/shard_map/ppermute | solution.py:169
  73.8 0.0 collective-permute-done.9.refs_9_
  73.9 1.9 %collective-permute-start.12 = (bf16[2,2,32,1152]{3,2,1,0:T(8,128)(2,1)S(1)}, bf16[2,2,32,1152]{3,2,1,0:T(8,128)(2,1)}, u32[]{:S(2)}, u32[]{:S(2)}) collective-permute-start(bf16[2,2,32,1152]{3,2,1,0:T(8,128)(2,1)S(1)} %collective-permute-done.4.refs_4_), channel_id=1, source_target_pairs={{0,32},{32,0},{1,33},{33,1},{2,34},{34,2},{3,35},{35,3},{4,36},{36... | collective-permute-start | bytes 884744 | tf_op jit(solution)/shard_map/ppermute | solution.py:159
  75.8 0.0 collective-permute-done.10.refs_10_
  75.8 3.4 %collective-permute-start.8 = (bf16[2,32,1152]{2,1,0:T(8,128)(2,1)S(1)}, bf16[2,32,1152]{2,1,0:T(8,128)(2,1)S(1)}, u32[]{:S(2)}, u32[]{:S(2)}) collective-permute-start(bf16[2,32,1152]{2,1,0:T(8,128)(2,1)S(1)} %slice_bitcast_fusion), channel_id=1, source_target_pairs={{0,128},{32,928},{64,192},{96,992},{128,256},{160,32},{192,320},{2... | collective-permute-start | bytes 442376 | tf_op jit(solution)/shard_map/ppermute | solution.py:169
  79.2 0.0 collective-permute-done.5.refs_5_
  79.2 1.9 %collective-permute-start.14 = (bf16[2,2,32,1152]{3,2,1,0:T(8,128)(2,1)S(1)}, bf16[2,2,32,1152]{3,2,1,0:T(8,128)(2,1)}, u32[]{:S(2)}, u32[]{:S(2)}) collective-permute-start(bf16[2,2,32,1152]{3,2,1,0:T(8,128)(2,1)S(1)} %collective-permute-done.6.refs_6_), channel_id=1, source_target_pairs={{0,32},{32,0},{1,33},{33,1},{2,34},{34,2},{3,35},{35,3},{4,36},{36... | collective-permute-start | bytes 884744 | tf_op jit(solution)/shard_map/ppermute | solution.py:159
  81.1 0.0 collective-permute-done.11.refs_11_
  81.1 2.4 %collective-permute-start.13 = (bf16[2,2,32,1152]{3,2,1,0:T(8,128)(2,1)}, bf16[2,2,32,1152]{3,2,1,0:T(8,128)(2,1)}, u32[]{:S(2)}, u32[]{:S(2)}) collective-permute-start(bf16[2,2,32,1152]{3,2,1,0:T(8,128)(2,1)} %collective-permute-done.5.refs_5_), channel_id=1, source_target_pairs={{0,32},{32,0},{1,33},{33,1},{2,34},{34,2},{3,35},{35,3},{4,36},{36... | collective-permute-start | bytes 884744 | tf_op jit(solution)/shard_map/ppermute | solution.py:159
  83.6 0.0 collective-permute-done.7.refs_7_
  83.6 1.9 %collective-permute-start.15 = (bf16[2,2,32,1152]{3,2,1,0:T(8,128)(2,1)}, bf16[2,2,32,1152]{3,2,1,0:T(8,128)(2,1)}, u32[]{:S(2)}, u32[]{:S(2)}) collective-permute-start(bf16[2,2,32,1152]{3,2,1,0:T(8,128)(2,1)} %collective-permute-done.7.refs_7_), channel_id=1, source_target_pairs={{0,32},{32,0},{1,33},{33,1},{2,34},{34,2},{3,35},{35,3},{4,36},{36... | collective-permute-start | bytes 884744 | tf_op jit(solution)/shard_map/ppermute | solution.py:159
  85.5 0.0 collective-permute-done.8.refs_8_
  85.5 3.1 %collective-permute-start.16 = (bf16[2,32,1152]{2,1,0:T(8,128)(2,1)S(1)}, bf16[2,32,1152]{2,1,0:T(8,128)(2,1)}, u32[]{:S(2)}, u32[]{:S(2)}) collective-permute-start(bf16[2,32,1152]{2,1,0:T(8,128)(2,1)S(1)} %collective-permute-done.8.refs_8_), channel_id=1, source_target_pairs={{0,32},{32,0},{1,33},{33,1},{2,34},{34,2},{3,35},{35,3},{4,36},{36... | collective-permute-start | bytes 442376 | tf_op jit(solution)/shard_map/ppermute | solution.py:159
  88.6 1.9 %shard_map.57.weight_ref = bf16[128,768]{1,0:T(8,128)(2,1)} custom-call(s32[8,64]{1,0:T(8,128)} %bitcast.13, f32[8,64]{1,0:T(8,128)} %bitcast.14), custom_call_target="tpu_custom_call" | custom-call | flops 25165824 | bytes 196608 | tf_op jit(solution)/shard_map/pallas_call | solution.py:148
  90.5 0.7 pad_add_fusion.place_ref
  91.2 0.0 collective-permute-done.12.refs_12_
  91.2 0.0 collective-permute-done.16.refs_16_
  91.2 0.0 collective-permute-done.13.refs_13_
  91.2 0.0 collective-permute-done.14.refs_14_
  91.2 0.0 collective-permute-done.15.refs_15_
  91.2 0.0 all-to-all-done.x_ref
  91.3 1.1 copy-done
  92.5 8.7 %shard_map.56 = bf16[32,24,1024]{2,1,0:T(8,128)(2,1)} custom-call(s32[2]{0:T(128)} %pad_add_fusion.place_ref, bf16[32,24,1024]{2,1,0:T(8,128)(2,1)} %copy-done, bf16[2,2,32,1152]{3,2,1,0:T(8,128)(2,1)} %copy-done.1, bf16[2,2,32,1152]{3,2,1,0:T(8,128)(2,1)} %copy-done.7, bf16[2,2,32,1152]{3,2,1,0:T(8,128)(2,1)} %copy-done.5, ...), custom_call_target="tpu_custom_call" | custom-call | flops 2415919104 | bytes 7864320 | tf_op jit(solution)/shard_map/pallas_call | solution.py:148
  101.2 49.4 %all_to_all.10.back_ref = bf16[32,24,1024]{2,1,0:T(8,128)(2,1)} all-to-all(bf16[32,24,1024]{2,1,0:T(8,128)(2,1)} %shard_map.56), channel_id=1, replica_groups=mesh['z'=16,'c'=2,'expert'=32] {'expert'}, dimensions={0} | all-to-all | bytes 3145728 | tf_op jit(solution)/shard_map/all_to_all | solution.py:163
  150.6 2.6 %shard_map.58 = bf16[64,1024]{1,0:T(8,128)(2,1)} custom-call(bf16[128,768]{1,0:T(8,128)(2,1)} %shard_map.57.weight_ref, bf16[32,24,1024]{2,1,0:T(8,128)(2,1)} %all_to_all.10.back_ref), custom_call_target="tpu_custom_call" | custom-call | flops 201326592 | bytes 1572864 | tf_op jit(solution)/shard_map/pallas_call | solution.py:148
  (23 shorter events, 0.1 us)
Async XLA Ops:
  2.9 10.6 %copy-start.2 = (bf16[2,32,768]{2,1,0:T(8,128)(2,1)S(1)}, bf16[2,32,768]{2,1,0:T(8,128)(2,1)}, u32[]{:S(2)}) copy-start(bf16[2,32,768]{2,1,0:T(8,128)(2,1)} %param.8) | copy-start | bytes 294916
  2.9 10.6 %copy-start.4 = (bf16[2,384,32]{1,2,0:T(8,128)(2,1)S(1)}, bf16[2,384,32]{1,2,0:T(8,128)(2,1)}, u32[]{:S(2)}) copy-start(bf16[2,384,32]{1,2,0:T(8,128)(2,1)} %param.9) | copy-start | bytes 147460
  2.9 88.3 %all-to-all-start = ((bf16[32,24,1024]{2,1,0:T(8,128)(2,1)}), bf16[32,24,1024]{2,1,0:T(8,128)(2,1)S(1)}, u32[]{:S(2)}, u32[]{:S(2)}) async-start(bf16[32,24,1024]{2,1,0:T(8,128)(2,1)} %shard_map.55), calls=%async_computation | async-start | bytes 3145728 | tf_op jit(solution)/shard_map/all_to_all | solution.py:163
  13.6 10.5 %collective-permute-start = (bf16[2,32,1152]{2,1,0:T(8,128)(2,1)S(1)}, bf16[2,32,1152]{2,1,0:T(8,128)(2,1)S(1)}, u32[]{:S(2)}, u32[]{:S(2)}) collective-permute-start(bf16[2,32,1152]{2,1,0:T(8,128)(2,1)S(1)} %get-tuple-element.10), channel_id=1, source_target_pairs={{0,32},{32,0},{1,33},{33,1},{2,34},{34,2},{3,35},{35,3},{4,36},{36... | collective-permute-start | bytes 442376 | tf_op jit(solution)/shard_map/ppermute | solution.py:159
  24.2 67.1 %copy-start.1 = (bf16[2,2,32,1152]{3,2,1,0:T(8,128)(2,1)}, bf16[2,2,32,1152]{3,2,1,0:T(8,128)(2,1)S(1)}, u32[]{:S(2)}) copy-start(bf16[2,2,32,1152]{3,2,1,0:T(8,128)(2,1)S(1)} %pad_maximum_fusion.refs_0_) | copy-start | bytes 884740
  24.2 18.1 %collective-permute-start.2 = (bf16[2,2,32,1152]{3,2,1,0:T(8,128)(2,1)S(1)}, bf16[2,2,32,1152]{3,2,1,0:T(8,128)(2,1)S(1)}, u32[]{:S(2)}, u32[]{:S(2)}) collective-permute-start(bf16[2,2,32,1152]{3,2,1,0:T(8,128)(2,1)S(1)} %pad_maximum_fusion.refs_0_), channel_id=1, source_target_pairs={{0,128},{32,928},{64,192},{96,992},{128,256},{160,32},{192,320},{2... | collective-permute-start | bytes 884744 | tf_op jit(solution)/shard_map/ppermute | solution.py:169
  42.3 49.0 %copy-start.5 = (bf16[2,2,32,1152]{3,2,1,0:T(8,128)(2,1)}, bf16[2,2,32,1152]{3,2,1,0:T(8,128)(2,1)S(1)}, u32[]{:S(2)}) copy-start(bf16[2,2,32,1152]{3,2,1,0:T(8,128)(2,1)S(1)} %collective-permute-done.2.refs_2_) | copy-start | bytes 884740
  42.3 12.4 %collective-permute-start.4 = (bf16[2,2,32,1152]{3,2,1,0:T(8,128)(2,1)S(1)}, bf16[2,2,32,1152]{3,2,1,0:T(8,128)(2,1)S(1)}, u32[]{:S(2)}, u32[]{:S(2)}) collective-permute-start(bf16[2,2,32,1152]{3,2,1,0:T(8,128)(2,1)S(1)} %collective-permute-done.2.refs_2_), channel_id=1, source_target_pairs={{0,128},{32,928},{64,192},{96,992},{128,256},{160,32},{192,320},{2... | collective-permute-start | bytes 884744 | tf_op jit(solution)/shard_map/ppermute | solution.py:169
  48.5 14.1 %collective-permute-start.1 = (bf16[2,2,32,1152]{3,2,1,0:T(8,128)(2,1)S(1)}, bf16[2,2,32,1152]{3,2,1,0:T(8,128)(2,1)S(1)}, u32[]{:S(2)}, u32[]{:S(2)}) collective-permute-start(bf16[2,2,32,1152]{3,2,1,0:T(8,128)(2,1)S(1)} %pad_maximum_fusion.refs_0_), channel_id=1, source_target_pairs={{0,64},{32,992},{64,128},{96,32},{128,192},{160,96},{192,256},{224... | collective-permute-start | bytes 884744 | tf_op jit(solution)/shard_map/ppermute | solution.py:169
  50.4 17.2 %collective-permute-start.3 = (bf16[2,2,32,1152]{3,2,1,0:T(8,128)(2,1)S(1)}, bf16[2,2,32,1152]{3,2,1,0:T(8,128)(2,1)S(1)}, u32[]{:S(2)}, u32[]{:S(2)}) collective-permute-start(bf16[2,2,32,1152]{3,2,1,0:T(8,128)(2,1)S(1)} %collective-permute-done.2.refs_2_), channel_id=1, source_target_pairs={{0,64},{32,992},{64,128},{96,32},{128,192},{160,96},{192,256},{224... | collective-permute-start | bytes 884744 | tf_op jit(solution)/shard_map/ppermute | solution.py:169
  54.6 36.6 %copy-start.6 = (bf16[2,2,32,1152]{3,2,1,0:T(8,128)(2,1)}, bf16[2,2,32,1152]{3,2,1,0:T(8,128)(2,1)S(1)}, u32[]{:S(2)}) copy-start(bf16[2,2,32,1152]{3,2,1,0:T(8,128)(2,1)S(1)} %collective-permute-done.4.refs_4_) | copy-start | bytes 884740
  54.6 14.9 %collective-permute-start.6 = (bf16[2,2,32,1152]{3,2,1,0:T(8,128)(2,1)S(1)}, bf16[2,2,32,1152]{3,2,1,0:T(8,128)(2,1)S(1)}, u32[]{:S(2)}, u32[]{:S(2)}) collective-permute-start(bf16[2,2,32,1152]{3,2,1,0:T(8,128)(2,1)S(1)} %collective-permute-done.4.refs_4_), channel_id=1, source_target_pairs={{0,128},{32,928},{64,192},{96,992},{128,256},{160,32},{192,320},{2... | collective-permute-start | bytes 884744 | tf_op jit(solution)/shard_map/ppermute | solution.py:169
  60.7 15.1 %collective-permute-start.10 = (bf16[2,2,32,1152]{3,2,1,0:T(8,128)(2,1)S(1)}, bf16[2,2,32,1152]{3,2,1,0:T(8,128)(2,1)S(1)}, u32[]{:S(2)}, u32[]{:S(2)}) collective-permute-start(bf16[2,2,32,1152]{3,2,1,0:T(8,128)(2,1)S(1)} %collective-permute-done.2.refs_2_), channel_id=1, source_target_pairs={{0,32},{32,0},{1,33},{33,1},{2,34},{34,2},{3,35},{35,3},{4,36},{36... | collective-permute-start | bytes 884744 | tf_op jit(solution)/shard_map/ppermute | solution.py:159
  62.6 28.6 %copy-start.7 = (bf16[2,2,32,1152]{3,2,1,0:T(8,128)(2,1)}, bf16[2,2,32,1152]{3,2,1,0:T(8,128)(2,1)S(1)}, u32[]{:S(2)}) copy-start(bf16[2,2,32,1152]{3,2,1,0:T(8,128)(2,1)S(1)} %collective-permute-done.1.refs_1_) | copy-start | bytes 884740
  62.6 11.2 %collective-permute-start.9 = (bf16[2,2,32,1152]{3,2,1,0:T(8,128)(2,1)S(1)}, bf16[2,2,32,1152]{3,2,1,0:T(8,128)(2,1)S(1)}, u32[]{:S(2)}, u32[]{:S(2)}) collective-permute-start(bf16[2,2,32,1152]{3,2,1,0:T(8,128)(2,1)S(1)} %collective-permute-done.1.refs_1_), channel_id=1, source_target_pairs={{0,32},{32,0},{1,33},{33,1},{2,34},{34,2},{3,35},{35,3},{4,36},{36... | collective-permute-start | bytes 884744 | tf_op jit(solution)/shard_map/ppermute | solution.py:159
  65.1 14.1 %collective-permute-start.5 = (bf16[2,2,32,1152]{3,2,1,0:T(8,128)(2,1)S(1)}, bf16[2,2,32,1152]{3,2,1,0:T(8,128)(2,1)}, u32[]{:S(2)}, u32[]{:S(2)}) collective-permute-start(bf16[2,2,32,1152]{3,2,1,0:T(8,128)(2,1)S(1)} %collective-permute-done.4.refs_4_), channel_id=1, source_target_pairs={{0,64},{32,992},{64,128},{96,32},{128,192},{160,96},{192,256},{224... | collective-permute-start | bytes 884744 | tf_op jit(solution)/shard_map/ppermute | solution.py:169
  67.6 23.7 %copy-start.8 = (bf16[2,2,32,1152]{3,2,1,0:T(8,128)(2,1)}, bf16[2,2,32,1152]{3,2,1,0:T(8,128)(2,1)S(1)}, u32[]{:S(2)}) copy-start(bf16[2,2,32,1152]{3,2,1,0:T(8,128)(2,1)S(1)} %collective-permute-done.3.refs_3_) | copy-start | bytes 884740
  67.6 13.5 %collective-permute-start.11 = (bf16[2,2,32,1152]{3,2,1,0:T(8,128)(2,1)S(1)}, bf16[2,2,32,1152]{3,2,1,0:T(8,128)(2,1)S(1)}, u32[]{:S(2)}, u32[]{:S(2)}) collective-permute-start(bf16[2,2,32,1152]{3,2,1,0:T(8,128)(2,1)S(1)} %collective-permute-done.3.refs_3_), channel_id=1, source_target_pairs={{0,32},{32,0},{1,33},{33,1},{2,34},{34,2},{3,35},{35,3},{4,36},{36... | collective-permute-start | bytes 884744 | tf_op jit(solution)/shard_map/ppermute | solution.py:159
  69.6 21.7 %copy-start.3 = (bf16[2,2,32,1152]{3,2,1,0:T(8,128)(2,1)}, bf16[2,2,32,1152]{3,2,1,0:T(8,128)(2,1)S(1)}, u32[]{:S(2)}) copy-start(bf16[2,2,32,1152]{3,2,1,0:T(8,128)(2,1)S(1)} %collective-permute-done.6.refs_6_) | copy-start | bytes 884740
  69.6 14.0 %collective-permute-start.7 = (bf16[2,2,32,1152]{3,2,1,0:T(8,128)(2,1)S(1)}, bf16[2,2,32,1152]{3,2,1,0:T(8,128)(2,1)}, u32[]{:S(2)}, u32[]{:S(2)}) collective-permute-start(bf16[2,2,32,1152]{3,2,1,0:T(8,128)(2,1)S(1)} %collective-permute-done.6.refs_6_), channel_id=1, source_target_pairs={{0,64},{32,992},{64,128},{96,32},{128,192},{160,96},{192,256},{224... | collective-permute-start | bytes 884744 | tf_op jit(solution)/shard_map/ppermute | solution.py:169
  73.8 14.8 %copy-start.10 = (bf16[2,2,32,1152]{3,2,1,0:T(8,128)(2,1)}, bf16[2,2,32,1152]{3,2,1,0:T(8,128)(2,1)S(1)}, u32[]{:S(2)}) copy-start(bf16[2,2,32,1152]{3,2,1,0:T(8,128)(2,1)S(1)} %collective-permute-done.9.refs_9_) | copy-start | bytes 884740
  73.9 17.3 %collective-permute-start.12 = (bf16[2,2,32,1152]{3,2,1,0:T(8,128)(2,1)S(1)}, bf16[2,2,32,1152]{3,2,1,0:T(8,128)(2,1)}, u32[]{:S(2)}, u32[]{:S(2)}) collective-permute-start(bf16[2,2,32,1152]{3,2,1,0:T(8,128)(2,1)S(1)} %collective-permute-done.4.refs_4_), channel_id=1, source_target_pairs={{0,32},{32,0},{1,33},{33,1},{2,34},{34,2},{3,35},{35,3},{4,36},{36... | collective-permute-start | bytes 884744 | tf_op jit(solution)/shard_map/ppermute | solution.py:159
  75.8 9.7 %copy-start.9 = (bf16[2,2,32,1152]{3,2,1,0:T(8,128)(2,1)}, bf16[2,2,32,1152]{3,2,1,0:T(8,128)(2,1)S(1)}, u32[]{:S(2)}) copy-start(bf16[2,2,32,1152]{3,2,1,0:T(8,128)(2,1)S(1)} %collective-permute-done.10.refs_10_) | copy-start | bytes 884740
  75.8 9.7 %collective-permute-start.8 = (bf16[2,32,1152]{2,1,0:T(8,128)(2,1)S(1)}, bf16[2,32,1152]{2,1,0:T(8,128)(2,1)S(1)}, u32[]{:S(2)}, u32[]{:S(2)}) collective-permute-start(bf16[2,32,1152]{2,1,0:T(8,128)(2,1)S(1)} %slice_bitcast_fusion), channel_id=1, source_target_pairs={{0,128},{32,928},{64,192},{96,992},{128,256},{160,32},{192,320},{2... | collective-permute-start | bytes 442376 | tf_op jit(solution)/shard_map/ppermute | solution.py:169
  79.2 12.0 %collective-permute-start.14 = (bf16[2,2,32,1152]{3,2,1,0:T(8,128)(2,1)S(1)}, bf16[2,2,32,1152]{3,2,1,0:T(8,128)(2,1)}, u32[]{:S(2)}, u32[]{:S(2)}) collective-permute-start(bf16[2,2,32,1152]{3,2,1,0:T(8,128)(2,1)S(1)} %collective-permute-done.6.refs_6_), channel_id=1, source_target_pairs={{0,32},{32,0},{1,33},{33,1},{2,34},{34,2},{3,35},{35,3},{4,36},{36... | collective-permute-start | bytes 884744 | tf_op jit(solution)/shard_map/ppermute | solution.py:159
  81.1 7.5 %copy-start.11 = (bf16[2,2,32,1152]{3,2,1,0:T(8,128)(2,1)}, bf16[2,2,32,1152]{3,2,1,0:T(8,128)(2,1)S(1)}, u32[]{:S(2)}) copy-start(bf16[2,2,32,1152]{3,2,1,0:T(8,128)(2,1)S(1)} %collective-permute-done.11.refs_11_) | copy-start | bytes 884740
  81.1 10.1 %collective-permute-start.13 = (bf16[2,2,32,1152]{3,2,1,0:T(8,128)(2,1)}, bf16[2,2,32,1152]{3,2,1,0:T(8,128)(2,1)}, u32[]{:S(2)}, u32[]{:S(2)}) collective-permute-start(bf16[2,2,32,1152]{3,2,1,0:T(8,128)(2,1)} %collective-permute-done.5.refs_5_), channel_id=1, source_target_pairs={{0,32},{32,0},{1,33},{33,1},{2,34},{34,2},{3,35},{35,3},{4,36},{36... | collective-permute-start | bytes 884744 | tf_op jit(solution)/shard_map/ppermute | solution.py:159
  83.6 7.7 %collective-permute-start.15 = (bf16[2,2,32,1152]{3,2,1,0:T(8,128)(2,1)}, bf16[2,2,32,1152]{3,2,1,0:T(8,128)(2,1)}, u32[]{:S(2)}, u32[]{:S(2)}) collective-permute-start(bf16[2,2,32,1152]{3,2,1,0:T(8,128)(2,1)} %collective-permute-done.7.refs_7_), channel_id=1, source_target_pairs={{0,32},{32,0},{1,33},{33,1},{2,34},{34,2},{3,35},{35,3},{4,36},{36... | collective-permute-start | bytes 884744 | tf_op jit(solution)/shard_map/ppermute | solution.py:159
  85.5 5.8 %copy-start.12 = (bf16[2,32,1152]{2,1,0:T(8,128)(2,1)}, bf16[2,32,1152]{2,1,0:T(8,128)(2,1)S(1)}, u32[]{:S(2)}) copy-start(bf16[2,32,1152]{2,1,0:T(8,128)(2,1)S(1)} %collective-permute-done.8.refs_8_) | copy-start | bytes 442372
  85.5 5.7 %collective-permute-start.16 = (bf16[2,32,1152]{2,1,0:T(8,128)(2,1)S(1)}, bf16[2,32,1152]{2,1,0:T(8,128)(2,1)}, u32[]{:S(2)}, u32[]{:S(2)}) collective-permute-start(bf16[2,32,1152]{2,1,0:T(8,128)(2,1)S(1)} %collective-permute-done.8.refs_8_), channel_id=1, source_target_pairs={{0,32},{32,0},{1,33},{33,1},{2,34},{34,2},{3,35},{35,3},{4,36},{36... | collective-permute-start | bytes 442376 | tf_op jit(solution)/shard_map/ppermute | solution.py:159
  91.3 1.1 copy-start

commit v6 on v5

--- a/solution.py
+++ b/solution.py
@@ -99,15 +99,17 @@
     return made[: owners * 8].reshape(shape), made[owners * 8 :].reshape(shape)
 
 
-def expert_kernel(place_ref, x_ref, *refs):
-    *blocks, y_ref, whole, sems = refs
-    chips = whole.shape[0]
+def expert_kernel(place_ref, x_hbm, *refs):
+    *blocks, y_hbm, x_ref, y_ref, whole, sems, row_sems = refs
+    chips = whole.shape[1]
     width, both = x_ref.shape[2], whole.shape[4]
     z, core = place_ref[0], place_ref[1]
-    copies = []
+    copies = [[], []]
 
     def put(block, chip, lane):
-        copies.append(pltpu.make_async_copy(block, whole.at[chip, lane], sems.at[len(copies)]))
+        for e in range(2):
+            sem = sems.at[e, len(copies[e])]
+            copies[e].append(pltpu.make_async_copy(block.at[e], whole.at[e, chip, lane], sem))
 
     count = chips // 2
     for k, block in enumerate(blocks):
@@ -119,38 +121,62 @@
         else:
             put(block.at[0], chip, lane)
             put(block.at[1], chip, 1 - lane)
-    for copy in copies:
-        copy.start()
-    for copy in copies:
-        copy.wait()
+    rows_in = pltpu.make_async_copy(x_hbm, x_ref, row_sems.at[0])
+    rows_in.start()
+    for e in range(2):
+        for copy in copies[e]:
+            copy.start()
+    rows_in.wait()
     wide = 2 * both // 3
-    made = []
+    made, out = [], []
     for e in range(2):
-        w_in = whole[:, :, e, :, :wide].reshape(width, wide)
-        w_out = whole[:, :, e, :, wide:].reshape(width, both - wide)
+        for copy in copies[e]:
+            copy.wait()
+        w_in = whole[e, :, :, :, :wide].reshape(width, wide)
+        w_out = whole[e, :, :, :, wide:].reshape(width, both - wide)
         full, rest = expert_rows(x_ref, 8 * e, w_in, w_out)
-        y_ref[:, 8 * e : 8 * e + 8] = full.astype(BF16)
+        y_ref[e] = full.astype(BF16)
+        out.append(pltpu.make_async_copy(y_ref.at[e], y_hbm.at[:, 8 * e : 8 * e + 8], row_sems.at[1 + e]))
+        out[e].start()
         made.append(rest)
     first = iota(made[0].shape, 1) < 4
-    y_ref[:, 16:24] = jnp.where(first, made[0], made[1]).astype(BF16)
-
-
-def combine_kernel(weight_ref, back_ref, out_ref):
+    y_ref[2] = jnp.where(first, made[0], made[1]).astype(BF16)
+    out.append(pltpu.make_async_copy(y_ref.at[2], y_hbm.at[:, 16:24], row_sems.at[3]))
+    out[2].start()
+    for copy in out:
+        copy.wait()
+
+
+def combine_kernel(weight_ref, back_hbm, out_ref, back_ref, sems):
     rows, width = out_ref.shape
-    mixed = dot(weight_ref[...], back_ref[...].reshape(-1, width))
+    owners, per, _ = back_ref.shape
+    parts = sems.shape[0]
+    some = owners // parts
+    copies = []
+    for k in range(parts):
+        at = pl.ds(k * some, some)
+        copies.append(pltpu.make_async_copy(back_hbm.at[at], back_ref.at[at], sems.at[k]))
+        copies[k].start()
+    mixed = 0.0
+    for k in range(parts):
+        copies[k].wait()
+        back = back_ref[k * some : (k + 1) * some].reshape(some * per, width)
+        mixed = mixed + dot(weight_ref[:, k * some * per : (k + 1) * some * per], back)
     out_ref[...] = (mixed[:rows] + mixed[rows:]).astype(BF16)
 
 
 VMEM = pl.BlockSpec(memory_space=pltpu.VMEM)
-
-
-def call(kernel, outs, args, flops, moved, specs=None, scratch=()):
+ANY = pl.BlockSpec(memory_space=pl.ANY)
+
+
+def call(kernel, outs, args, flops, moved, specs=None, out_specs=VMEM, scratch=(), limit=None):
     return pl.pallas_call(
         kernel,
         out_shape=outs,
         in_specs=[VMEM] * len(args) if specs is None else specs,
-        out_specs=VMEM,
+        out_specs=out_specs,
         scratch_shapes=list(scratch),
+        compiler_params=pltpu.CompilerParams(vmem_limit_bytes=limit),
         cost_estimate=pl.CostEstimate(flops=flops, bytes_accessed=moved, transcendentals=0),
     )(*args)
 
@@ -215,12 +241,16 @@
         (place, arrived, *blocks),
         2 * 1024 * 3 * hidden * width,
         4 * slots * width + 12 * hidden * width,
-        specs=[pl.BlockSpec(memory_space=pltpu.SMEM), VMEM]
-        + [pl.BlockSpec(memory_space=pl.ANY)] * len(blocks),
+        specs=[pl.BlockSpec(memory_space=pltpu.SMEM)] + [ANY] * (1 + len(blocks)),
+        out_specs=ANY,
         scratch=[
-            pltpu.VMEM((chips, 2, 2, BLOCK, 3 * hidden), BF16),
-            pltpu.SemaphoreType.DMA((2 * chips,)),
+            pltpu.VMEM((owners, ROWS, width), BF16),
+            pltpu.VMEM((3, owners, 8, width), BF16),
+            pltpu.VMEM((2, chips, 2, BLOCK, 3 * hidden), BF16),
+            pltpu.SemaphoreType.DMA((2, 2 * chips)),
+            pltpu.SemaphoreType.DMA((4,)),
         ],
+        limit=28 << 20,
     )
     produced, weight = lax.optimization_barrier((produced, weight))
     back = exchanged(produced)
@@ -230,6 +260,9 @@
         (weight, back),
         4 * slots * rows * width,
         2 * slots * width,
+        specs=[VMEM, ANY],
+        scratch=[pltpu.VMEM((owners, ROWS, width), BF16), pltpu.SemaphoreType.DMA((2,))],
+        limit=16 << 20,
     )
 
 

time: 154 us -> 156 us (1.013)
  local copies, waits for them, and re-layouts: 1.2 us -> 5.03 us
    unnamed x26 -> x18, local copies, waits for them, and re-layouts: 1.19 us -> 5.02 us
where the time goes in v6:
time: 156 us; the launch traced here: 155 us
  starting transfers between devices  74.7 us (48%)
  blocking collectives  49.2 us (32%)
  Pallas kernels  16.1 us (10%)
  waiting for transfers between devices  9.84 us (6%)
  local copies, waits for them, and re-layouts  5.03 us (3%)
    all_to_all x1, blocking collectives, exchanged(): return lax.all_to_all(x, 'expert', split_axis=0, concat_axis=0, tiled=True)  49.2 us
    ppermute x8, starting transfers between devices, along(): return lax.ppermute(x, ('z', 'c'), pairs)  37.8 us
    ppermute x9, starting transfers between devices, swapped(): return lax.ppermute(x, 'c', [(0, 1), (1, 0)])  26.3 us
    pallas_call x4, Pallas kernels, call(): pl.pallas_call(kernel, out_shape=outs, in_specs=[VMEM] * len(args) if spe...  16.1 us
    all_to_all x1, starting transfers between devices, exchanged(): return lax.all_to_all(x, 'expert', split_axis=0, concat_axis=0, tiled=True)  10.6 us
    ppermute x8, waiting for transfers between devices, along(): return lax.ppermute(x, ('z', 'c'), pairs)  8.83 us
    unnamed x18, local copies, waits for them, and re-layouts  5.02 us
  transfers between devices with their start and end apart: 18, of which 3 were waited for; matrix products, arithmetic and copies ran while one was open for 0% of the time, Pallas kernels for 1%

profile of v6, /device:TPU:1, one launch (start us, length us, event | category | flops | bytes accessed | tf_op | source)
XLA Modules:
  0.0 155.4 jit_solution(12028276478158964860)
XLA Ops:
  0.0 2.9 %shard_map.55 = bf16[32,24,1024]{2,1,0:T(8,128)(2,1)} custom-call(s32[8,64]{1,0:T(8,128)} %bitcast.12, bf16[64,1024]{1,0:T(8,128)(2,1)} %tok_ref.1), custom_call_target="tpu_custom_call" | custom-call | flops 100663296 | bytes 1572864 | tf_op jit(solution)/shard_map/pallas_call | solution.py:173
  2.9 10.6 %all-to-all-start = ((bf16[32,24,1024]{2,1,0:T(8,128)(2,1)}), bf16[32,24,1024]{2,1,0:T(8,128)(2,1)S(1)}, u32[]{:S(2)}, u32[]{:S(2)}) async-start(bf16[32,24,1024]{2,1,0:T(8,128)(2,1)} %shard_map.55), calls=%async_computation | async-start | bytes 3145728 | tf_op jit(solution)/shard_map/all_to_all | solution.py:189
  13.6 9.5 %collective-permute-start = (bf16[2,32,1152]{2,1,0:T(8,128)(2,1)S(1)}, bf16[2,32,1152]{2,1,0:T(8,128)(2,1)S(1)}, u32[]{:S(2)}, u32[]{:S(2)}) collective-permute-start(bf16[2,32,1152]{2,1,0:T(8,128)(2,1)S(1)} %get-tuple-element.10), channel_id=1, source_target_pairs={{0,32},{32,0},{1,33},{33,1},{2,34},{34,2},{3,35},{35,3},{4,36},{36... | collective-permute-start | bytes 442376 | tf_op jit(solution)/shard_map/ppermute | solution.py:185
  23.1 1.0 collective-permute-done
  24.1 11.3 %collective-permute-start.2 = (bf16[2,2,32,1152]{3,2,1,0:T(8,128)(2,1)S(1)}, bf16[2,2,32,1152]{3,2,1,0:T(8,128)(2,1)S(1)}, u32[]{:S(2)}, u32[]{:S(2)}) collective-permute-start(bf16[2,2,32,1152]{3,2,1,0:T(8,128)(2,1)S(1)} %pad_maximum_fusion.refs_0_), channel_id=1, source_target_pairs={{0,128},{32,928},{64,192},{96,992},{128,256},{160,32},{192,320},{2... | collective-permute-start | bytes 884744 | tf_op jit(solution)/shard_map/ppermute | solution.py:195
  35.4 6.8 %collective-permute-done.2.refs_2_ = bf16[2,2,32,1152]{3,2,1,0:T(8,128)(2,1)S(1)} collective-permute-done((bf16[2,2,32,1152]{3,2,1,0:T(8,128)(2,1)S(1)}, bf16[2,2,32,1152]{3,2,1,0:T(8,128)(2,1)S(1)}, u32[]{:S(2)}, u32[]{:S(2)}) %collective-permute-start.2) | collective-permute-done | bytes 294944 | tf_op jit(solution)/shard_map/ppermute | solution.py:195
  42.2 6.2 %collective-permute-start.4 = (bf16[2,2,32,1152]{3,2,1,0:T(8,128)(2,1)S(1)}, bf16[2,2,32,1152]{3,2,1,0:T(8,128)(2,1)S(1)}, u32[]{:S(2)}, u32[]{:S(2)}) collective-permute-start(bf16[2,2,32,1152]{3,2,1,0:T(8,128)(2,1)S(1)} %collective-permute-done.2.refs_2_), channel_id=1, source_target_pairs={{0,128},{32,928},{64,192},{96,992},{128,256},{160,32},{192,320},{2... | collective-permute-start | bytes 884744 | tf_op jit(solution)/shard_map/ppermute | solution.py:195
  48.5 1.9 %collective-permute-start.1 = (bf16[2,2,32,1152]{3,2,1,0:T(8,128)(2,1)S(1)}, bf16[2,2,32,1152]{3,2,1,0:T(8,128)(2,1)S(1)}, u32[]{:S(2)}, u32[]{:S(2)}) collective-permute-start(bf16[2,2,32,1152]{3,2,1,0:T(8,128)(2,1)S(1)} %pad_maximum_fusion.refs_0_), channel_id=1, source_target_pairs={{0,64},{32,992},{64,128},{96,32},{128,192},{160,96},{192,256},{224... | collective-permute-start | bytes 884744 | tf_op jit(solution)/shard_map/ppermute | solution.py:195
  50.4 2.2 %collective-permute-start.3 = (bf16[2,2,32,1152]{3,2,1,0:T(8,128)(2,1)S(1)}, bf16[2,2,32,1152]{3,2,1,0:T(8,128)(2,1)S(1)}, u32[]{:S(2)}, u32[]{:S(2)}) collective-permute-start(bf16[2,2,32,1152]{3,2,1,0:T(8,128)(2,1)S(1)} %collective-permute-done.2.refs_2_), channel_id=1, source_target_pairs={{0,64},{32,992},{64,128},{96,32},{128,192},{160,96},{192,256},{224... | collective-permute-start | bytes 884744 | tf_op jit(solution)/shard_map/ppermute | solution.py:195
  52.6 2.0 %collective-permute-done.4.refs_4_ = bf16[2,2,32,1152]{3,2,1,0:T(8,128)(2,1)S(1)} collective-permute-done((bf16[2,2,32,1152]{3,2,1,0:T(8,128)(2,1)S(1)}, bf16[2,2,32,1152]{3,2,1,0:T(8,128)(2,1)S(1)}, u32[]{:S(2)}, u32[]{:S(2)}) %collective-permute-start.4) | collective-permute-done | bytes 294944 | tf_op jit(solution)/shard_map/ppermute | solution.py:195
  54.6 6.1 %collective-permute-start.6 = (bf16[2,2,32,1152]{3,2,1,0:T(8,128)(2,1)S(1)}, bf16[2,2,32,1152]{3,2,1,0:T(8,128)(2,1)S(1)}, u32[]{:S(2)}, u32[]{:S(2)}) collective-permute-start(bf16[2,2,32,1152]{3,2,1,0:T(8,128)(2,1)S(1)} %collective-permute-done.4.refs_4_), channel_id=1, source_target_pairs={{0,128},{32,928},{64,192},{96,992},{128,256},{160,32},{192,320},{2... | collective-permute-start | bytes 884744 | tf_op jit(solution)/shard_map/ppermute | solution.py:195
  60.7 1.9 %collective-permute-start.10 = (bf16[2,2,32,1152]{3,2,1,0:T(8,128)(2,1)S(1)}, bf16[2,2,32,1152]{3,2,1,0:T(8,128)(2,1)S(1)}, u32[]{:S(2)}, u32[]{:S(2)}) collective-permute-start(bf16[2,2,32,1152]{3,2,1,0:T(8,128)(2,1)S(1)} %collective-permute-done.2.refs_2_), channel_id=1, source_target_pairs={{0,32},{32,0},{1,33},{33,1},{2,34},{34,2},{3,35},{35,3},{4,36},{36... | collective-permute-start | bytes 884744 | tf_op jit(solution)/shard_map/ppermute | solution.py:185
  62.6 0.0 collective-permute-done.1.refs_1_
  62.6 2.4 %collective-permute-start.9 = (bf16[2,2,32,1152]{3,2,1,0:T(8,128)(2,1)S(1)}, bf16[2,2,32,1152]{3,2,1,0:T(8,128)(2,1)S(1)}, u32[]{:S(2)}, u32[]{:S(2)}) collective-permute-start(bf16[2,2,32,1152]{3,2,1,0:T(8,128)(2,1)S(1)} %collective-permute-done.1.refs_1_), channel_id=1, source_target_pairs={{0,32},{32,0},{1,33},{33,1},{2,34},{34,2},{3,35},{35,3},{4,36},{36... | collective-permute-start | bytes 884744 | tf_op jit(solution)/shard_map/ppermute | solution.py:185
  65.0 2.5 %collective-permute-start.5 = (bf16[2,2,32,1152]{3,2,1,0:T(8,128)(2,1)S(1)}, bf16[2,2,32,1152]{3,2,1,0:T(8,128)(2,1)}, u32[]{:S(2)}, u32[]{:S(2)}) collective-permute-start(bf16[2,2,32,1152]{3,2,1,0:T(8,128)(2,1)S(1)} %collective-permute-done.4.refs_4_), channel_id=1, source_target_pairs={{0,64},{32,992},{64,128},{96,32},{128,192},{160,96},{192,256},{224... | collective-permute-start | bytes 884744 | tf_op jit(solution)/shard_map/ppermute | solution.py:195
  67.6 0.0 collective-permute-done.3.refs_3_
  67.6 1.9 %collective-permute-start.11 = (bf16[2,2,32,1152]{3,2,1,0:T(8,128)(2,1)S(1)}, bf16[2,2,32,1152]{3,2,1,0:T(8,128)(2,1)S(1)}, u32[]{:S(2)}, u32[]{:S(2)}) collective-permute-start(bf16[2,2,32,1152]{3,2,1,0:T(8,128)(2,1)S(1)} %collective-permute-done.3.refs_3_), channel_id=1, source_target_pairs={{0,32},{32,0},{1,33},{33,1},{2,34},{34,2},{3,35},{35,3},{4,36},{36... | collective-permute-start | bytes 884744 | tf_op jit(solution)/shard_map/ppermute | solution.py:185
  69.5 0.0 collective-permute-done.6.refs_6_
  69.5 4.2 %collective-permute-start.7 = (bf16[2,2,32,1152]{3,2,1,0:T(8,128)(2,1)S(1)}, bf16[2,2,32,1152]{3,2,1,0:T(8,128)(2,1)}, u32[]{:S(2)}, u32[]{:S(2)}) collective-permute-start(bf16[2,2,32,1152]{3,2,1,0:T(8,128)(2,1)S(1)} %collective-permute-done.6.refs_6_), channel_id=1, source_target_pairs={{0,64},{32,992},{64,128},{96,32},{128,192},{160,96},{192,256},{224... | collective-permute-start | bytes 884744 | tf_op jit(solution)/shard_map/ppermute | solution.py:195
  73.8 0.0 collective-permute-done.9.refs_9_
  73.8 0.7 copy-done.3
  74.5 1.9 %collective-permute-start.12 = (bf16[2,2,32,1152]{3,2,1,0:T(8,128)(2,1)S(1)}, bf16[2,2,32,1152]{3,2,1,0:T(8,128)(2,1)}, u32[]{:S(2)}, u32[]{:S(2)}) collective-permute-start(bf16[2,2,32,1152]{3,2,1,0:T(8,128)(2,1)S(1)} %collective-permute-done.4.refs_4_), channel_id=1, source_target_pairs={{0,32},{32,0},{1,33},{33,1},{2,34},{34,2},{3,35},{35,3},{4,36},{36... | collective-permute-start | bytes 884744 | tf_op jit(solution)/shard_map/ppermute | solution.py:185
  76.4 0.0 collective-permute-done.10.refs_10_
  76.4 0.7 copy-done.1
  77.1 3.4 %collective-permute-start.8 = (bf16[2,32,1152]{2,1,0:T(8,128)(2,1)S(1)}, bf16[2,32,1152]{2,1,0:T(8,128)(2,1)S(1)}, u32[]{:S(2)}, u32[]{:S(2)}) collective-permute-start(bf16[2,32,1152]{2,1,0:T(8,128)(2,1)S(1)} %slice_bitcast_fusion), channel_id=1, source_target_pairs={{0,128},{32,928},{64,192},{96,992},{128,256},{160,32},{192,320},{2... | collective-permute-start | bytes 442376 | tf_op jit(solution)/shard_map/ppermute | solution.py:195
  80.5 0.0 collective-permute-done.5.refs_5_
  80.5 1.9 %collective-permute-start.14 = (bf16[2,2,32,1152]{3,2,1,0:T(8,128)(2,1)S(1)}, bf16[2,2,32,1152]{3,2,1,0:T(8,128)(2,1)}, u32[]{:S(2)}, u32[]{:S(2)}) collective-permute-start(bf16[2,2,32,1152]{3,2,1,0:T(8,128)(2,1)S(1)} %collective-permute-done.6.refs_6_), channel_id=1, source_target_pairs={{0,32},{32,0},{1,33},{33,1},{2,34},{34,2},{3,35},{35,3},{4,36},{36... | collective-permute-start | bytes 884744 | tf_op jit(solution)/shard_map/ppermute | solution.py:185
  82.4 0.0 collective-permute-done.11.refs_11_
  82.5 0.7 copy-done.5
  83.2 2.4 %collective-permute-start.13 = (bf16[2,2,32,1152]{3,2,1,0:T(8,128)(2,1)}, bf16[2,2,32,1152]{3,2,1,0:T(8,128)(2,1)}, u32[]{:S(2)}, u32[]{:S(2)}) collective-permute-start(bf16[2,2,32,1152]{3,2,1,0:T(8,128)(2,1)} %collective-permute-done.5.refs_5_), channel_id=1, source_target_pairs={{0,32},{32,0},{1,33},{33,1},{2,34},{34,2},{3,35},{35,3},{4,36},{36... | collective-permute-start | bytes 884744 | tf_op jit(solution)/shard_map/ppermute | solution.py:185
  85.6 0.0 collective-permute-done.7.refs_7_
  85.6 1.9 %collective-permute-start.15 = (bf16[2,2,32,1152]{3,2,1,0:T(8,128)(2,1)}, bf16[2,2,32,1152]{3,2,1,0:T(8,128)(2,1)}, u32[]{:S(2)}, u32[]{:S(2)}) collective-permute-start(bf16[2,2,32,1152]{3,2,1,0:T(8,128)(2,1)} %collective-permute-done.7.refs_7_), channel_id=1, source_target_pairs={{0,32},{32,0},{1,33},{33,1},{2,34},{34,2},{3,35},{35,3},{4,36},{36... | collective-permute-start | bytes 884744 | tf_op jit(solution)/shard_map/ppermute | solution.py:185
  87.5 0.0 collective-permute-done.8.refs_8_
  87.5 2.4 %collective-permute-start.16 = (bf16[2,32,1152]{2,1,0:T(8,128)(2,1)S(1)}, bf16[2,32,1152]{2,1,0:T(8,128)(2,1)}, u32[]{:S(2)}, u32[]{:S(2)}) collective-permute-start(bf16[2,32,1152]{2,1,0:T(8,128)(2,1)S(1)} %collective-permute-done.8.refs_8_), channel_id=1, source_target_pairs={{0,32},{32,0},{1,33},{33,1},{2,34},{34,2},{3,35},{35,3},{4,36},{36... | collective-permute-start | bytes 442376 | tf_op jit(solution)/shard_map/ppermute | solution.py:185
  90.0 1.9 %shard_map.57.weight_ref = bf16[128,768]{1,0:T(8,128)(2,1)} custom-call(s32[8,64]{1,0:T(8,128)} %bitcast.13, f32[8,64]{1,0:T(8,128)} %bitcast.14), custom_call_target="tpu_custom_call" | custom-call | flops 25165824 | bytes 196608 | tf_op jit(solution)/shard_map/pallas_call | solution.py:173
  91.9 0.1 pad_add_fusion.place_ref
  91.9 0.0 collective-permute-done.12.refs_12_
  91.9 0.0 collective-permute-done.16.refs_16_
  91.9 0.0 collective-permute-done.13.refs_13_
  91.9 0.0 collective-permute-done.14.refs_14_
  92.0 0.0 collective-permute-done.15.refs_15_
  92.0 0.0 all-to-all-done.x_hbm
  92.0 1.0 copy-done.2
  92.9 1.0 copy-done.4
  93.9 1.0 copy-done.6
  94.9 10.0 %shard_map.56 = bf16[32,24,1024]{2,1,0:T(8,128)(2,1)S(1)} custom-call(s32[2]{0:T(128)S(1)} %pad_add_fusion.place_ref, bf16[32,24,1024]{2,1,0:T(8,128)(2,1)S(1)} %all-to-all-done.x_hbm, bf16[2,2,32,1152]{3,2,1,0:T(8,128)(2,1)S(1)} %pad_maximum_fusion.refs_0_, bf16[2,2,32,1152]{3,2,1,0:T(8,128)(2,1)S(1)} %collective-permute-done.1.refs_1_, ...), custom_call_target="tpu_custom_call" | custom-call | flops 2415919104 | bytes 7864320 | tf_op jit(solution)/shard_map/pallas_call | solution.py:173
  104.9 49.2 %all_to_all.10.back_hbm = bf16[32,24,1024]{2,1,0:T(8,128)(2,1)S(1)} all-to-all(bf16[32,24,1024]{2,1,0:T(8,128)(2,1)S(1)} %shard_map.56), channel_id=1, replica_groups=mesh['z'=16,'c'=2,'expert'=32] {'expert'}, dimensions={0} | all-to-all | bytes 3145728 | tf_op jit(solution)/shard_map/all_to_all | solution.py:189
  154.1 1.3 shard_map.58
  (15 shorter events, 0.1 us)
Async XLA Ops:
  2.9 10.6 %copy-start.7 = (bf16[2,32,768]{2,1,0:T(8,128)(2,1)S(1)}, bf16[2,32,768]{2,1,0:T(8,128)(2,1)}, u32[]{:S(2)}) copy-start(bf16[2,32,768]{2,1,0:T(8,128)(2,1)} %param.8) | copy-start | bytes 294916
  2.9 10.6 %copy-start.8 = (bf16[2,384,32]{1,2,0:T(8,128)(2,1)S(1)}, bf16[2,384,32]{1,2,0:T(8,128)(2,1)}, u32[]{:S(2)}) copy-start(bf16[2,384,32]{1,2,0:T(8,128)(2,1)} %param.9) | copy-start | bytes 147460
  2.9 89.0 %all-to-all-start = ((bf16[32,24,1024]{2,1,0:T(8,128)(2,1)}), bf16[32,24,1024]{2,1,0:T(8,128)(2,1)S(1)}, u32[]{:S(2)}, u32[]{:S(2)}) async-start(bf16[32,24,1024]{2,1,0:T(8,128)(2,1)} %shard_map.55), calls=%async_computation | async-start | bytes 3145728 | tf_op jit(solution)/shard_map/all_to_all | solution.py:189
  13.6 10.5 %collective-permute-start = (bf16[2,32,1152]{2,1,0:T(8,128)(2,1)S(1)}, bf16[2,32,1152]{2,1,0:T(8,128)(2,1)S(1)}, u32[]{:S(2)}, u32[]{:S(2)}) collective-permute-start(bf16[2,32,1152]{2,1,0:T(8,128)(2,1)S(1)} %get-tuple-element.10), channel_id=1, source_target_pairs={{0,32},{32,0},{1,33},{33,1},{2,34},{34,2},{3,35},{35,3},{4,36},{36... | collective-permute-start | bytes 442376 | tf_op jit(solution)/shard_map/ppermute | solution.py:185
  24.1 18.1 %collective-permute-start.2 = (bf16[2,2,32,1152]{3,2,1,0:T(8,128)(2,1)S(1)}, bf16[2,2,32,1152]{3,2,1,0:T(8,128)(2,1)S(1)}, u32[]{:S(2)}, u32[]{:S(2)}) collective-permute-start(bf16[2,2,32,1152]{3,2,1,0:T(8,128)(2,1)S(1)} %pad_maximum_fusion.refs_0_), channel_id=1, source_target_pairs={{0,128},{32,928},{64,192},{96,992},{128,256},{160,32},{192,320},{2... | collective-permute-start | bytes 884744 | tf_op jit(solution)/shard_map/ppermute | solution.py:195
  42.2 12.4 %collective-permute-start.4 = (bf16[2,2,32,1152]{3,2,1,0:T(8,128)(2,1)S(1)}, bf16[2,2,32,1152]{3,2,1,0:T(8,128)(2,1)S(1)}, u32[]{:S(2)}, u32[]{:S(2)}) collective-permute-start(bf16[2,2,32,1152]{3,2,1,0:T(8,128)(2,1)S(1)} %collective-permute-done.2.refs_2_), channel_id=1, source_target_pairs={{0,128},{32,928},{64,192},{96,992},{128,256},{160,32},{192,320},{2... | collective-permute-start | bytes 884744 | tf_op jit(solution)/shard_map/ppermute | solution.py:195
  48.5 14.1 %collective-permute-start.1 = (bf16[2,2,32,1152]{3,2,1,0:T(8,128)(2,1)S(1)}, bf16[2,2,32,1152]{3,2,1,0:T(8,128)(2,1)S(1)}, u32[]{:S(2)}, u32[]{:S(2)}) collective-permute-start(bf16[2,2,32,1152]{3,2,1,0:T(8,128)(2,1)S(1)} %pad_maximum_fusion.refs_0_), channel_id=1, source_target_pairs={{0,64},{32,992},{64,128},{96,32},{128,192},{160,96},{192,256},{224... | collective-permute-start | bytes 884744 | tf_op jit(solution)/shard_map/ppermute | solution.py:195
  50.4 17.2 %collective-permute-start.3 = (bf16[2,2,32,1152]{3,2,1,0:T(8,128)(2,1)S(1)}, bf16[2,2,32,1152]{3,2,1,0:T(8,128)(2,1)S(1)}, u32[]{:S(2)}, u32[]{:S(2)}) collective-permute-start(bf16[2,2,32,1152]{3,2,1,0:T(8,128)(2,1)S(1)} %collective-permute-done.2.refs_2_), channel_id=1, source_target_pairs={{0,64},{32,992},{64,128},{96,32},{128,192},{160,96},{192,256},{224... | collective-permute-start | bytes 884744 | tf_op jit(solution)/shard_map/ppermute | solution.py:195
  54.6 14.9 %collective-permute-start.6 = (bf16[2,2,32,1152]{3,2,1,0:T(8,128)(2,1)S(1)}, bf16[2,2,32,1152]{3,2,1,0:T(8,128)(2,1)S(1)}, u32[]{:S(2)}, u32[]{:S(2)}) collective-permute-start(bf16[2,2,32,1152]{3,2,1,0:T(8,128)(2,1)S(1)} %collective-permute-done.4.refs_4_), channel_id=1, source_target_pairs={{0,128},{32,928},{64,192},{96,992},{128,256},{160,32},{192,320},{2... | collective-permute-start | bytes 884744 | tf_op jit(solution)/shard_map/ppermute | solution.py:195
  60.7 15.8 %collective-permute-start.10 = (bf16[2,2,32,1152]{3,2,1,0:T(8,128)(2,1)S(1)}, bf16[2,2,32,1152]{3,2,1,0:T(8,128)(2,1)S(1)}, u32[]{:S(2)}, u32[]{:S(2)}) collective-permute-start(bf16[2,2,32,1152]{3,2,1,0:T(8,128)(2,1)S(1)} %collective-permute-done.2.refs_2_), channel_id=1, source_target_pairs={{0,32},{32,0},{1,33},{33,1},{2,34},{34,2},{3,35},{35,3},{4,36},{36... | collective-permute-start | bytes 884744 | tf_op jit(solution)/shard_map/ppermute | solution.py:185
  62.6 11.2 %collective-permute-start.9 = (bf16[2,2,32,1152]{3,2,1,0:T(8,128)(2,1)S(1)}, bf16[2,2,32,1152]{3,2,1,0:T(8,128)(2,1)S(1)}, u32[]{:S(2)}, u32[]{:S(2)}) collective-permute-start(bf16[2,2,32,1152]{3,2,1,0:T(8,128)(2,1)S(1)} %collective-permute-done.1.refs_1_), channel_id=1, source_target_pairs={{0,32},{32,0},{1,33},{33,1},{2,34},{34,2},{3,35},{35,3},{4,36},{36... | collective-permute-start | bytes 884744 | tf_op jit(solution)/shard_map/ppermute | solution.py:185
  65.0 15.5 %collective-permute-start.5 = (bf16[2,2,32,1152]{3,2,1,0:T(8,128)(2,1)S(1)}, bf16[2,2,32,1152]{3,2,1,0:T(8,128)(2,1)}, u32[]{:S(2)}, u32[]{:S(2)}) collective-permute-start(bf16[2,2,32,1152]{3,2,1,0:T(8,128)(2,1)S(1)} %collective-permute-done.4.refs_4_), channel_id=1, source_target_pairs={{0,64},{32,992},{64,128},{96,32},{128,192},{160,96},{192,256},{224... | collective-permute-start | bytes 884744 | tf_op jit(solution)/shard_map/ppermute | solution.py:195
  67.6 14.9 %collective-permute-start.11 = (bf16[2,2,32,1152]{3,2,1,0:T(8,128)(2,1)S(1)}, bf16[2,2,32,1152]{3,2,1,0:T(8,128)(2,1)S(1)}, u32[]{:S(2)}, u32[]{:S(2)}) collective-permute-start(bf16[2,2,32,1152]{3,2,1,0:T(8,128)(2,1)S(1)} %collective-permute-done.3.refs_3_), channel_id=1, source_target_pairs={{0,32},{32,0},{1,33},{33,1},{2,34},{34,2},{3,35},{35,3},{4,36},{36... | collective-permute-start | bytes 884744 | tf_op jit(solution)/shard_map/ppermute | solution.py:185
  69.5 16.1 %collective-permute-start.7 = (bf16[2,2,32,1152]{3,2,1,0:T(8,128)(2,1)S(1)}, bf16[2,2,32,1152]{3,2,1,0:T(8,128)(2,1)}, u32[]{:S(2)}, u32[]{:S(2)}) collective-permute-start(bf16[2,2,32,1152]{3,2,1,0:T(8,128)(2,1)S(1)} %collective-permute-done.6.refs_6_), channel_id=1, source_target_pairs={{0,64},{32,992},{64,128},{96,32},{128,192},{160,96},{192,256},{224... | collective-permute-start | bytes 884744 | tf_op jit(solution)/shard_map/ppermute | solution.py:195
  73.8 0.7 copy-start.3
  74.5 17.4 %collective-permute-start.12 = (bf16[2,2,32,1152]{3,2,1,0:T(8,128)(2,1)S(1)}, bf16[2,2,32,1152]{3,2,1,0:T(8,128)(2,1)}, u32[]{:S(2)}, u32[]{:S(2)}) collective-permute-start(bf16[2,2,32,1152]{3,2,1,0:T(8,128)(2,1)S(1)} %collective-permute-done.4.refs_4_), channel_id=1, source_target_pairs={{0,32},{32,0},{1,33},{33,1},{2,34},{34,2},{3,35},{35,3},{4,36},{36... | collective-permute-start | bytes 884744 | tf_op jit(solution)/shard_map/ppermute | solution.py:185
  76.4 0.7 copy-start.1
  77.1 10.4 %collective-permute-start.8 = (bf16[2,32,1152]{2,1,0:T(8,128)(2,1)S(1)}, bf16[2,32,1152]{2,1,0:T(8,128)(2,1)S(1)}, u32[]{:S(2)}, u32[]{:S(2)}) collective-permute-start(bf16[2,32,1152]{2,1,0:T(8,128)(2,1)S(1)} %slice_bitcast_fusion), channel_id=1, source_target_pairs={{0,128},{32,928},{64,192},{96,992},{128,256},{160,32},{192,320},{2... | collective-permute-start | bytes 442376 | tf_op jit(solution)/shard_map/ppermute | solution.py:195
  80.5 11.4 %collective-permute-start.14 = (bf16[2,2,32,1152]{3,2,1,0:T(8,128)(2,1)S(1)}, bf16[2,2,32,1152]{3,2,1,0:T(8,128)(2,1)}, u32[]{:S(2)}, u32[]{:S(2)}) collective-permute-start(bf16[2,2,32,1152]{3,2,1,0:T(8,128)(2,1)S(1)} %collective-permute-done.6.refs_6_), channel_id=1, source_target_pairs={{0,32},{32,0},{1,33},{33,1},{2,34},{34,2},{3,35},{35,3},{4,36},{36... | collective-permute-start | bytes 884744 | tf_op jit(solution)/shard_map/ppermute | solution.py:185
  82.5 0.7 copy-start.5
  83.2 8.8 %collective-permute-start.13 = (bf16[2,2,32,1152]{3,2,1,0:T(8,128)(2,1)}, bf16[2,2,32,1152]{3,2,1,0:T(8,128)(2,1)}, u32[]{:S(2)}, u32[]{:S(2)}) collective-permute-start(bf16[2,2,32,1152]{3,2,1,0:T(8,128)(2,1)} %collective-permute-done.5.refs_5_), channel_id=1, source_target_pairs={{0,32},{32,0},{1,33},{33,1},{2,34},{34,2},{3,35},{35,3},{4,36},{36... | collective-permute-start | bytes 884744 | tf_op jit(solution)/shard_map/ppermute | solution.py:185
  85.6 6.4 %collective-permute-start.15 = (bf16[2,2,32,1152]{3,2,1,0:T(8,128)(2,1)}, bf16[2,2,32,1152]{3,2,1,0:T(8,128)(2,1)}, u32[]{:S(2)}, u32[]{:S(2)}) collective-permute-start(bf16[2,2,32,1152]{3,2,1,0:T(8,128)(2,1)} %collective-permute-done.7.refs_7_), channel_id=1, source_target_pairs={{0,32},{32,0},{1,33},{33,1},{2,34},{34,2},{3,35},{35,3},{4,36},{36... | collective-permute-start | bytes 884744 | tf_op jit(solution)/shard_map/ppermute | solution.py:185
  87.5 4.4 %collective-permute-start.16 = (bf16[2,32,1152]{2,1,0:T(8,128)(2,1)S(1)}, bf16[2,32,1152]{2,1,0:T(8,128)(2,1)}, u32[]{:S(2)}, u32[]{:S(2)}) collective-permute-start(bf16[2,32,1152]{2,1,0:T(8,128)(2,1)S(1)} %collective-permute-done.8.refs_8_), channel_id=1, source_target_pairs={{0,32},{32,0},{1,33},{33,1},{2,34},{34,2},{3,35},{35,3},{4,36},{36... | collective-permute-start | bytes 442376 | tf_op jit(solution)/shard_map/ppermute | solution.py:185
  92.0 1.0 copy-start.2
  92.9 1.0 copy-start.4
  93.9 1.0 copy-start.6
  104.9 49.2 %copy-start = (bf16[128,768]{1,0:T(8,128)(2,1)S(1)}, bf16[128,768]{1,0:T(8,128)(2,1)}, u32[]{:S(2)}) copy-start(bf16[128,768]{1,0:T(8,128)(2,1)} %shard_map.57.weight_ref) | copy-start | bytes 589828

commit v7 on v6

--- a/solution.py
+++ b/solution.py
@@ -112,7 +112,9 @@
             copies[e].append(pltpu.make_async_copy(block.at[e], whole.at[e, chip, lane], sem))
 
     count = chips // 2
-    for k, block in enumerate(blocks):
+    own, others = blocks[: count + 1], blocks[count + 1 :]
+    others = [stack.at[k] for stack in others[:2] for k in range(stack.shape[0])] + others[2:]
+    for k, block in enumerate(own + others):
         distance = k if k <= count else k - count
         lane = core if k <= count else 1 - core
         chip = lax.rem(z + (2 * lane - 1) * distance + chips, chips)
@@ -204,7 +206,10 @@
         coming = along(far if 2 * step < count else far[0], 2)
         held[2 * step - 1] = along(far, 1)
         held[2 * step] = far = coming
-    return held + [swapped(held[d]) for d in range(1, count + 1)]
+    first = jnp.stack(held[1:5])
+    second = jnp.stack(held[5:7])
+    others = [swapped(first), swapped(second)]
+    return held + others + [swapped(held[7]), swapped(held[8])]
 
 
 def shards(tokens, expert_ids, gates, w_in, w_out):
@@ -250,7 +255,7 @@
             pltpu.SemaphoreType.DMA((2, 2 * chips)),
             pltpu.SemaphoreType.DMA((4,)),
         ],
-        limit=28 << 20,
+        limit=24 << 20,
     )
     produced, weight = lax.optimization_barrier((produced, weight))
     back = exchanged(produced)

time: 156 us -> 155 us (level)
  the two profiles are of different devices: /device:TPU:1 before, /device:TPU:8 now
where the time goes in v7:
time: 155 us; the launch traced here: 154 us
  starting transfers between devices  52.4 us (34%)
  blocking collectives  49.6 us (32%)
  waiting for transfers between devices  33.4 us (22%)
  Pallas kernels  15.1 us (10%)
  other arithmetic  2.23 us (1%)
    all_to_all x1, blocking collectives, exchanged(): return lax.all_to_all(x, 'expert', split_axis=0, concat_axis=0, tiled=True)  49.6 us
    ppermute x8, waiting for transfers between devices, along(): return lax.ppermute(x, ('z', 'c'), pairs)  32 us
    ppermute x8, starting transfers between devices, along(): return lax.ppermute(x, ('z', 'c'), pairs)  24.4 us
    all_to_all x1, starting transfers between devices, exchanged(): return lax.all_to_all(x, 'expert', split_axis=0, concat_axis=0, tiled=True)  16.8 us
    pallas_call x4, Pallas kernels, call(): pl.pallas_call(kernel, out_shape=outs, in_specs=[VMEM] * len(args) if spe...  15.1 us
    ppermute x5, starting transfers between devices, swapped(): return lax.ppermute(x, 'c', [(0, 1), (1, 0)])  11.1 us
  transfers between devices with their start and end apart: 14, of which 6 were waited for; matrix products, arithmetic and copies ran while one was open for 1% of the time, Pallas kernels for 1%

profile of v7, /device:TPU:8, one launch (start us, length us, event | category | flops | bytes accessed | tf_op | source)
XLA Modules:
  0.0 153.9 jit_solution(69278994267326561)
XLA Ops:
  0.0 2.9 %shard_map.55 = bf16[32,24,1024]{2,1,0:T(8,128)(2,1)} custom-call(s32[8,64]{1,0:T(8,128)} %bitcast.24, bf16[64,1024]{1,0:T(8,128)(2,1)} %tok_ref.1), custom_call_target="tpu_custom_call" | custom-call | flops 100663296 | bytes 1572864 | tf_op jit(solution)/shard_map/pallas_call | solution.py:175
  2.9 0.0 copy-start.3
  2.9 0.0 copy-start.4
  2.9 16.8 %all-to-all-start = ((bf16[32,24,1024]{2,1,0:T(8,128)(2,1)}), bf16[32,24,1024]{2,1,0:T(8,128)(2,1)S(1)}, u32[]{:S(2)}, u32[]{:S(2)}) async-start(bf16[32,24,1024]{2,1,0:T(8,128)(2,1)} %shard_map.55), calls=%async_computation | async-start | bytes 3145728 | tf_op jit(solution)/shard_map/all_to_all | solution.py:191
  19.8 0.0 copy-done.3
  19.8 0.0 copy-done.4
  19.8 1.9 %collective-permute-start = (bf16[2,32,1152]{2,1,0:T(8,128)(2,1)S(1)}, bf16[2,32,1152]{2,1,0:T(8,128)(2,1)S(1)}, u32[]{:S(2)}, u32[]{:S(2)}) collective-permute-start(bf16[2,32,1152]{2,1,0:T(8,128)(2,1)S(1)} %get-tuple-element.10), channel_id=1, source_target_pairs={{0,32},{32,0},{1,33},{33,1},{2,34},{34,2},{3,35},{35,3},{4,36},{36... | collective-permute-start | bytes 442376 | tf_op jit(solution)/shard_map/ppermute | solution.py:187
  21.8 1.3 collective-permute-done
  23.1 1.9 %collective-permute-start.2 = (bf16[2,2,32,1152]{3,2,1,0:T(8,128)(2,1)S(1)}, bf16[2,2,32,1152]{3,2,1,0:T(8,128)(2,1)S(1)}, u32[]{:S(2)}, u32[]{:S(2)}) collective-permute-start(bf16[2,2,32,1152]{3,2,1,0:T(8,128)(2,1)S(1)} %pad_maximum_fusion.2.refs_0_), channel_id=1, source_target_pairs={{0,128},{32,928},{64,192},{96,992},{128,256},{160,32},{192,320},{2... | collective-permute-start | bytes 884744 | tf_op jit(solution)/shard_map/ppermute | solution.py:197
  25.1 14.6 %collective-permute-done.2.refs_2_ = bf16[2,2,32,1152]{3,2,1,0:T(8,128)(2,1)S(1)} collective-permute-done((bf16[2,2,32,1152]{3,2,1,0:T(8,128)(2,1)S(1)}, bf16[2,2,32,1152]{3,2,1,0:T(8,128)(2,1)S(1)}, u32[]{:S(2)}, u32[]{:S(2)}) %collective-permute-start.2) | collective-permute-done | bytes 294944 | tf_op jit(solution)/shard_map/ppermute | solution.py:197
  39.6 1.9 %collective-permute-start.4 = (bf16[2,2,32,1152]{3,2,1,0:T(8,128)(2,1)S(1)}, bf16[2,2,32,1152]{3,2,1,0:T(8,128)(2,1)S(1)}, u32[]{:S(2)}, u32[]{:S(2)}) collective-permute-start(bf16[2,2,32,1152]{3,2,1,0:T(8,128)(2,1)S(1)} %collective-permute-done.2.refs_2_), channel_id=1, source_target_pairs={{0,128},{32,928},{64,192},{96,992},{128,256},{160,32},{192,320},{2... | collective-permute-start | bytes 884744 | tf_op jit(solution)/shard_map/ppermute | solution.py:197
  41.5 6.4 %collective-permute-start.1 = (bf16[2,2,32,1152]{3,2,1,0:T(8,128)(2,1)S(1)}, bf16[2,2,32,1152]{3,2,1,0:T(8,128)(2,1)S(1)}, u32[]{:S(2)}, u32[]{:S(2)}) collective-permute-start(bf16[2,2,32,1152]{3,2,1,0:T(8,128)(2,1)S(1)} %pad_maximum_fusion.2.refs_0_), channel_id=1, source_target_pairs={{0,64},{32,992},{64,128},{96,32},{128,192},{160,96},{192,256},{224... | collective-permute-start | bytes 884744 | tf_op jit(solution)/shard_map/ppermute | solution.py:197
  47.9 1.9 %collective-permute-start.3 = (bf16[2,2,32,1152]{3,2,1,0:T(8,128)(2,1)S(1)}, bf16[2,2,32,1152]{3,2,1,0:T(8,128)(2,1)S(1)}, u32[]{:S(2)}, u32[]{:S(2)}) collective-permute-start(bf16[2,2,32,1152]{3,2,1,0:T(8,128)(2,1)S(1)} %collective-permute-done.2.refs_2_), channel_id=1, source_target_pairs={{0,64},{32,992},{64,128},{96,32},{128,192},{160,96},{192,256},{224... | collective-permute-start | bytes 884744 | tf_op jit(solution)/shard_map/ppermute | solution.py:197
  49.9 1.6 %collective-permute-done.4.refs_4_ = bf16[2,2,32,1152]{3,2,1,0:T(8,128)(2,1)S(1)} collective-permute-done((bf16[2,2,32,1152]{3,2,1,0:T(8,128)(2,1)S(1)}, bf16[2,2,32,1152]{3,2,1,0:T(8,128)(2,1)S(1)}, u32[]{:S(2)}, u32[]{:S(2)}) %collective-permute-start.4) | collective-permute-done | bytes 294944 | tf_op jit(solution)/shard_map/ppermute | solution.py:197
  51.5 6.5 %collective-permute-start.5 = (bf16[2,2,32,1152]{3,2,1,0:T(8,128)(2,1)S(1)}, bf16[2,2,32,1152]{3,2,1,0:T(8,128)(2,1)S(1)}, u32[]{:S(2)}, u32[]{:S(2)}) collective-permute-start(bf16[2,2,32,1152]{3,2,1,0:T(8,128)(2,1)S(1)} %collective-permute-done.4.refs_4_), channel_id=1, source_target_pairs={{0,64},{32,992},{64,128},{96,32},{128,192},{160,96},{192,256},{224... | collective-permute-start | bytes 884744 | tf_op jit(solution)/shard_map/ppermute | solution.py:197
  58.0 1.9 %collective-permute-start.6 = (bf16[2,2,32,1152]{3,2,1,0:T(8,128)(2,1)S(1)}, bf16[2,2,32,1152]{3,2,1,0:T(8,128)(2,1)S(1)}, u32[]{:S(2)}, u32[]{:S(2)}) collective-permute-start(bf16[2,2,32,1152]{3,2,1,0:T(8,128)(2,1)S(1)} %collective-permute-done.4.refs_4_), channel_id=1, source_target_pairs={{0,128},{32,928},{64,192},{96,992},{128,256},{160,32},{192,320},{2... | collective-permute-start | bytes 884744 | tf_op jit(solution)/shard_map/ppermute | solution.py:197
  60.0 0.0 collective-permute-done.1.refs_1_
  60.0 1.0 collective-permute-done.3.refs_3_
  60.9 1.2 pad_maximum_fusion
  62.1 3.0 %collective-permute-start.9 = (bf16[4,2,2,32,1152]{4,3,2,1,0:T(8,128)(2,1)}, bf16[4,2,2,32,1152]{4,3,2,1,0:T(8,128)(2,1)}, u32[]{:S(2)}, u32[]{:S(2)}) collective-permute-start(bf16[4,2,2,32,1152]{4,3,2,1,0:T(8,128)(2,1)} %pad_maximum_fusion), channel_id=1, source_target_pairs={{0,32},{32,0},{1,33},{33,1},{2,34},{34,2},{3,35},{35,3},{4,36},{36... | collective-permute-start | bytes 3538952 | tf_op jit(solution)/shard_map/ppermute | solution.py:187
  65.1 0.0 collective-permute-done.5.refs_5_
  65.1 0.0 copy-start.1
  65.1 7.3 %collective-permute-done.6.refs_6_ = bf16[2,2,32,1152]{3,2,1,0:T(8,128)(2,1)S(1)} collective-permute-done((bf16[2,2,32,1152]{3,2,1,0:T(8,128)(2,1)S(1)}, bf16[2,2,32,1152]{3,2,1,0:T(8,128)(2,1)S(1)}, u32[]{:S(2)}, u32[]{:S(2)}) %collective-permute-start.6) | collective-permute-done | bytes 294944 | tf_op jit(solution)/shard_map/ppermute | solution.py:197
  72.4 0.9 pad_maximum_fusion.1
  73.3 1.9 %collective-permute-start.10 = (bf16[2,2,2,32,1152]{4,3,2,1,0:T(8,128)(2,1)}, bf16[2,2,2,32,1152]{4,3,2,1,0:T(8,128)(2,1)}, u32[]{:S(2)}, u32[]{:S(2)}) collective-permute-start(bf16[2,2,2,32,1152]{4,3,2,1,0:T(8,128)(2,1)} %pad_maximum_fusion.1), channel_id=1, source_target_pairs={{0,32},{32,0},{1,33},{33,1},{2,34},{34,2},{3,35},{35,3},{4,36},{36... | collective-permute-start | bytes 1769480 | tf_op jit(solution)/shard_map/ppermute | solution.py:187
  75.3 1.9 %collective-permute-start.7 = (bf16[2,2,32,1152]{3,2,1,0:T(8,128)(2,1)S(1)}, bf16[2,2,32,1152]{3,2,1,0:T(8,128)(2,1)}, u32[]{:S(2)}, u32[]{:S(2)}) collective-permute-start(bf16[2,2,32,1152]{3,2,1,0:T(8,128)(2,1)S(1)} %collective-permute-done.6.refs_6_), channel_id=1, source_target_pairs={{0,64},{32,992},{64,128},{96,32},{128,192},{160,96},{192,256},{224... | collective-permute-start | bytes 884744 | tf_op jit(solution)/shard_map/ppermute | solution.py:197
  77.2 1.9 %collective-permute-start.8 = (bf16[2,32,1152]{2,1,0:T(8,128)(2,1)S(1)}, bf16[2,32,1152]{2,1,0:T(8,128)(2,1)S(1)}, u32[]{:S(2)}, u32[]{:S(2)}) collective-permute-start(bf16[2,32,1152]{2,1,0:T(8,128)(2,1)S(1)} %slice_bitcast_fusion), channel_id=1, source_target_pairs={{0,128},{32,928},{64,192},{96,992},{128,256},{160,32},{192,320},{2... | collective-permute-start | bytes 442376 | tf_op jit(solution)/shard_map/ppermute | solution.py:197
  79.1 7.6 %collective-permute-done.7.refs_7_ = bf16[2,2,32,1152]{3,2,1,0:T(8,128)(2,1)} collective-permute-done((bf16[2,2,32,1152]{3,2,1,0:T(8,128)(2,1)S(1)}, bf16[2,2,32,1152]{3,2,1,0:T(8,128)(2,1)}, u32[]{:S(2)}, u32[]{:S(2)}) %collective-permute-start.7) | collective-permute-done | bytes 294944 | tf_op jit(solution)/shard_map/ppermute | solution.py:197
  86.7 0.0 copy-done.1
  86.7 1.9 %collective-permute-start.11 = (bf16[2,2,32,1152]{3,2,1,0:T(8,128)(2,1)}, bf16[2,2,32,1152]{3,2,1,0:T(8,128)(2,1)}, u32[]{:S(2)}, u32[]{:S(2)}) collective-permute-start(bf16[2,2,32,1152]{3,2,1,0:T(8,128)(2,1)} %collective-permute-done.7.refs_7_), channel_id=1, source_target_pairs={{0,32},{32,0},{1,33},{33,1},{2,34},{34,2},{3,35},{35,3},{4,36},{36... | collective-permute-start | bytes 884744 | tf_op jit(solution)/shard_map/ppermute | solution.py:187
  88.6 0.0 collective-permute-done.8.refs_8_
  88.6 2.4 %collective-permute-start.12 = (bf16[2,32,1152]{2,1,0:T(8,128)(2,1)S(1)}, bf16[2,32,1152]{2,1,0:T(8,128)(2,1)}, u32[]{:S(2)}, u32[]{:S(2)}) collective-permute-start(bf16[2,32,1152]{2,1,0:T(8,128)(2,1)S(1)} %collective-permute-done.8.refs_8_), channel_id=1, source_target_pairs={{0,32},{32,0},{1,33},{33,1},{2,34},{34,2},{3,35},{35,3},{4,36},{36... | collective-permute-start | bytes 442376 | tf_op jit(solution)/shard_map/ppermute | solution.py:187
  91.0 1.9 %shard_map.57.weight_ref = bf16[128,768]{1,0:T(8,128)(2,1)} custom-call(s32[8,64]{1,0:T(8,128)} %bitcast.25, f32[8,64]{1,0:T(8,128)} %bitcast.26), custom_call_target="tpu_custom_call" | custom-call | flops 25165824 | bytes 196608 | tf_op jit(solution)/shard_map/pallas_call | solution.py:175
  93.0 0.1 pad_add_fusion.place_ref
  93.0 0.0 collective-permute-done.12.refs_12_
  93.0 0.0 collective-permute-done.10.refs_10_
  93.0 0.0 collective-permute-done.11.refs_11_
  93.0 0.0 collective-permute-done.9.refs_9_
  93.1 0.0 all-to-all-done.x_hbm
  93.1 0.0 copy-start.2
  93.1 1.0 copy-done.2
  94.0 9.0 %shard_map.56 = bf16[32,24,1024]{2,1,0:T(8,128)(2,1)S(1)} custom-call(s32[2]{0:T(128)S(1)} %pad_add_fusion.place_ref, bf16[32,24,1024]{2,1,0:T(8,128)(2,1)S(1)} %all-to-all-done.x_hbm, bf16[2,2,32,1152]{3,2,1,0:T(8,128)(2,1)S(1)} %pad_maximum_fusion.2.refs_0_, bf16[2,2,32,1152]{3,2,1,0:T(8,128)(2,1)S(1)} %collective-permute-done.1.refs_1_, ...), custom_call_target="tpu_custom_call" | custom-call | flops 2415919104 | bytes 7864320 | tf_op jit(solution)/shard_map/pallas_call | solution.py:175
  103.1 0.0 copy-start
  103.1 49.6 %all_to_all.10.back_hbm = bf16[32,24,1024]{2,1,0:T(8,128)(2,1)S(1)} all-to-all(bf16[32,24,1024]{2,1,0:T(8,128)(2,1)S(1)} %shard_map.56), channel_id=1, replica_groups=mesh['z'=16,'c'=2,'expert'=32] {'expert'}, dimensions={0} | all-to-all | bytes 3145728 | tf_op jit(solution)/shard_map/all_to_all | solution.py:191
  152.6 0.0 copy-done
  152.6 1.3 shard_map.58
  (3 shorter events, 0.1 us)
Async XLA Ops:
  2.9 16.9 %copy-start.3 = (bf16[2,32,768]{2,1,0:T(8,128)(2,1)S(1)}, bf16[2,32,768]{2,1,0:T(8,128)(2,1)}, u32[]{:S(2)}) copy-start(bf16[2,32,768]{2,1,0:T(8,128)(2,1)} %param.8) | copy-start | bytes 294916
  2.9 16.9 %copy-start.4 = (bf16[2,384,32]{1,2,0:T(8,128)(2,1)S(1)}, bf16[2,384,32]{1,2,0:T(8,128)(2,1)}, u32[]{:S(2)}) copy-start(bf16[2,384,32]{1,2,0:T(8,128)(2,1)} %param.9) | copy-start | bytes 147460
  2.9 90.1 %all-to-all-start = ((bf16[32,24,1024]{2,1,0:T(8,128)(2,1)}), bf16[32,24,1024]{2,1,0:T(8,128)(2,1)S(1)}, u32[]{:S(2)}, u32[]{:S(2)}) async-start(bf16[32,24,1024]{2,1,0:T(8,128)(2,1)} %shard_map.55), calls=%async_computation | async-start | bytes 3145728 | tf_op jit(solution)/shard_map/all_to_all | solution.py:191
  19.8 3.3 %collective-permute-start = (bf16[2,32,1152]{2,1,0:T(8,128)(2,1)S(1)}, bf16[2,32,1152]{2,1,0:T(8,128)(2,1)S(1)}, u32[]{:S(2)}, u32[]{:S(2)}) collective-permute-start(bf16[2,32,1152]{2,1,0:T(8,128)(2,1)S(1)} %get-tuple-element.10), channel_id=1, source_target_pairs={{0,32},{32,0},{1,33},{33,1},{2,34},{34,2},{3,35},{35,3},{4,36},{36... | collective-permute-start | bytes 442376 | tf_op jit(solution)/shard_map/ppermute | solution.py:187
  23.1 16.5 %collective-permute-start.2 = (bf16[2,2,32,1152]{3,2,1,0:T(8,128)(2,1)S(1)}, bf16[2,2,32,1152]{3,2,1,0:T(8,128)(2,1)S(1)}, u32[]{:S(2)}, u32[]{:S(2)}) collective-permute-start(bf16[2,2,32,1152]{3,2,1,0:T(8,128)(2,1)S(1)} %pad_maximum_fusion.2.refs_0_), channel_id=1, source_target_pairs={{0,128},{32,928},{64,192},{96,992},{128,256},{160,32},{192,320},{2... | collective-permute-start | bytes 884744 | tf_op jit(solution)/shard_map/ppermute | solution.py:197
  39.6 11.9 %collective-permute-start.4 = (bf16[2,2,32,1152]{3,2,1,0:T(8,128)(2,1)S(1)}, bf16[2,2,32,1152]{3,2,1,0:T(8,128)(2,1)S(1)}, u32[]{:S(2)}, u32[]{:S(2)}) collective-permute-start(bf16[2,2,32,1152]{3,2,1,0:T(8,128)(2,1)S(1)} %collective-permute-done.2.refs_2_), channel_id=1, source_target_pairs={{0,128},{32,928},{64,192},{96,992},{128,256},{160,32},{192,320},{2... | collective-permute-start | bytes 884744 | tf_op jit(solution)/shard_map/ppermute | solution.py:197
  41.5 18.4 %collective-permute-start.1 = (bf16[2,2,32,1152]{3,2,1,0:T(8,128)(2,1)S(1)}, bf16[2,2,32,1152]{3,2,1,0:T(8,128)(2,1)S(1)}, u32[]{:S(2)}, u32[]{:S(2)}) collective-permute-start(bf16[2,2,32,1152]{3,2,1,0:T(8,128)(2,1)S(1)} %pad_maximum_fusion.2.refs_0_), channel_id=1, source_target_pairs={{0,64},{32,992},{64,128},{96,32},{128,192},{160,96},{192,256},{224... | collective-permute-start | bytes 884744 | tf_op jit(solution)/shard_map/ppermute | solution.py:197
  47.9 13.0 %collective-permute-start.3 = (bf16[2,2,32,1152]{3,2,1,0:T(8,128)(2,1)S(1)}, bf16[2,2,32,1152]{3,2,1,0:T(8,128)(2,1)S(1)}, u32[]{:S(2)}, u32[]{:S(2)}) collective-permute-start(bf16[2,2,32,1152]{3,2,1,0:T(8,128)(2,1)S(1)} %collective-permute-done.2.refs_2_), channel_id=1, source_target_pairs={{0,64},{32,992},{64,128},{96,32},{128,192},{160,96},{192,256},{224... | collective-permute-start | bytes 884744 | tf_op jit(solution)/shard_map/ppermute | solution.py:197
  51.5 13.6 %collective-permute-start.5 = (bf16[2,2,32,1152]{3,2,1,0:T(8,128)(2,1)S(1)}, bf16[2,2,32,1152]{3,2,1,0:T(8,128)(2,1)S(1)}, u32[]{:S(2)}, u32[]{:S(2)}) collective-permute-start(bf16[2,2,32,1152]{3,2,1,0:T(8,128)(2,1)S(1)} %collective-permute-done.4.refs_4_), channel_id=1, source_target_pairs={{0,64},{32,992},{64,128},{96,32},{128,192},{160,96},{192,256},{224... | collective-permute-start | bytes 884744 | tf_op jit(solution)/shard_map/ppermute | solution.py:197
  58.0 14.4 %collective-permute-start.6 = (bf16[2,2,32,1152]{3,2,1,0:T(8,128)(2,1)S(1)}, bf16[2,2,32,1152]{3,2,1,0:T(8,128)(2,1)S(1)}, u32[]{:S(2)}, u32[]{:S(2)}) collective-permute-start(bf16[2,2,32,1152]{3,2,1,0:T(8,128)(2,1)S(1)} %collective-permute-done.4.refs_4_), channel_id=1, source_target_pairs={{0,128},{32,928},{64,192},{96,992},{128,256},{160,32},{192,320},{2... | collective-permute-start | bytes 884744 | tf_op jit(solution)/shard_map/ppermute | solution.py:197
  62.1 30.9 %collective-permute-start.9 = (bf16[4,2,2,32,1152]{4,3,2,1,0:T(8,128)(2,1)}, bf16[4,2,2,32,1152]{4,3,2,1,0:T(8,128)(2,1)}, u32[]{:S(2)}, u32[]{:S(2)}) collective-permute-start(bf16[4,2,2,32,1152]{4,3,2,1,0:T(8,128)(2,1)} %pad_maximum_fusion), channel_id=1, source_target_pairs={{0,32},{32,0},{1,33},{33,1},{2,34},{34,2},{3,35},{35,3},{4,36},{36... | collective-permute-start | bytes 3538952 | tf_op jit(solution)/shard_map/ppermute | solution.py:187
  65.1 21.6 %copy-start.1 = (bf16[2,2,32,1152]{3,2,1,0:T(8,128)(2,1)}, bf16[2,2,32,1152]{3,2,1,0:T(8,128)(2,1)S(1)}, u32[]{:S(2)}) copy-start(bf16[2,2,32,1152]{3,2,1,0:T(8,128)(2,1)S(1)} %collective-permute-done.5.refs_5_) | copy-start | bytes 884740
  73.3 19.7 %collective-permute-start.10 = (bf16[2,2,2,32,1152]{4,3,2,1,0:T(8,128)(2,1)}, bf16[2,2,2,32,1152]{4,3,2,1,0:T(8,128)(2,1)}, u32[]{:S(2)}, u32[]{:S(2)}) collective-permute-start(bf16[2,2,2,32,1152]{4,3,2,1,0:T(8,128)(2,1)} %pad_maximum_fusion.1), channel_id=1, source_target_pairs={{0,32},{32,0},{1,33},{33,1},{2,34},{34,2},{3,35},{35,3},{4,36},{36... | collective-permute-start | bytes 1769480 | tf_op jit(solution)/shard_map/ppermute | solution.py:187
  75.3 11.4 %collective-permute-start.7 = (bf16[2,2,32,1152]{3,2,1,0:T(8,128)(2,1)S(1)}, bf16[2,2,32,1152]{3,2,1,0:T(8,128)(2,1)}, u32[]{:S(2)}, u32[]{:S(2)}) collective-permute-start(bf16[2,2,32,1152]{3,2,1,0:T(8,128)(2,1)S(1)} %collective-permute-done.6.refs_6_), channel_id=1, source_target_pairs={{0,64},{32,992},{64,128},{96,32},{128,192},{160,96},{192,256},{224... | collective-permute-start | bytes 884744 | tf_op jit(solution)/shard_map/ppermute | solution.py:197
  77.2 11.4 %collective-permute-start.8 = (bf16[2,32,1152]{2,1,0:T(8,128)(2,1)S(1)}, bf16[2,32,1152]{2,1,0:T(8,128)(2,1)S(1)}, u32[]{:S(2)}, u32[]{:S(2)}) collective-permute-start(bf16[2,32,1152]{2,1,0:T(8,128)(2,1)S(1)} %slice_bitcast_fusion), channel_id=1, source_target_pairs={{0,128},{32,928},{64,192},{96,992},{128,256},{160,32},{192,320},{2... | collective-permute-start | bytes 442376 | tf_op jit(solution)/shard_map/ppermute | solution.py:197
  86.7 6.3 %collective-permute-start.11 = (bf16[2,2,32,1152]{3,2,1,0:T(8,128)(2,1)}, bf16[2,2,32,1152]{3,2,1,0:T(8,128)(2,1)}, u32[]{:S(2)}, u32[]{:S(2)}) collective-permute-start(bf16[2,2,32,1152]{3,2,1,0:T(8,128)(2,1)} %collective-permute-done.7.refs_7_), channel_id=1, source_target_pairs={{0,32},{32,0},{1,33},{33,1},{2,34},{34,2},{3,35},{35,3},{4,36},{36... | collective-permute-start | bytes 884744 | tf_op jit(solution)/shard_map/ppermute | solution.py:187
  88.6 4.4 %collective-permute-start.12 = (bf16[2,32,1152]{2,1,0:T(8,128)(2,1)S(1)}, bf16[2,32,1152]{2,1,0:T(8,128)(2,1)}, u32[]{:S(2)}, u32[]{:S(2)}) collective-permute-start(bf16[2,32,1152]{2,1,0:T(8,128)(2,1)S(1)} %collective-permute-done.8.refs_8_), channel_id=1, source_target_pairs={{0,32},{32,0},{1,33},{33,1},{2,34},{34,2},{3,35},{35,3},{4,36},{36... | collective-permute-start | bytes 442376 | tf_op jit(solution)/shard_map/ppermute | solution.py:187
  93.1 1.0 copy-start.2
  103.1 49.6 %copy-start = (bf16[128,768]{1,0:T(8,128)(2,1)S(1)}, bf16[128,768]{1,0:T(8,128)(2,1)}, u32[]{:S(2)}) copy-start(bf16[128,768]{1,0:T(8,128)(2,1)} %shard_map.57.weight_ref) | copy-start | bytes 589828

commit v8 on v6

--- a/solution.py
+++ b/solution.py
@@ -86,17 +86,22 @@
         weight_ref[at * rows : (at + 1) * rows, :] = weight.T
 
 
-def expert_rows(x_ref, start, w_in, w_out):
-    owners, _, width = x_ref.shape
+def paired(first, second):
+    upper = iota(first.shape, 1) < 4
+    return (
+        jnp.where(upper, first, pltpu.roll(second, 4, 1)),
+        jnp.where(upper, pltpu.roll(first, 4, 1), second),
+    )
+
+
+def expert_rows(full, rest, w_in, w_out):
     hidden = w_out.shape[1]
-    full = x_ref[:, start : start + 8, :].reshape(owners * 8, width)
-    rest = x_ref[:, 16:24, :].reshape(owners * 8, width)
+    count = full.shape[0]
     joint = dot(jnp.concatenate([full, rest], axis=0), w_in)
     gate, up = joint[:, :hidden], joint[:, hidden:]
     activated = (gate * jax.nn.sigmoid(gate) * up).astype(BF16)
     made = dot_t(activated, w_out)
-    shape = (owners, 8, width)
-    return made[: owners * 8].reshape(shape), made[owners * 8 :].reshape(shape)
+    return made[:count], made[count:]
 
 
 def expert_kernel(place_ref, x_hbm, *refs):
@@ -112,7 +117,12 @@
             copies[e].append(pltpu.make_async_copy(block.at[e], whole.at[e, chip, lane], sem))
 
     count = chips // 2
-    for k, block in enumerate(blocks):
+    single = []
+    for block in blocks:
+        stacked = len(block.shape) == 5
+        single += [block.at[k] for k in range(block.shape[0])] if stacked else [block]
+    del single[count + 1]
+    for k, block in enumerate(single):
         distance = k if k <= count else k - count
         lane = core if k <= count else 1 - core
         chip = lax.rem(z + (2 * lane - 1) * distance + chips, chips)
@@ -127,20 +137,24 @@
         for copy in copies[e]:
             copy.start()
     rows_in.wait()
+    owners = x_ref.shape[0]
     wide = 2 * both // 3
     made, out = [], []
+    rest = x_ref[:, 16:24, :].astype(F32).reshape(owners // 2, 2, 8, width)
+    rests = [part.reshape(owners * 4, width).astype(BF16) for part in paired(rest[:, 0], rest[:, 1])]
     for e in range(2):
         for copy in copies[e]:
             copy.wait()
         w_in = whole[e, :, :, :, :wide].reshape(width, wide)
         w_out = whole[e, :, :, :, wide:].reshape(width, both - wide)
-        full, rest = expert_rows(x_ref, 8 * e, w_in, w_out)
-        y_ref[e] = full.astype(BF16)
+        rows = x_ref[:, 8 * e : 8 * e + 8, :].reshape(owners * 8, width)
+        full, few = expert_rows(rows, rests[e], w_in, w_out)
+        y_ref[e] = full.reshape(owners, 8, width).astype(BF16)
         out.append(pltpu.make_async_copy(y_ref.at[e], y_hbm.at[:, 8 * e : 8 * e + 8], row_sems.at[1 + e]))
         out[e].start()
-        made.append(rest)
-    first = iota(made[0].shape, 1) < 4
-    y_ref[2] = jnp.where(first, made[0], made[1]).astype(BF16)
+        made.append(few.reshape(owners // 2, 8, width))
+    even, odd = paired(*made)
+    y_ref[2] = jnp.stack([even, odd], axis=1).reshape(owners, 8, width).astype(BF16)
     out.append(pltpu.make_async_copy(y_ref.at[2], y_hbm.at[:, 16:24], row_sems.at[3]))
     out[2].start()
     for copy in out:
@@ -204,7 +218,11 @@
         coming = along(far if 2 * step < count else far[0], 2)
         held[2 * step - 1] = along(far, 1)
         held[2 * step] = far = coming
-    return held + [swapped(held[d]) for d in range(1, count + 1)]
+    first = jnp.stack(held[0:5])
+    second = jnp.stack(held[5:7])
+    others = [swapped(first), swapped(second)]
+    others += [swapped(held[7]), swapped(held[8])]
+    return [first, second, held[7], held[8]] + others
 
 
 def shards(tokens, expert_ids, gates, w_in, w_out):
@@ -250,7 +268,7 @@
             pltpu.SemaphoreType.DMA((2, 2 * chips)),
             pltpu.SemaphoreType.DMA((4,)),
         ],
-        limit=28 << 20,
+        limit=18 << 20,
     )
     produced, weight = lax.optimization_barrier((produced, weight))
     back = exchanged(produced)

time: 156 us -> 151 us (0.968)
  starting transfers between devices: 74.7 us -> 66.9 us
  waiting for transfers between devices: 9.84 us -> 14.2 us
  local copies, waits for them, and re-layouts: 5.03 us -> 2.99 us
  Pallas kernels: 16.1 us -> 14.2 us
  other arithmetic: 0.13 us -> 1.85 us
    ppermute x8, starting transfers between devices: 37.8 us -> 30 us  [along(): return lax.ppermute(x, ('z', 'c'), pairs)]
    ppermute x8, waiting for transfers between devices: 8.83 us -> 13.2 us  [along(): return lax.ppermute(x, ('z', 'c'), pairs)]
    unnamed x18 -> x5, local copies, waits for them, and re-layouts: 5.02 us -> 2.22 us
    pallas_call x4, Pallas kernels: 16.1 us -> 14.2 us  [call(): pl.pallas_call(kernel, out_shape=outs, in_specs=[VMEM] * len(args) if spe...]
    ppermute x9 -> x5, starting transfers between devices: 26.3 us -> 27.2 us  [swapped(): return lax.ppermute(x, 'c', [(0, 1), (1, 0)])]
  transfers between devices with their start and end apart: 18 -> 14, of which waited for: 3 -> 6; matrix products, arithmetic and copies ran while one was open for 0% -> 3% of each run, Pallas kernels for 1% -> 3%
where the time goes in v8:
time: 151 us; the launch traced here: 150 us
  starting transfers between devices  66.9 us (44%)
  blocking collectives  49.6 us (33%)
  waiting for transfers between devices  14.2 us (9%)
  Pallas kernels  14.2 us (9%)
  local copies, waits for them, and re-layouts  2.99 us (2%)
  other arithmetic  1.85 us (1%)
    all_to_all x1, blocking collectives, exchanged(): return lax.all_to_all(x, 'expert', split_axis=0, concat_axis=0, tiled=True)  49.6 us
    ppermute x8, starting transfers between devices, along(): return lax.ppermute(x, ('z', 'c'), pairs)  30 us
    ppermute x5, starting transfers between devices, swapped(): return lax.ppermute(x, 'c', [(0, 1), (1, 0)])  27.2 us
    pallas_call x4, Pallas kernels, call(): pl.pallas_call(kernel, out_shape=outs, in_specs=[VMEM] * len(args) if spe...  14.2 us
    ppermute x8, waiting for transfers between devices, along(): return lax.ppermute(x, ('z', 'c'), pairs)  13.2 us
    all_to_all x1, starting transfers between devices, exchanged(): return lax.all_to_all(x, 'expert', split_axis=0, concat_axis=0, tiled=True)  9.67 us
  transfers between devices with their start and end apart: 14, of which 6 were waited for; matrix products, arithmetic and copies ran while one was open for 3% of the time, Pallas kernels for 3%

profile of v8, /device:TPU:1, one launch (start us, length us, event | category | flops | bytes accessed | tf_op | source)
XLA Modules:
  0.0 150.1 jit_solution(10649594751608094803)
XLA Ops:
  0.0 0.9 fusion
  0.9 16.0 %collective-permute-start = (bf16[2,32,1152]{2,1,0:T(8,128)(2,1)S(1)}, bf16[2,32,1152]{2,1,0:T(8,128)(2,1)S(1)}, u32[]{:S(2)}, u32[]{:S(2)}) collective-permute-start(bf16[2,32,1152]{2,1,0:T(8,128)(2,1)S(1)} %get-tuple-element.10), channel_id=1, source_target_pairs={{0,32},{32,0},{1,33},{33,1},{2,34},{34,2},{3,35},{35,3},{4,36},{36... | collective-permute-start | bytes 442376 | tf_op jit(solution)/shard_map/ppermute | solution.py:199
  17.0 1.0 collective-permute-done
  18.0 5.3 %collective-permute-start.2 = (bf16[2,2,32,1152]{3,2,1,0:T(8,128)(2,1)S(1)}, bf16[2,2,32,1152]{3,2,1,0:T(8,128)(2,1)S(1)}, u32[]{:S(2)}, u32[]{:S(2)}) collective-permute-start(bf16[2,2,32,1152]{3,2,1,0:T(8,128)(2,1)S(1)} %pad_maximum_fusion.1), channel_id=1, source_target_pairs={{0,128},{32,928},{64,192},{96,992},{128,256},{160,32},{192,320},{2... | collective-permute-start | bytes 884744 | tf_op jit(solution)/shard_map/ppermute | solution.py:209
  23.3 2.2 %collective-permute-start.1 = (bf16[2,2,32,1152]{3,2,1,0:T(8,128)(2,1)S(1)}, bf16[2,2,32,1152]{3,2,1,0:T(8,128)(2,1)S(1)}, u32[]{:S(2)}, u32[]{:S(2)}) collective-permute-start(bf16[2,2,32,1152]{3,2,1,0:T(8,128)(2,1)S(1)} %pad_maximum_fusion.1), channel_id=1, source_target_pairs={{0,64},{32,992},{64,128},{96,32},{128,192},{160,96},{192,256},{224... | collective-permute-start | bytes 884744 | tf_op jit(solution)/shard_map/ppermute | solution.py:209
  25.5 2.9 %shard_map.55 = bf16[32,24,1024]{2,1,0:T(8,128)(2,1)} custom-call(s32[8,64]{1,0:T(8,128)} %bitcast.27, bf16[64,1024]{1,0:T(8,128)(2,1)} %tok_ref.1), custom_call_target="tpu_custom_call" | custom-call | flops 100663296 | bytes 1572864 | tf_op jit(solution)/shard_map/pallas_call | solution.py:187
  28.4 9.7 %all-to-all-start = ((bf16[32,24,1024]{2,1,0:T(8,128)(2,1)}), bf16[32,24,1024]{2,1,0:T(8,128)(2,1)S(1)}, u32[]{:S(2)}, u32[]{:S(2)}) async-start(bf16[32,24,1024]{2,1,0:T(8,128)(2,1)} %shard_map.55), calls=%async_computation | async-start | bytes 3145728 | tf_op jit(solution)/shard_map/all_to_all | solution.py:203
  38.1 0.7 bitcast_dynamic-update-slice_fusion.4
  38.9 0.0 collective-permute-done.2
  38.9 2.2 %collective-permute-start.3 = (bf16[2,2,32,1152]{3,2,1,0:T(8,128)(2,1)S(1)}, bf16[2,2,32,1152]{3,2,1,0:T(8,128)(2,1)S(1)}, u32[]{:S(2)}, u32[]{:S(2)}) collective-permute-start(bf16[2,2,32,1152]{3,2,1,0:T(8,128)(2,1)S(1)} %collective-permute-done.2), channel_id=1, source_target_pairs={{0,64},{32,992},{64,128},{96,32},{128,192},{160,96},{192,256},{224... | collective-permute-start | bytes 884744 | tf_op jit(solution)/shard_map/ppermute | solution.py:209
  41.0 3.4 %collective-permute-start.4 = (bf16[2,2,32,1152]{3,2,1,0:T(8,128)(2,1)S(1)}, bf16[2,2,32,1152]{3,2,1,0:T(8,128)(2,1)S(1)}, u32[]{:S(2)}, u32[]{:S(2)}) collective-permute-start(bf16[2,2,32,1152]{3,2,1,0:T(8,128)(2,1)S(1)} %collective-permute-done.2), channel_id=1, source_target_pairs={{0,128},{32,928},{64,192},{96,992},{128,256},{160,32},{192,320},{2... | collective-permute-start | bytes 884744 | tf_op jit(solution)/shard_map/ppermute | solution.py:209
  44.4 0.0 collective-permute-done.1
  44.4 0.7 bitcast_dynamic-update-slice_fusion.3
  45.2 0.8 bitcast_dynamic-update-slice_fusion.2
  45.9 0.7 collective-permute-done.3
  46.6 0.7 bitcast_dynamic-update-slice_fusion.1
  47.3 6.5 %collective-permute-done.4 = bf16[2,2,32,1152]{3,2,1,0:T(8,128)(2,1)S(1)} collective-permute-done((bf16[2,2,32,1152]{3,2,1,0:T(8,128)(2,1)S(1)}, bf16[2,2,32,1152]{3,2,1,0:T(8,128)(2,1)S(1)}, u32[]{:S(2)}, u32[]{:S(2)}) %collective-permute-start.4) | collective-permute-done | bytes 294944 | tf_op jit(solution)/shard_map/ppermute | solution.py:209
  53.8 0.8 bitcast_dynamic-update-slice_fusion.refs_0_
  54.6 1.9 %collective-permute-start.9 = (bf16[5,2,2,32,1152]{4,3,2,1,0:T(8,128)(2,1)}, bf16[5,2,2,32,1152]{4,3,2,1,0:T(8,128)(2,1)}, u32[]{:S(2)}, u32[]{:S(2)}) collective-permute-start(bf16[5,2,2,32,1152]{4,3,2,1,0:T(8,128)(2,1)} %bitcast_dynamic-update-slice_fusion.refs_0_), channel_id=1, source_target_pairs={{0,32},{32,0},{1,33},{33,1},{2,34},{34,2},{3,35},{35,3},{4,36},{36... | collective-permute-start | bytes 4423688 | tf_op jit(solution)/shard_map/ppermute | solution.py:199
  56.5 3.6 %collective-permute-start.6 = (bf16[2,2,32,1152]{3,2,1,0:T(8,128)(2,1)S(1)}, bf16[2,2,32,1152]{3,2,1,0:T(8,128)(2,1)S(1)}, u32[]{:S(2)}, u32[]{:S(2)}) collective-permute-start(bf16[2,2,32,1152]{3,2,1,0:T(8,128)(2,1)S(1)} %collective-permute-done.4), channel_id=1, source_target_pairs={{0,128},{32,928},{64,192},{96,992},{128,256},{160,32},{192,320},{2... | collective-permute-start | bytes 884744 | tf_op jit(solution)/shard_map/ppermute | solution.py:209
  60.1 5.8 %collective-permute-start.5 = (bf16[2,2,32,1152]{3,2,1,0:T(8,128)(2,1)S(1)}, bf16[2,2,32,1152]{3,2,1,0:T(8,128)(2,1)S(1)}, u32[]{:S(2)}, u32[]{:S(2)}) collective-permute-start(bf16[2,2,32,1152]{3,2,1,0:T(8,128)(2,1)S(1)} %collective-permute-done.4), channel_id=1, source_target_pairs={{0,64},{32,992},{64,128},{96,32},{128,192},{160,96},{192,256},{224... | collective-permute-start | bytes 884744 | tf_op jit(solution)/shard_map/ppermute | solution.py:209
  66.0 1.7 %collective-permute-done.6 = bf16[2,2,32,1152]{3,2,1,0:T(8,128)(2,1)S(1)} collective-permute-done((bf16[2,2,32,1152]{3,2,1,0:T(8,128)(2,1)S(1)}, bf16[2,2,32,1152]{3,2,1,0:T(8,128)(2,1)S(1)}, u32[]{:S(2)}, u32[]{:S(2)}) %collective-permute-start.6) | collective-permute-done | bytes 294944 | tf_op jit(solution)/shard_map/ppermute | solution.py:209
  67.6 4.1 %collective-permute-done.5 = bf16[2,2,32,1152]{3,2,1,0:T(8,128)(2,1)S(1)} collective-permute-done((bf16[2,2,32,1152]{3,2,1,0:T(8,128)(2,1)S(1)}, bf16[2,2,32,1152]{3,2,1,0:T(8,128)(2,1)S(1)}, u32[]{:S(2)}, u32[]{:S(2)}) %collective-permute-start.5) | collective-permute-done | bytes 294944 | tf_op jit(solution)/shard_map/ppermute | solution.py:209
  71.8 0.1 pad_maximum_fusion.refs_1_
  71.8 2.3 %collective-permute-start.10 = (bf16[2,2,2,32,1152]{4,3,2,1,0:T(8,128)(2,1)S(1)}, bf16[2,2,2,32,1152]{4,3,2,1,0:T(8,128)(2,1)S(1)}, u32[]{:S(2)}, u32[]{:S(2)}) collective-permute-start(bf16[2,2,2,32,1152]{4,3,2,1,0:T(8,128)(2,1)S(1)} %pad_maximum_fusion.refs_1_), channel_id=1, source_target_pairs={{0,32},{32,0},{1,33},{33,1},{2,34},{34,2},{3,35},{35,3},{4,36},{36... | collective-permute-start | bytes 1769480 | tf_op jit(solution)/shard_map/ppermute | solution.py:199
  74.2 4.1 %collective-permute-start.7 = (bf16[2,2,32,1152]{3,2,1,0:T(8,128)(2,1)S(1)}, bf16[2,2,32,1152]{3,2,1,0:T(8,128)(2,1)S(1)}, u32[]{:S(2)}, u32[]{:S(2)}) collective-permute-start(bf16[2,2,32,1152]{3,2,1,0:T(8,128)(2,1)S(1)} %collective-permute-done.6), channel_id=1, source_target_pairs={{0,64},{32,992},{64,128},{96,32},{128,192},{160,96},{192,256},{224... | collective-permute-start | bytes 884744 | tf_op jit(solution)/shard_map/ppermute | solution.py:209
  78.3 3.4 %collective-permute-start.8 = (bf16[2,32,1152]{2,1,0:T(8,128)(2,1)S(1)}, bf16[2,32,1152]{2,1,0:T(8,128)(2,1)S(1)}, u32[]{:S(2)}, u32[]{:S(2)}) collective-permute-start(bf16[2,32,1152]{2,1,0:T(8,128)(2,1)S(1)} %slice_bitcast_fusion), channel_id=1, source_target_pairs={{0,128},{32,928},{64,192},{96,992},{128,256},{160,32},{192,320},{2... | collective-permute-start | bytes 442376 | tf_op jit(solution)/shard_map/ppermute | solution.py:209
  81.7 0.2 collective-permute-done.7.refs_2_
  81.9 4.1 %collective-permute-start.11 = (bf16[2,2,32,1152]{3,2,1,0:T(8,128)(2,1)S(1)}, bf16[2,2,32,1152]{3,2,1,0:T(8,128)(2,1)S(1)}, u32[]{:S(2)}, u32[]{:S(2)}) collective-permute-start(bf16[2,2,32,1152]{3,2,1,0:T(8,128)(2,1)S(1)} %collective-permute-done.7.refs_2_), channel_id=1, source_target_pairs={{0,32},{32,0},{1,33},{33,1},{2,34},{34,2},{3,35},{35,3},{4,36},{36... | collective-permute-start | bytes 884744 | tf_op jit(solution)/shard_map/ppermute | solution.py:199
  86.0 0.0 collective-permute-done.8.refs_3_
  86.0 2.9 %collective-permute-start.12 = (bf16[2,32,1152]{2,1,0:T(8,128)(2,1)S(1)}, bf16[2,32,1152]{2,1,0:T(8,128)(2,1)}, u32[]{:S(2)}, u32[]{:S(2)}) collective-permute-start(bf16[2,32,1152]{2,1,0:T(8,128)(2,1)S(1)} %collective-permute-done.8.refs_3_), channel_id=1, source_target_pairs={{0,32},{32,0},{1,33},{33,1},{2,34},{34,2},{3,35},{35,3},{4,36},{36... | collective-permute-start | bytes 442376 | tf_op jit(solution)/shard_map/ppermute | solution.py:199
  89.0 1.9 %shard_map.57.weight_ref = bf16[128,768]{1,0:T(8,128)(2,1)} custom-call(s32[8,64]{1,0:T(8,128)} %bitcast.28, f32[8,64]{1,0:T(8,128)} %bitcast.29), custom_call_target="tpu_custom_call" | custom-call | flops 25165824 | bytes 196608 | tf_op jit(solution)/shard_map/pallas_call | solution.py:187
  90.9 0.1 pad_add_fusion.place_ref
  90.9 0.0 collective-permute-done.12.refs_7_
  90.9 0.0 collective-permute-done.10.refs_5_
  90.9 0.0 collective-permute-done.11.refs_6_
  90.9 0.0 collective-permute-done.9.refs_4_
  91.0 0.0 all-to-all-done.x_hbm
  91.0 8.1 %shard_map.56 = bf16[32,24,1024]{2,1,0:T(8,128)(2,1)S(1)} custom-call(s32[2]{0:T(128)S(1)} %pad_add_fusion.place_ref, bf16[32,24,1024]{2,1,0:T(8,128)(2,1)S(1)} %all-to-all-done.x_hbm, bf16[5,2,2,32,1152]{4,3,2,1,0:T(8,128)(2,1)} %bitcast_dynamic-update-slice_fusion.refs_0_, bf16[2,2,2,32,1152]{4,3,2,1,0:T(8,128)(2,1)S(1)} %pad_maximum_fusion.refs_1_, ...), custom_call_target="tpu_custom_call" | custom-call | flops 2415919104 | bytes 7864320 | tf_op jit(solution)/shard_map/pallas_call | solution.py:187
  99.1 0.0 copy-start
  99.1 49.6 %all_to_all.10.back_hbm = bf16[32,24,1024]{2,1,0:T(8,128)(2,1)S(1)} all-to-all(bf16[32,24,1024]{2,1,0:T(8,128)(2,1)S(1)} %shard_map.56), channel_id=1, replica_groups=mesh['z'=16,'c'=2,'expert'=32] {'expert'}, dimensions={0} | all-to-all | bytes 3145728 | tf_op jit(solution)/shard_map/all_to_all | solution.py:203
  148.8 0.0 copy-done
  148.8 1.3 shard_map.58
  (2 shorter events, 0.0 us)
Async XLA Ops:
  0.9 17.0 %collective-permute-start = (bf16[2,32,1152]{2,1,0:T(8,128)(2,1)S(1)}, bf16[2,32,1152]{2,1,0:T(8,128)(2,1)S(1)}, u32[]{:S(2)}, u32[]{:S(2)}) collective-permute-start(bf16[2,32,1152]{2,1,0:T(8,128)(2,1)S(1)} %get-tuple-element.10), channel_id=1, source_target_pairs={{0,32},{32,0},{1,33},{33,1},{2,34},{34,2},{3,35},{35,3},{4,36},{36... | collective-permute-start | bytes 442376 | tf_op jit(solution)/shard_map/ppermute | solution.py:199
  18.0 20.9 %collective-permute-start.2 = (bf16[2,2,32,1152]{3,2,1,0:T(8,128)(2,1)S(1)}, bf16[2,2,32,1152]{3,2,1,0:T(8,128)(2,1)S(1)}, u32[]{:S(2)}, u32[]{:S(2)}) collective-permute-start(bf16[2,2,32,1152]{3,2,1,0:T(8,128)(2,1)S(1)} %pad_maximum_fusion.1), channel_id=1, source_target_pairs={{0,128},{32,928},{64,192},{96,992},{128,256},{160,32},{192,320},{2... | collective-permute-start | bytes 884744 | tf_op jit(solution)/shard_map/ppermute | solution.py:209
  23.3 21.1 %collective-permute-start.1 = (bf16[2,2,32,1152]{3,2,1,0:T(8,128)(2,1)S(1)}, bf16[2,2,32,1152]{3,2,1,0:T(8,128)(2,1)S(1)}, u32[]{:S(2)}, u32[]{:S(2)}) collective-permute-start(bf16[2,2,32,1152]{3,2,1,0:T(8,128)(2,1)S(1)} %pad_maximum_fusion.1), channel_id=1, source_target_pairs={{0,64},{32,992},{64,128},{96,32},{128,192},{160,96},{192,256},{224... | collective-permute-start | bytes 884744 | tf_op jit(solution)/shard_map/ppermute | solution.py:209
  28.4 62.5 %all-to-all-start = ((bf16[32,24,1024]{2,1,0:T(8,128)(2,1)}), bf16[32,24,1024]{2,1,0:T(8,128)(2,1)S(1)}, u32[]{:S(2)}, u32[]{:S(2)}) async-start(bf16[32,24,1024]{2,1,0:T(8,128)(2,1)} %shard_map.55), calls=%async_computation | async-start | bytes 3145728 | tf_op jit(solution)/shard_map/all_to_all | solution.py:203
  38.9 7.8 %collective-permute-start.3 = (bf16[2,2,32,1152]{3,2,1,0:T(8,128)(2,1)S(1)}, bf16[2,2,32,1152]{3,2,1,0:T(8,128)(2,1)S(1)}, u32[]{:S(2)}, u32[]{:S(2)}) collective-permute-start(bf16[2,2,32,1152]{3,2,1,0:T(8,128)(2,1)S(1)} %collective-permute-done.2), channel_id=1, source_target_pairs={{0,64},{32,992},{64,128},{96,32},{128,192},{160,96},{192,256},{224... | collective-permute-start | bytes 884744 | tf_op jit(solution)/shard_map/ppermute | solution.py:209
  41.0 12.8 %collective-permute-start.4 = (bf16[2,2,32,1152]{3,2,1,0:T(8,128)(2,1)S(1)}, bf16[2,2,32,1152]{3,2,1,0:T(8,128)(2,1)S(1)}, u32[]{:S(2)}, u32[]{:S(2)}) collective-permute-start(bf16[2,2,32,1152]{3,2,1,0:T(8,128)(2,1)S(1)} %collective-permute-done.2), channel_id=1, source_target_pairs={{0,128},{32,928},{64,192},{96,992},{128,256},{160,32},{192,320},{2... | collective-permute-start | bytes 884744 | tf_op jit(solution)/shard_map/ppermute | solution.py:209
  54.6 36.4 %collective-permute-start.9 = (bf16[5,2,2,32,1152]{4,3,2,1,0:T(8,128)(2,1)}, bf16[5,2,2,32,1152]{4,3,2,1,0:T(8,128)(2,1)}, u32[]{:S(2)}, u32[]{:S(2)}) collective-permute-start(bf16[5,2,2,32,1152]{4,3,2,1,0:T(8,128)(2,1)} %bitcast_dynamic-update-slice_fusion.refs_0_), channel_id=1, source_target_pairs={{0,32},{32,0},{1,33},{33,1},{2,34},{34,2},{3,35},{35,3},{4,36},{36... | collective-permute-start | bytes 4423688 | tf_op jit(solution)/shard_map/ppermute | solution.py:199
  56.5 11.1 %collective-permute-start.6 = (bf16[2,2,32,1152]{3,2,1,0:T(8,128)(2,1)S(1)}, bf16[2,2,32,1152]{3,2,1,0:T(8,128)(2,1)S(1)}, u32[]{:S(2)}, u32[]{:S(2)}) collective-permute-start(bf16[2,2,32,1152]{3,2,1,0:T(8,128)(2,1)S(1)} %collective-permute-done.4), channel_id=1, source_target_pairs={{0,128},{32,928},{64,192},{96,992},{128,256},{160,32},{192,320},{2... | collective-permute-start | bytes 884744 | tf_op jit(solution)/shard_map/ppermute | solution.py:209
  60.1 11.7 %collective-permute-start.5 = (bf16[2,2,32,1152]{3,2,1,0:T(8,128)(2,1)S(1)}, bf16[2,2,32,1152]{3,2,1,0:T(8,128)(2,1)S(1)}, u32[]{:S(2)}, u32[]{:S(2)}) collective-permute-start(bf16[2,2,32,1152]{3,2,1,0:T(8,128)(2,1)S(1)} %collective-permute-done.4), channel_id=1, source_target_pairs={{0,64},{32,992},{64,128},{96,32},{128,192},{160,96},{192,256},{224... | collective-permute-start | bytes 884744 | tf_op jit(solution)/shard_map/ppermute | solution.py:209
  71.8 19.1 %collective-permute-start.10 = (bf16[2,2,2,32,1152]{4,3,2,1,0:T(8,128)(2,1)S(1)}, bf16[2,2,2,32,1152]{4,3,2,1,0:T(8,128)(2,1)S(1)}, u32[]{:S(2)}, u32[]{:S(2)}) collective-permute-start(bf16[2,2,2,32,1152]{4,3,2,1,0:T(8,128)(2,1)S(1)} %pad_maximum_fusion.refs_1_), channel_id=1, source_target_pairs={{0,32},{32,0},{1,33},{33,1},{2,34},{34,2},{3,35},{35,3},{4,36},{36... | collective-permute-start | bytes 1769480 | tf_op jit(solution)/shard_map/ppermute | solution.py:199
  74.2 7.8 %collective-permute-start.7 = (bf16[2,2,32,1152]{3,2,1,0:T(8,128)(2,1)S(1)}, bf16[2,2,32,1152]{3,2,1,0:T(8,128)(2,1)S(1)}, u32[]{:S(2)}, u32[]{:S(2)}) collective-permute-start(bf16[2,2,32,1152]{3,2,1,0:T(8,128)(2,1)S(1)} %collective-permute-done.6), channel_id=1, source_target_pairs={{0,64},{32,992},{64,128},{96,32},{128,192},{160,96},{192,256},{224... | collective-permute-start | bytes 884744 | tf_op jit(solution)/shard_map/ppermute | solution.py:209
  78.3 7.7 %collective-permute-start.8 = (bf16[2,32,1152]{2,1,0:T(8,128)(2,1)S(1)}, bf16[2,32,1152]{2,1,0:T(8,128)(2,1)S(1)}, u32[]{:S(2)}, u32[]{:S(2)}) collective-permute-start(bf16[2,32,1152]{2,1,0:T(8,128)(2,1)S(1)} %slice_bitcast_fusion), channel_id=1, source_target_pairs={{0,128},{32,928},{64,192},{96,992},{128,256},{160,32},{192,320},{2... | collective-permute-start | bytes 442376 | tf_op jit(solution)/shard_map/ppermute | solution.py:209
  81.9 9.0 %collective-permute-start.11 = (bf16[2,2,32,1152]{3,2,1,0:T(8,128)(2,1)S(1)}, bf16[2,2,32,1152]{3,2,1,0:T(8,128)(2,1)S(1)}, u32[]{:S(2)}, u32[]{:S(2)}) collective-permute-start(bf16[2,2,32,1152]{3,2,1,0:T(8,128)(2,1)S(1)} %collective-permute-done.7.refs_2_), channel_id=1, source_target_pairs={{0,32},{32,0},{1,33},{33,1},{2,34},{34,2},{3,35},{35,3},{4,36},{36... | collective-permute-start | bytes 884744 | tf_op jit(solution)/shard_map/ppermute | solution.py:199
  86.0 4.9 %collective-permute-start.12 = (bf16[2,32,1152]{2,1,0:T(8,128)(2,1)S(1)}, bf16[2,32,1152]{2,1,0:T(8,128)(2,1)}, u32[]{:S(2)}, u32[]{:S(2)}) collective-permute-start(bf16[2,32,1152]{2,1,0:T(8,128)(2,1)S(1)} %collective-permute-done.8.refs_3_), channel_id=1, source_target_pairs={{0,32},{32,0},{1,33},{33,1},{2,34},{34,2},{3,35},{35,3},{4,36},{36... | collective-permute-start | bytes 442376 | tf_op jit(solution)/shard_map/ppermute | solution.py:199
  99.1 49.7 %copy-start = (bf16[128,768]{1,0:T(8,128)(2,1)S(1)}, bf16[128,768]{1,0:T(8,128)(2,1)}, u32[]{:S(2)}) copy-start(bf16[128,768]{1,0:T(8,128)(2,1)} %shard_map.57.weight_ref) | copy-start | bytes 589828
